TPU v7x, 32 devices: a whole 2x2x4 slice. The times are simulated.
32 devices in a mesh: dp: 4 (over z), vocab: 8 (over y, x, core).
Axes of the slice: x: 2, y: 2, z: 4, core: 2. Of those that a mesh axis runs over, the one named last changes fastest.
Arguments:
- teacher_logits: bfloat16 [512, 64000], P('dp', 'vocab'), may hold values from -64 to 320
- student_hidden: bfloat16 [512, 2304], P('dp'), may hold values from -100 to 100
- student_head: bfloat16 [2304, 16384], P('dp', 'vocab'), may hold values from -0.625 to 0.625
- keep_ids: int32 [128, 128], replicated, may hold values from -1 to 63999, as said below
- block_owner: int32 [128], replicated, may hold values from 0 to 7, as said below
- block_count: int32 [128], replicated, may hold values from 32 to 128
Outputs:
- head_grad: bfloat16 [2304, 16384], P('dp', 'vocab')
- hidden_grad: bfloat16 [512, 2304], P(('dp', 'vocab'))
Inputs may be any that keep to these rules, and one draw needn't show every extreme that they name: `keep_ids`: lanes below block_count[b] hold ids, the others -1. The ids of the whole table increase along each block and from block to block, and the ids of one block lie in one range of 8000 ids (the same id // 8000). One such range holds at most 32 blocks. `block_owner`: every vocab index owns exactly 16 blocks. The blocks of one range of 8000 ids owned by one vocab index number at most 4, and some pair reaches 4.
All inputs are finite; a program needn't handle non-finite values.
Results may differ from a plain program's by a relative error of at most 0.0049.
Values may be sent and summed in bfloat16 or wider, within the bound.
No kernel may reach another device: no remote copies, remote signals or barrier semaphores. Data moves between devices by JAX's collectives and lax.ppermute only.
A program may use at most 64 MiB of HBM per device.

v0:
```python
import jax
import jax.numpy as jnp
from jax import lax
from jax.sharding import PartitionSpec as P

loss_scale = 8192.0


def joined(value, axis, join):
    pieces = jax.tree.map(lambda part: lax.all_gather(part, axis), value)
    head = jax.tree.map(lambda part: part[0], pieces)
    tail = jax.tree.map(lambda part: part[1:], pieces)
    running, _ = lax.scan(lambda running, section: (join(running, section), None), head, tail)
    return running


def combine_softmax(former, latter):
    joined_top = jnp.maximum(former[0], latter[0])
    joined_total = former[1] * jnp.exp(former[0] - joined_top) + latter[1] * jnp.exp(
        latter[0] - joined_top
    )
    extras = tuple((former[index] + latter[index] for index in range(2, len(former))))
    return (joined_top, joined_total) + extras


def shards(teacher_logits, student_hidden, student_head, keep_ids, block_owner, block_count):
    shard_count = lax.axis_size("vocab")
    my_shard = lax.axis_index("vocab")
    tok_rows, vocab_rows = teacher_logits.shape
    lane_count = keep_ids.shape[1]
    kept_blocks = block_owner.shape[0] // shard_count
    capacity = (2 * kept_blocks + shard_count - 1) // shard_count
    numbers = jnp.arange(block_owner.shape[0], dtype=jnp.int32)
    lane_index = jnp.arange(lane_count, dtype=jnp.int32)
    source = keep_ids[:, 0] // vocab_rows
    owner_before = (block_owner[None, :] == block_owner[:, None]) & (
        numbers[None, :] < numbers[:, None]
    )
    ordinal = jnp.sum(owner_before.astype(jnp.int32), axis=1)
    pair_rank = jnp.sum(
        (owner_before & (source[None, :] == source[:, None])).astype(jnp.int32), axis=1
    )
    values = teacher_logits.astype(jnp.float32)
    local_peak = jnp.max(values, axis=1)
    local_total = jnp.sum(jnp.exp(values - local_peak[:, None]), axis=1)
    top_logit, exp_total = joined((local_peak, local_total), "vocab", combine_softmax)
    send_slots = jnp.arange(shard_count * capacity, dtype=jnp.int32)
    outgoing = (
        (source == my_shard)[None, :]
        & (block_owner[None, :] == (send_slots // capacity)[:, None])
        & (pair_rank[None, :] == (send_slots % capacity)[:, None])
    )
    present = jnp.any(outgoing, axis=1)
    chosen = jnp.sum(jnp.where(outgoing, numbers[None, :], 0), axis=1)
    live_slots = present[:, None] & (lane_index[None, :] < block_count[chosen][:, None])
    columns = jnp.where(live_slots, keep_ids[chosen] - my_shard * vocab_rows, 0).reshape(-1)
    picked = jnp.take(teacher_logits, columns, axis=1).astype(jnp.float32)
    kept_probs = jnp.where(
        live_slots.reshape(-1)[None, :],
        jnp.exp(picked - top_logit[:, None]) / exp_total[:, None],
        0.0,
    )
    arrived = lax.all_to_all(
        kept_probs.astype(jnp.bfloat16), "vocab", split_axis=1, concat_axis=1, tiled=True
    )
    incoming = (block_owner[None, :] == my_shard) & (
        ordinal[None, :] == jnp.arange(kept_blocks, dtype=jnp.int32)[:, None]
    )
    own_blocks = jnp.sum(jnp.where(incoming, numbers[None, :], 0), axis=1)
    anchor = (source[own_blocks] * capacity + pair_rank[own_blocks]) * lane_count
    positions = (anchor[:, None] + lane_index[None, :]).reshape(-1)
    target = jnp.take(arrived, positions, axis=1).astype(jnp.float32)
    valid_cols = (lane_index[None, :] < block_count[own_blocks][:, None]).reshape(-1)
    scores = jnp.dot(
        student_hidden,
        lax.all_gather(student_head, "dp", axis=0, tiled=True),
        preferred_element_type=jnp.float32,
    )
    masked = jnp.where(valid_cols[None, :], scores, -jnp.inf)
    local_top = jnp.max(masked, axis=1)
    mass_part = jnp.sum(target, axis=1)
    local_weight = jnp.where(valid_cols[None, :], jnp.exp(masked - local_top[:, None]), 0.0)
    student_top, exp_norm, kept_mass = joined(
        (local_top, jnp.sum(local_weight, axis=1), mass_part), "vocab", combine_softmax
    )
    weight = local_weight * jnp.exp(local_top - student_top)[:, None]
    gradient = loss_scale * (weight / exp_norm[:, None] * kept_mass[:, None] - target)
    logit_grads = gradient.astype(jnp.bfloat16)
    slices = lax.all_to_all(student_hidden, "dp", split_axis=1, concat_axis=0, tiled=True)
    head_grad = lax.dot_general(
        slices,
        lax.all_gather(logit_grads, "dp", axis=0, tiled=True),
        (((0,), (0,)), ((), ())),
        preferred_element_type=jnp.float32,
    ).astype(jnp.bfloat16)
    partial_sums = lax.dot_general(
        logit_grads,
        lax.all_gather(student_head, "dp", axis=0, tiled=True),
        (((1,), (1,)), ((), ())),
        preferred_element_type=jnp.float32,
    )
    hidden_grad = lax.psum_scatter(partial_sums, "vocab", scatter_dimension=0, tiled=True)
    return (head_grad, hidden_grad.astype(jnp.bfloat16))


def solution(mesh):
    return jax.shard_map(
        shards,
        mesh=mesh,
        in_specs=(P("dp", "vocab"), P("dp", None), P("dp", "vocab"), P(), P(), P()),
        out_specs=(P("dp", "vocab"), P(("dp", "vocab"), None)),
        check_vma=False,
    )
```

profile of v0, /device:TPU:0, one launch (start us, length us, event | category | flops | bytes accessed | tf_op | source)
XLA Modules:
  0.0 303.5 jit_solution(15925542410932017132)
XLA Ops:
  7.2 0.7 all-gather.13.cloned.1.call-update
  7.9 0.8 copy-done.1
  8.8 1.1 reduce_max.28
  9.8 1.1 exponential_reduce_fusion
  10.9 10.3 %all-gather.8 = f32[8,1,128]{2,1,0:T(1,128)S(1)} all-gather(f32[1,1,128]{2,1,0:T(1,128)S(1)} %bitcast.132), channel_id=5, replica_groups=mesh['dp'=4,'vocab'=8] {'vocab'}, dimensions={0}, use_global_device_ids=true | all-gather | bytes 4608 | tf_op jit(solution)/shard_map/all_gather | solution.py:10
  21.2 8.7 %all-gather.7 = f32[8,1,128]{2,1,0:T(1,128)S(1)} all-gather(f32[1,1,128]{2,1,0:T(1,128)S(1)} %get-tuple-element.115), channel_id=4, replica_groups=mesh['dp'=4,'vocab'=8] {'vocab'}, dimensions={0}, use_global_device_ids=true | all-gather | bytes 4608 | tf_op jit(solution)/shard_map/all_gather | solution.py:10
  31.0 0.6 gather_fusion.4
  31.6 0.7 gather_fusion.3
  32.6 12.1 %gather_fusion.5 = bf16[4096,128]{1,0:T(8,128)(2,1)S(1)} fusion(bf16[128,8000]{0,1:T(8,128)(2,1)S(1)} %copy-done.1, s32[4096]{0:T(1024)S(1)} %broadcast_clamp_fusion), kind=kCustom, calls=%fused_computation.5 | custom fusion | bytes 2113536 | tf_op jit(solution)/shard_map/jit(_take)/gather | solution.py:57
  45.1 2.5 select_convert_fusion
  47.6 3.6 %all-to-all-start = ((bf16[128,8,512]{0,2,1:T(8,128)(2,1)}), bf16[128,8,512]{0,2,1:T(8,128)(2,1)S(1)}, u32[]{:S(2)}, u32[]{:S(2)}) async-start(bf16[128,8,512]{0,2,1:T(8,128)(2,1)} %select_convert_fusion), calls=%async_computation | async-start | bytes 2097152 | tf_op jit(solution)/shard_map/all_to_all | solution.py:63
  51.3 0.7 gather_fusion.2
  52.0 0.7 gather_fusion.1
  52.7 0.7 gather_fusion
  53.6 12.9 %all-to-all-done = bf16[128,8,512]{0,2,1:T(8,128)(2,1)S(1)} async-done(((bf16[128,8,512]{0,2,1:T(8,128)(2,1)}), bf16[128,8,512]{0,2,1:T(8,128)(2,1)S(1)}, u32[]{:S(2)}, u32[]{:S(2)}) %all-to-all-start) | async-done | bytes 1048608 | tf_op jit(solution)/shard_map/all_to_all | solution.py:63
  66.5 6.2 %gather_fusion.6 = bf16[2048,128]{1,0:T(8,128)(2,1)S(1)} fusion(bf16[128,4096]{0,1:T(8,128)(2,1)S(1)} %bitcast.119, s32[2048]{0:T(1024)S(1)} %broadcast_clamp_fusion.1), kind=kCustom, calls=%fused_computation.6 | custom fusion | bytes 1056768 | tf_op jit(solution)/shard_map/jit(_take)/gather | solution.py:72
  73.1 7.8 %all-gather.9 = f32[8,1,128]{2,1,0:T(1,128)S(1)} all-gather(f32[1,1,128]{2,1,0:T(1,128)S(1)} %bitcast.133), channel_id=6, replica_groups=mesh['dp'=4,'vocab'=8] {'vocab'}, dimensions={0}, use_global_device_ids=true | all-gather | bytes 4608 | tf_op jit(solution)/shard_map/all_gather | solution.py:10
  80.9 98.2 %all-gather.13.cloned.1.call-done = bf16[2304,2048]{1,0:T(8,128)(2,1)} async-done(((bf16[576,2048]{1,0:T(8,128)(2,1)}), bf16[2304,2048]{1,0:T(8,128)(2,1)}) %all-gather.13.cloned.1.call-update) | async-done | bytes 9437200 | tf_op jit(solution)/shard_map/all_gather | solution.py:76
  179.1 5.2 %fusion.36 = (f32[128]{0:T(128)S(1)}, f32[128,2048]{1,0:T(8,128)S(1)}) fusion(bf16[128,2304]{1,0:T(8,128)(2,1)S(1)} %copy-done.3, bf16[2304,2048]{1,0:T(8,128)(2,1)} %all-gather.13.cloned.1.call-done, pred[2048]{0:T(1024)(128)(4,1)S(1)} %fusion.27), kind=kOutput, calls=%fused_computation.101 | convolution fusion | flops 1208483712 | bytes 11078144 | tf_op jit(solution)/shard_map/dot_general | solution.py:74
  184.3 0.3 fusion.16
  184.6 8.8 %all-gather.6 = f32[8,1,128]{2,1,0:T(1,128)S(1)} all-gather(f32[1,1,128]{2,1,0:T(1,128)S(1)} %bitcast.131), channel_id=3, replica_groups=mesh['dp'=4,'vocab'=8] {'vocab'}, dimensions={0}, use_global_device_ids=true | all-gather | bytes 4608 | tf_op jit(solution)/shard_map/all_gather | solution.py:10
  193.4 8.7 %all-gather.5 = f32[8,1,128]{2,1,0:T(1,128)S(1)} all-gather(f32[1,1,128]{2,1,0:T(1,128)S(1)} %bitcast.130), channel_id=2, replica_groups=mesh['dp'=4,'vocab'=8] {'vocab'}, dimensions={0}, use_global_device_ids=true | all-gather | bytes 4608 | tf_op jit(solution)/shard_map/all_gather | solution.py:10
  202.1 0.3 while.27
  202.5 0.5 fusion.15
  203.0 8.1 %fusion.37 = f32[128,2304]{1,0:T(8,128)} fusion(bf16[128,2048]{1,0:T(8,128)(2,1)S(1)} %fusion.15, bf16[2304,2048]{1,0:T(8,128)(2,1)} %all-gather.13.cloned.1.call-done), kind=kOutput, calls=%fused_computation.102 | convolution fusion | flops 1207959552 | bytes 11141120 | tf_op jit(solution)/shard_map/dot_general | solution.py:96
  211.2 0.7 all-gather.15.cloned.1.call-update
  211.9 1.1 copy.24
  212.9 3.5 %all-to-all-start.1 = ((bf16[128,4,576]{0,2,1:T(8,128)(2,1)}), bf16[128,4,576]{0,2,1:T(8,128)(2,1)S(1)}, u32[]{:S(2)}, u32[]{:S(2)}) async-start(bf16[128,4,576]{0,2,1:T(8,128)(2,1)} %bitcast.31), calls=%async_computation.1 | async-start | bytes 1179648 | tf_op jit(solution)/shard_map/all_to_all | solution.py:89
  216.4 28.8 %reduce-scatter.2.cloned.1.call-done = f32[16,2304]{1,0:T(8,128)} async-done(((f32[128,2304]{1,0:T(8,128)}), f32[16,2304]{1,0:T(8,128)}) %reduce-scatter.2.cloned.1.call-update) | async-done | bytes 147472 | tf_op jit(solution)/shard_map/reduce_scatter | solution.py:102
  245.3 1.6 convert_element_type.41
  246.8 45.7 %all-gather.15.cloned.1.call-done = bf16[512,2048]{1,0:T(8,128)(2,1)} async-done(((bf16[128,2048]{1,0:T(8,128)(2,1)}), bf16[512,2048]{1,0:T(8,128)(2,1)}) %all-gather.15.cloned.1.call-update) | async-done | bytes 2097168 | tf_op jit(solution)/shard_map/all_gather | solution.py:92
  292.5 4.4 %fusion.12 = bf16[576,2048]{1,0:T(8,128)(2,1)} fusion(bf16[512,2048]{1,0:T(8,128)(2,1)} %all-gather.15.cloned.1.call-done, bf16[128,4,576]{0,2,1:T(8,128)(2,1)S(1)} %all-to-all-done.1), kind=kOutput, calls=%fused_computation.26 | convolution fusion | flops 1209139200 | bytes 5046272 | tf_op jit(solution)/shard_map/dot_general | solution.py:90
  (79 shorter events, 3.1 us)
Async XLA Ops:
  7.2 24.4 %copy-start = (s32[128]{0:T(128)S(1)}, s32[128]{0:T(128)}, u32[]{:S(2)}) copy-start(s32[128]{0:T(128)} %param.15) | copy-start | bytes 1540
  7.2 1.6 copy-start.1
  7.2 171.9 %all-gather.13.cloned.1.call-start = ((), (), s32[]{:S(2)}) async-start(), calls=%async_computation.3 | async-start | bytes 11796480 | tf_op jit(solution)/shard_map/all_gather | solution.py:76
  8.8 21.2 %copy-start.4 = (s32[128,128]{1,0:T(8,128)S(1)}, s32[128,128]{1,0:T(8,128)}, u32[]{:S(2)}) copy-start(s32[128,128]{1,0:T(8,128)} %param.13) | copy-start | bytes 196612
  8.8 21.5 %copy-start.5 = (s32[128]{0:T(128)S(1)}, s32[128]{0:T(128)}, u32[]{:S(2)}) copy-start(s32[128]{0:T(128)} %param.14) | copy-start | bytes 1540
  47.6 18.9 %all-to-all-start = ((bf16[128,8,512]{0,2,1:T(8,128)(2,1)}), bf16[128,8,512]{0,2,1:T(8,128)(2,1)S(1)}, u32[]{:S(2)}, u32[]{:S(2)}) async-start(bf16[128,8,512]{0,2,1:T(8,128)(2,1)} %select_convert_fusion), calls=%async_computation | async-start | bytes 2097152 | tf_op jit(solution)/shard_map/all_to_all | solution.py:63
  51.2 194.1 %reduce-scatter.2.cloned.1.call-start = ((), (), s32[]{:S(2)}) async-start(), calls=%async_computation.5 | async-start | bytes 1327104 | tf_op jit(solution)/shard_map/reduce_scatter | solution.py:102
  66.5 112.6 %copy-start.3 = (bf16[128,2304]{1,0:T(8,128)(2,1)S(1)}, bf16[128,2304]{1,0:T(8,128)(2,1)}, u32[]{:S(2)}) copy-start(bf16[128,2304]{1,0:T(8,128)(2,1)} %param.11) | copy-start | bytes 1769476
  203.0 8.1 %copy-start.2 = (bf16[128,2048]{1,0:T(8,128)(2,1)}, bf16[128,2048]{1,0:T(8,128)(2,1)S(1)}, u32[]{:S(2)}) copy-start(bf16[128,2048]{1,0:T(8,128)(2,1)S(1)} %fusion.15) | copy-start | bytes 1572868
  211.1 81.4 %all-gather.15.cloned.1.call-start = ((), (), s32[]{:S(2)}) async-start(), calls=%async_computation.4 | async-start | bytes 2621440 | tf_op jit(solution)/shard_map/all_gather | solution.py:92
  212.9 33.9 %all-to-all-start.1 = ((bf16[128,4,576]{0,2,1:T(8,128)(2,1)}), bf16[128,4,576]{0,2,1:T(8,128)(2,1)S(1)}, u32[]{:S(2)}, u32[]{:S(2)}) async-start(bf16[128,4,576]{0,2,1:T(8,128)(2,1)} %bitcast.31), calls=%async_computation.1 | async-start | bytes 1179648 | tf_op jit(solution)/shard_map/all_to_all | solution.py:89
Sparse Core Ops, SparseCore 0:
  9.6 169.4 all-gather.12
  211.3 33.9 reduce-scatter.1
  246.8 45.6 all-gather.14
where the time goes:
time: 304 us; the launch traced here: 303 us
  waiting for transfers between devices  187 us (62%)
  blocking collectives  44.3 us (15%)
  local copies, waits for them, and re-layouts  24.1 us (8%)
  matrix products  17.7 us (6%)
  between operations  14 us (5%)
  other arithmetic  9.02 us (3%)
  starting transfers between devices  7.16 us (2%)
    all_gather x1, waiting for transfers between devices, shards(): lax.all_gather(student_head, 'dp', axis=0, tiled=True)  98.2 us
    all_gather x1, waiting for transfers between devices, shards(): lax.all_gather(logit_grads, 'dp', axis=0, tiled=True)  45.7 us
    all_gather x5, blocking collectives, joined(): pieces = jax.tree.map(lambda part: lax.all_gather(part, axis), value)  44.3 us
    reduce_scatter x1, waiting for transfers between devices, shards(): lax.psum_scatter(partial_sums, 'vocab', scatter_dimension=0, tiled=True)  28.8 us
    all_to_all x1, waiting for transfers between devices, shards(): lax.all_to_all(kept_probs.astype(jnp.bfloat16), 'vocab', split_axis=1, co...  12.9 us
    gather x1, local copies, waits for them, and re-layouts, shards(): picked = jnp.take(teacher_logits, columns, axis=1).astype(jnp.float32)  12.1 us
    dot_general x1, matrix products, shards(): lax.dot_general(logit_grads, lax.all_gather(student_head, 'dp', axis=0, t...  8.1 us
    gather x2, local copies, waits for them, and re-layouts, shards(): target = jnp.take(arrived, positions, axis=1).astype(jnp.float32)  6.4 us
  transfers between devices with their start and end apart: 5, of which 4 were waited for; matrix products, arithmetic and copies ran while one was open for 10% of the time, Pallas kernels for 0%

commit v1 on v0

v1 whole, which is shorter than its diff:
```python
import jax
import jax.numpy as jnp
from jax import lax
from jax.sharding import PartitionSpec as P

loss_scale = 8192.0


def exchange(value, axes):
    count = lax.axis_size(axes)
    copies = jnp.broadcast_to(value[None], (count,) + value.shape)
    return lax.all_to_all(copies, axes, split_axis=0, concat_axis=0, tiled=True)


def line_gather(value, axis):
    size = lax.axis_size(axis)
    ups, downs = [], []
    rising = falling = value
    for step in range(size - 1):
        rising = lax.ppermute(rising, axis, [(p, p + 1) for p in range(step, size - 1)])
        falling = lax.ppermute(falling, axis, [(p + 1, p) for p in range(size - 1 - step)])
        ups.append(rising)
        downs.append(falling)
    return [ups[k - 1] + downs[size - k - 1] for k in range(1, size)]


def halving_sum(value, axis):
    size = lax.axis_size(axis)
    index = lax.axis_index(axis)
    tail = value.shape[1:]
    groups = 1
    bit = 1
    while bit < size:
        pairs = [(i, i ^ bit) for i in range(size)]
        split = value.reshape((size // (2 * bit), 2, 1) + tail)
        mine = (index // bit) % 2
        keep = lax.dynamic_index_in_dim(split, mine, 1, keepdims=False)
        send = lax.dynamic_index_in_dim(split, 1 - mine, 1, keepdims=False)
        value = (keep + lax.ppermute(send, axis, pairs)).reshape((size // (2 * bit),) + tail)
        bit *= 2
    return value[0]


def shards(teacher_logits, student_hidden, student_head, keep_ids, block_owner, block_count):
    planes = lax.axis_size("dp")
    plane = lax.axis_index("dp")
    shard_count = lax.axis_size("vocab")
    my_shard = lax.axis_index("vocab")
    tok_rows, vocab_rows = teacher_logits.shape
    slab, own_cols = student_head.shape
    width = student_hidden.shape[1]
    lane_count = keep_ids.shape[1]
    kept_blocks = block_owner.shape[0] // shard_count
    part_blocks = kept_blocks // planes
    part_cols = own_cols // planes
    slice_rows = tok_rows // shard_count
    tokens = planes * tok_rows
    capacity = (2 * kept_blocks + shard_count - 1) // shard_count

    head = lax.all_to_all(
        student_head.reshape(slab, planes, part_cols).transpose(1, 0, 2),
        "dp", split_axis=0, concat_axis=0, tiled=True,
    ).reshape(width, part_cols)

    numbers = jnp.arange(block_owner.shape[0], dtype=jnp.int32)
    lane_index = jnp.arange(lane_count, dtype=jnp.int32)
    source = keep_ids[:, 0] // vocab_rows
    owner_before = (block_owner[None, :] == block_owner[:, None]) & (
        numbers[None, :] < numbers[:, None]
    )
    ordinal = jnp.sum(owner_before.astype(jnp.int32), axis=1)
    pair_rank = jnp.sum(
        (owner_before & (source[None, :] == source[:, None])).astype(jnp.int32), axis=1
    )
    send_slots = jnp.arange(shard_count * capacity, dtype=jnp.int32)
    outgoing = (
        (source == my_shard)[None, :]
        & (block_owner[None, :] == (send_slots // capacity)[:, None])
        & (pair_rank[None, :] == (send_slots % capacity)[:, None])
    )
    present = jnp.any(outgoing, axis=1)
    chosen = jnp.sum(jnp.where(outgoing, numbers[None, :], 0), axis=1)
    live_slots = present[:, None] & (lane_index[None, :] < block_count[chosen][:, None])
    columns = jnp.where(live_slots, keep_ids[chosen] - my_shard * vocab_rows, 0).reshape(-1)

    picked = jnp.take(teacher_logits, columns, axis=1)
    arrived = lax.all_to_all(
        picked.reshape(tok_rows, shard_count * capacity, lane_count).transpose(1, 0, 2),
        "vocab", split_axis=0, concat_axis=0, tiled=True,
    )
    incoming = (block_owner[None, :] == my_shard) & (
        ordinal[None, :] == jnp.arange(kept_blocks, dtype=jnp.int32)[:, None]
    )
    own_blocks = jnp.sum(jnp.where(incoming, numbers[None, :], 0), axis=1)
    anchor = source[own_blocks] * capacity + pair_rank[own_blocks]
    target = lax.all_to_all(
        jnp.take(arrived, anchor, axis=0), "dp", split_axis=0, concat_axis=0, tiled=True
    )
    target = (
        target.reshape(planes, part_blocks, tok_rows, lane_count)
        .transpose(0, 2, 1, 3)
        .reshape(tokens, part_cols)
        .astype(jnp.float32)
    )
    own_counts = block_count[lax.dynamic_slice_in_dim(own_blocks, plane * part_blocks, part_blocks)]
    valid_cols = (lane_index[None, :] < own_counts[:, None]).reshape(-1)[None, :]

    hidden_slice = lax.dynamic_slice_in_dim(student_hidden, my_shard * slice_rows, slice_rows)
    hidden = exchange(exchange(hidden_slice, "dp"), "vocab")
    hidden = (
        hidden.reshape(shard_count, planes, slice_rows, width)
        .transpose(1, 0, 2, 3)
        .reshape(tokens, width)
    )

    values = teacher_logits.astype(jnp.float32)
    local_peak = jnp.max(values, axis=1)
    local_total = jnp.sum(jnp.exp(values - local_peak[:, None]), axis=1)
    stats = exchange(jnp.stack([local_peak, local_total]), ("dp", "vocab"))
    stats = stats.reshape(planes, shard_count, 2, tok_rows)
    peak = jnp.max(stats[:, :, 0], axis=1)
    total = jnp.sum(stats[:, :, 1] * jnp.exp(stats[:, :, 0] - peak[:, None]), axis=1)
    kept = jnp.where(
        valid_cols, jnp.exp(target - peak.reshape(-1, 1)) / total.reshape(-1, 1), 0.0
    ).astype(jnp.bfloat16).astype(jnp.float32)

    scores = jnp.dot(hidden, head, preferred_element_type=jnp.float32)
    masked = jnp.where(valid_cols, scores, -jnp.inf)
    local_top = jnp.max(masked, axis=1)
    weight = jnp.where(valid_cols, jnp.exp(masked - local_top[:, None]), 0.0)
    student = exchange(
        jnp.stack([local_top, jnp.sum(weight, axis=1), jnp.sum(kept, axis=1)]), ("dp", "vocab")
    ).reshape(planes * shard_count, 3, tokens)
    student_top = jnp.max(student[:, 0], axis=0)
    exp_norm = jnp.sum(student[:, 1] * jnp.exp(student[:, 0] - student_top), axis=0)
    kept_mass = jnp.sum(student[:, 2], axis=0)
    factor = jnp.exp(local_top - student_top) / exp_norm * kept_mass
    gradient = (loss_scale * (weight * factor[:, None] - kept)).astype(jnp.bfloat16)

    partial_sums = lax.dot_general(
        gradient, head, (((1,), (1,)), ((), ())), preferred_element_type=jnp.float32
    )
    partial_sums = (
        partial_sums.reshape(planes, shard_count, slice_rows, width).transpose(1, 0, 2, 3)
    )
    partial_sums = halving_sum(partial_sums, "vocab")
    partial_sums = lax.all_to_all(partial_sums, "dp", split_axis=0, concat_axis=0, tiled=True)
    hidden_grad = jnp.sum(partial_sums.reshape(planes, slice_rows, width), axis=0)

    own_hidden = lax.dynamic_slice_in_dim(hidden, plane * slab, slab, axis=1)
    head_grad = jnp.zeros((slab, own_cols), jnp.bfloat16)
    for distance, columns_part in enumerate([gradient] + line_gather(gradient, "dp")):
        origin = lax.rem(plane + planes - distance, planes)
        block = lax.dot_general(
            own_hidden, columns_part, (((0,), (0,)), ((), ())), preferred_element_type=jnp.float32
        ).astype(jnp.bfloat16)
        head_grad = lax.dynamic_update_slice_in_dim(head_grad, block, origin * part_cols, axis=1)
    return (head_grad, hidden_grad.astype(jnp.bfloat16))


def solution(mesh):
    return jax.shard_map(
        shards,
        mesh=mesh,
        in_specs=(P("dp", "vocab"), P("dp", None), P("dp", "vocab"), P(), P(), P()),
        out_specs=(P("dp", "vocab"), P(("dp", "vocab"), None)),
        check_vma=False,
    )
```

time: 304 us -> 291 us (0.957); the launches traced: 303 us -> 286 us
  starting transfers between devices: 7.16 us -> 47.7 us
  blocking collectives: 44.3 us -> 13.6 us
  waiting for transfers between devices: 187 us -> 157 us
  between operations: 14 us -> 1.16 us
  local copies, waits for them, and re-layouts: 24.1 us -> 35 us
  other arithmetic: 9.02 us -> 16.4 us
    all_gather x2 -> x0, waiting for transfers between devices: 144 us -> none  [the longest x1 98.2 us: shards(): lax.all_gather(student_head, 'dp', axis=0, tiled=True)]
    all_to_all x2 -> x7, waiting for transfers between devices: 12.9 us -> 105 us  [the longest x1 48.5 us: shards(): lax.all_to_all(student_head.reshape(slab, planes, part_cols).transpose(1,...]
    ppermute x0 -> x9, waiting for transfers between devices: none -> 52.1 us  [the longest x3 31.3 us: halving_sum(): lax.ppermute(send, axis, pairs)]
    all_gather x5 -> x0, blocking collectives: 44.3 us -> none  [joined(): pieces = jax.tree.map(lambda part: lax.all_gather(part, axis), value)]
    all_to_all x2 -> x7, starting transfers between devices: 7.04 us -> 37 us  [the longest x4 23.8 us: exchange(): return lax.all_to_all(copies, axes, split_axis=0, concat_axis=0, tiled=True)]
    reduce_scatter x1 -> x0, waiting for transfers between devices: 28.8 us -> none  [shards(): lax.psum_scatter(partial_sums, 'vocab', scatter_dimension=0, tiled=True)]
    all_to_all x0 -> x1, blocking collectives: none -> 13.6 us  [shards(): lax.all_to_all(jnp.take(arrived, anchor, axis=0), 'dp', split_axis=0, con...]
    ppermute x0 -> x9, starting transfers between devices: none -> 10.7 us  [the longest x3 5.52 us: line_gather(): lax.ppermute(rising, axis, [(p, p + 1) for p in range(step, size - 1)])]
  transfers between devices with their start and end apart: 5 -> 16, of which waited for: 4 -> 10; matrix products, arithmetic and copies ran while one was open for 10% -> 14% of each run, Pallas kernels for 0% -> 0%
where the time goes in v1:
time: 291 us; the launch traced here: 286 us
  waiting for transfers between devices  157 us (54%)
  starting transfers between devices  47.7 us (16%)
  local copies, waits for them, and re-layouts  35 us (12%)
  other arithmetic  16.4 us (6%)
  matrix products  15.6 us (5%)
  blocking collectives  13.6 us (5%)
    all_to_all x1, waiting for transfers between devices, shards(): lax.all_to_all(student_head.reshape(slab, planes, part_cols).transpose(1,...  48.5 us
    all_to_all x4, waiting for transfers between devices, exchange(): return lax.all_to_all(copies, axes, split_axis=0, concat_axis=0, tiled=True)  42.2 us
    ppermute x3, waiting for transfers between devices, halving_sum(): lax.ppermute(send, axis, pairs)  31.3 us
    all_to_all x4, starting transfers between devices, exchange(): return lax.all_to_all(copies, axes, split_axis=0, concat_axis=0, tiled=True)  23.8 us
    gather x2, local copies, waits for them, and re-layouts, shards(): picked = jnp.take(teacher_logits, columns, axis=1)  16.7 us
    all_to_all x1, waiting for transfers between devices, shards(): lax.all_to_all(picked.reshape(tok_rows, shard_count * capacity, lane_coun...  14 us
    all_to_all x1, blocking collectives, shards(): lax.all_to_all(jnp.take(arrived, anchor, axis=0), 'dp', split_axis=0, con...  13.6 us
    ppermute x3, waiting for transfers between devices, line_gather(): lax.ppermute(falling, axis, [(p + 1, p) for p in range(size - 1 - step)])  12.7 us
  transfers between devices with their start and end apart: 16, of which 10 were waited for; matrix products, arithmetic and copies ran while one was open for 14% of the time, Pallas kernels for 0%

profile of v1, /device:TPU:0, one launch (start us, length us, event | category | flops | bytes accessed | tf_op | source)
XLA Modules:
  0.0 286.3 jit_solution(9834765727213962322)
XLA Ops:
  0.7 2.8 reduce_max.46
  3.5 2.6 exponential_reduce_fusion
  6.8 7.3 %all-to-all-start.5 = ((f32[32,2,128]{2,1,0:T(2,128)}), f32[32,2,128]{2,1,0:T(2,128)S(1)}, u32[]{:S(2)}, u32[]{:S(2)}) async-start(f32[32,2,128]{2,1,0:T(2,128)} %broadcast_in_dim.148), calls=%async_computation.5 | async-start | bytes 65536 | tf_op jit(solution)/shard_map/all_to_all | solution.py:12
  16.4 15.0 %gather_fusion.5 = bf16[4096,128]{1,0:T(8,128)(2,1)} fusion(bf16[128,8000]{0,1:T(8,128)(2,1)S(1)} %copy-done.2, s32[4096]{0:T(1024)S(1)} %broadcast_clamp_fusion), kind=kCustom, calls=%fused_computation.5 | custom fusion | bytes 2113536 | tf_op jit(solution)/shard_map/jit(_take)/gather | solution.py:86
  34.3 4.0 %all-to-all-start.3 = ((bf16[32,128,128]{2,1,0:T(8,128)(2,1)}), bf16[32,128,128]{2,1,0:T(8,128)(2,1)S(1)}, u32[]{:S(2)}, u32[]{:S(2)}) async-start(bf16[32,128,128]{2,1,0:T(8,128)(2,1)} %select_bitcast_fusion), calls=%async_computation.3 | async-start | bytes 2097152 | tf_op jit(solution)/shard_map/all_to_all | solution.py:87
  39.7 14.0 %all-to-all-done.3 = bf16[32,128,128]{2,1,0:T(8,128)(2,1)S(1)} async-done(((bf16[32,128,128]{2,1,0:T(8,128)(2,1)}), bf16[32,128,128]{2,1,0:T(8,128)(2,1)S(1)}, u32[]{:S(2)}, u32[]{:S(2)}) %all-to-all-start.3) | async-done | bytes 1048608 | tf_op jit(solution)/shard_map/all_to_all | solution.py:87
  54.4 4.6 %all-to-all-start = ((bf16[4,16,2304]{2,1,0:T(8,128)(2,1)}), bf16[4,16,2304]{2,1,0:T(8,128)(2,1)S(1)}, u32[]{:S(2)}, u32[]{:S(2)}) async-start(bf16[4,16,2304]{2,1,0:T(8,128)(2,1)} %broadcast_in_dim.85), calls=%async_computation | async-start | bytes 589824 | tf_op jit(solution)/shard_map/all_to_all | solution.py:12
  59.8 6.3 %all-to-all-done = bf16[4,16,2304]{2,1,0:T(8,128)(2,1)S(1)} async-done(((bf16[4,16,2304]{2,1,0:T(8,128)(2,1)}), bf16[4,16,2304]{2,1,0:T(8,128)(2,1)S(1)}, u32[]{:S(2)}, u32[]{:S(2)}) %all-to-all-start) | async-done | bytes 294944 | tf_op jit(solution)/shard_map/all_to_all | solution.py:12
  66.1 13.6 %all_to_all.40 = bf16[16,128,128]{2,1,0:T(8,128)(2,1)S(1)} all-to-all(bf16[16,128,128]{2,1,0:T(8,128)(2,1)S(1)} %broadcast_select_fusion), channel_id=1, replica_groups=mesh['dp'=4,'vocab'=8] {'dp'}, dimensions={0} | all-to-all | bytes 1048576 | tf_op jit(solution)/shard_map/all_to_all | solution.py:96
  81.3 7.1 %all-to-all-start.1 = ((bf16[8,4,16,2304]{3,2,1,0:T(8,128)(2,1)}), bf16[8,4,16,2304]{3,2,1,0:T(8,128)(2,1)S(1)}, u32[]{:S(2)}, u32[]{:S(2)}) async-start(bf16[8,4,16,2304]{3,2,1,0:T(8,128)(2,1)} %broadcast_in_dim.134), calls=%async_computation.1 | async-start | bytes 4718592 | tf_op jit(solution)/shard_map/all_to_all | solution.py:12
  88.4 3.3 %copy.63 = bf16[72,4,8,512]{3,2,0,1:T(8,128)(2,1)} copy(bf16[72,4,8,512]{3,2,1,0:T(8,128)(2,1)} %bitcast.110) | data formatting | bytes 4718592 | tf_op jit(solution)/shard_map/reshape | solution.py:61
  91.7 26.1 %all-to-all-done.1 = bf16[8,4,16,2304]{3,2,1,0:T(8,128)(2,1)S(1)} async-done(((bf16[8,4,16,2304]{3,2,1,0:T(8,128)(2,1)}), bf16[8,4,16,2304]{3,2,1,0:T(8,128)(2,1)S(1)}, u32[]{:S(2)}, u32[]{:S(2)}) %all-to-all-start.1) | async-done | bytes 2359328 | tf_op jit(solution)/shard_map/all_to_all | solution.py:12
  117.8 4.5 %all-to-all-start.2 = ((bf16[4,576,512]{2,1,0:T(8,128)(2,1)}), bf16[4,576,512]{2,1,0:T(8,128)(2,1)}, u32[]{:S(2)}, u32[]{:S(2)}) async-start(bf16[4,576,512]{2,1,0:T(8,128)(2,1)} %bitcast.106), calls=%async_computation.2 | async-start | bytes 4718592 | tf_op jit(solution)/shard_map/all_to_all | solution.py:60
  125.2 48.5 %all-to-all-done.2 = bf16[4,576,512]{2,1,0:T(8,128)(2,1)} async-done(((bf16[4,576,512]{2,1,0:T(8,128)(2,1)}), bf16[4,576,512]{2,1,0:T(8,128)(2,1)}, u32[]{:S(2)}, u32[]{:S(2)}) %all-to-all-start.2) | async-done | bytes 2359328 | tf_op jit(solution)/shard_map/all_to_all | solution.py:60
  173.7 3.8 %fusion.41 = (f32[512]{0:T(512)S(1)}, f32[512,512]{1,0:T(8,128)S(1)}) fusion(bf16[512,2304]{1,0:T(8,128)(2,1)} %bitcast.111, bf16[2304,512]{1,0:T(8,128)(2,1)} %bitcast.5, pred[512]{0:T(512)(128)(4,1)S(1)} %get-tuple-element.18), kind=kOutput, calls=%fused_computation.114 | convolution fusion | flops 1208483328 | bytes 5769728 | tf_op jit(solution)/shard_map/dot_general | solution.py:127
  178.7 4.8 %all-to-all-start.6 = ((f32[32,3,512]{2,1,0:T(4,128)}), f32[32,3,512]{2,1,0:T(4,128)S(1)}, u32[]{:S(2)}, u32[]{:S(2)}) async-start(f32[32,3,512]{2,1,0:T(4,128)} %broadcast_in_dim.150), calls=%async_computation.6 | async-start | bytes 524288 | tf_op jit(solution)/shard_map/all_to_all | solution.py:12
  184.2 9.8 %all-to-all-done.6 = f32[32,3,512]{2,1,0:T(4,128)S(1)} async-done(((f32[32,3,512]{2,1,0:T(4,128)}), f32[32,3,512]{2,1,0:T(4,128)S(1)}, u32[]{:S(2)}, u32[]{:S(2)}) %all-to-all-start.6) | async-done | bytes 196640 | tf_op jit(solution)/shard_map/all_to_all | solution.py:12
  194.8 3.3 %fusion.42 = f32[4,8,16,2304]{3,2,1,0:T(8,128)S(1)} fusion(bf16[4,8,16,512]{3,2,1,0:T(8,128)(2,1)S(1)} %bitcast.116, bf16[2304,512,1,1]{1,0,3,2:T(8,128)(2,1)} %bitcast.33), kind=kOutput, calls=%fused_computation.115 | convolution fusion | flops 1207959552 | bytes 7602176 | tf_op jit(solution)/shard_map/dot_general | solution.py:140
  198.3 1.9 copy-done.3
  200.2 4.7 %collective-permute-done.6 = f32[4,1,4,16,2304]{4,3,0,2,1:T(8,128)} collective-permute-done((f32[4,1,4,16,2304]{4,3,0,2,1:T(8,128)S(1)}, f32[4,1,4,16,2304]{4,3,0,2,1:T(8,128)}, u32[]{:S(2)}, u32[]{:S(2)}) %collective-permute-start.6) | collective-permute-done | bytes 2359328 | tf_op jit(solution)/shard_map/ppermute | solution.py:39
  204.9 2.6 bitcast_add_fusion
  210.4 26.6 %collective-permute-done.7 = f32[2,1,4,16,2304]{4,3,0,2,1:T(8,128)} collective-permute-done((f32[2,1,4,16,2304]{4,3,0,2,1:T(8,128)}, f32[2,1,4,16,2304]{4,3,0,2,1:T(8,128)}, u32[]{:S(2)}, u32[]{:S(2)}) %collective-permute-start.7) | collective-permute-done | bytes 1179680 | tf_op jit(solution)/shard_map/ppermute | solution.py:39
  240.4 3.4 %collective-permute-start = (bf16[512,512]{1,0:T(8,128)(2,1)S(1)}, bf16[512,512]{1,0:T(8,128)(2,1)}, u32[]{:S(2)}, u32[]{:S(2)}) collective-permute-start(bf16[512,512]{1,0:T(8,128)(2,1)S(1)} %copy-done.8), channel_id=1, source_target_pairs={{0,8},{8,16},{16,24},{1,9},{9,17},{17,25},{2,10},{10,18},{18,26},{... | collective-permute-start | bytes 1572872 | tf_op jit(solution)/shard_map/ppermute | solution.py:20
  245.0 8.2 %collective-permute-done = bf16[512,512]{1,0:T(8,128)(2,1)} collective-permute-done((bf16[512,512]{1,0:T(8,128)(2,1)S(1)}, bf16[512,512]{1,0:T(8,128)(2,1)}, u32[]{:S(2)}, u32[]{:S(2)}) %collective-permute-start) | collective-permute-done | bytes 524320 | tf_op jit(solution)/shard_map/ppermute | solution.py:20
  254.7 3.8 %collective-permute-done.2 = bf16[512,512]{1,0:T(8,128)(2,1)} collective-permute-done((bf16[512,512]{1,0:T(8,128)(2,1)}, bf16[512,512]{1,0:T(8,128)(2,1)}, u32[]{:S(2)}, u32[]{:S(2)}) %collective-permute-start.2) | collective-permute-done | bytes 524320 | tf_op jit(solution)/shard_map/ppermute | solution.py:21
  259.8 2.0 add_bitcast_fusion
  261.7 4.7 %all-to-all-start.7 = ((f32[4,16,2304]{2,1,0:T(8,128)}), f32[4,16,2304]{2,1,0:T(8,128)S(1)}, u32[]{:S(2)}, u32[]{:S(2)}) async-start(f32[4,16,2304]{2,1,0:T(8,128)} %add_bitcast_fusion), calls=%async_computation.7 | async-start | bytes 1179648 | tf_op jit(solution)/shard_map/all_to_all | solution.py:147
  266.7 2.3 fusion.3
  269.8 8.9 %collective-permute-done.3 = bf16[512,512]{1,0:T(8,128)(2,1)} collective-permute-done((bf16[512,512]{1,0:T(8,128)(2,1)}, bf16[512,512]{1,0:T(8,128)(2,1)}, u32[]{:S(2)}, u32[]{:S(2)}) %collective-permute-start.3) | collective-permute-done | bytes 524320 | tf_op jit(solution)/shard_map/ppermute | solution.py:21
  278.7 2.1 fusion.2
  280.8 2.1 fusion.1
  282.9 1.9 fusion
  (91 shorter events, 28.6 us)
Async XLA Ops:
  0.6 39.0 %copy-start = (bf16[128,2304]{1,0:T(8,128)(2,1)S(1)}, bf16[128,2304]{1,0:T(8,128)(2,1)}, u32[]{:S(2)}) copy-start(bf16[128,2304]{1,0:T(8,128)(2,1)} %param.7) | copy-start | bytes 1769476
  0.6 15.8 %copy-start.2 = (bf16[128,8000]{0,1:T(8,128)(2,1)S(1)}, bf16[128,8000]{0,1:T(8,128)(2,1)}, u32[]{:S(2)}) copy-start(bf16[128,8000]{0,1:T(8,128)(2,1)} %param.6) | copy-start | bytes 6144004
  0.7 13.5 %copy-start.9 = (s32[128,128]{1,0:T(8,128)S(1)}, s32[128,128]{1,0:T(8,128)}, u32[]{:S(2)}) copy-start(s32[128,128]{1,0:T(8,128)} %param.9) | copy-start | bytes 196612
  0.7 13.7 %copy-start.10 = (s32[128]{0:T(128)S(1)}, s32[128]{0:T(128)}, u32[]{:S(2)}) copy-start(s32[128]{0:T(128)} %param.10) | copy-start | bytes 1540
  0.7 14.9 %copy-start.1 = (s32[128]{0:T(128)S(1)}, s32[128]{0:T(128)}, u32[]{:S(2)}) copy-start(s32[128]{0:T(128)} %param.11) | copy-start | bytes 1540
  6.8 27.5 %all-to-all-start.5 = ((f32[32,2,128]{2,1,0:T(2,128)}), f32[32,2,128]{2,1,0:T(2,128)S(1)}, u32[]{:S(2)}, u32[]{:S(2)}) async-start(f32[32,2,128]{2,1,0:T(2,128)} %broadcast_in_dim.148), calls=%async_computation.5 | async-start | bytes 65536 | tf_op jit(solution)/shard_map/all_to_all | solution.py:12
  34.3 19.3 %all-to-all-start.3 = ((bf16[32,128,128]{2,1,0:T(8,128)(2,1)}), bf16[32,128,128]{2,1,0:T(8,128)(2,1)S(1)}, u32[]{:S(2)}, u32[]{:S(2)}) async-start(bf16[32,128,128]{2,1,0:T(8,128)(2,1)} %select_bitcast_fusion), calls=%async_computation.3 | async-start | bytes 2097152 | tf_op jit(solution)/shard_map/all_to_all | solution.py:87
  54.4 11.7 %all-to-all-start = ((bf16[4,16,2304]{2,1,0:T(8,128)(2,1)}), bf16[4,16,2304]{2,1,0:T(8,128)(2,1)S(1)}, u32[]{:S(2)}, u32[]{:S(2)}) async-start(bf16[4,16,2304]{2,1,0:T(8,128)(2,1)} %broadcast_in_dim.85), calls=%async_computation | async-start | bytes 589824 | tf_op jit(solution)/shard_map/all_to_all | solution.py:12
  81.3 36.6 %all-to-all-start.1 = ((bf16[8,4,16,2304]{3,2,1,0:T(8,128)(2,1)}), bf16[8,4,16,2304]{3,2,1,0:T(8,128)(2,1)S(1)}, u32[]{:S(2)}, u32[]{:S(2)}) async-start(bf16[8,4,16,2304]{3,2,1,0:T(8,128)(2,1)} %broadcast_in_dim.134), calls=%async_computation.1 | async-start | bytes 4718592 | tf_op jit(solution)/shard_map/all_to_all | solution.py:12
  117.8 55.9 %all-to-all-start.2 = ((bf16[4,576,512]{2,1,0:T(8,128)(2,1)}), bf16[4,576,512]{2,1,0:T(8,128)(2,1)}, u32[]{:S(2)}, u32[]{:S(2)}) async-start(bf16[4,576,512]{2,1,0:T(8,128)(2,1)} %bitcast.106), calls=%async_computation.2 | async-start | bytes 4718592 | tf_op jit(solution)/shard_map/all_to_all | solution.py:60
  178.7 15.3 %all-to-all-start.6 = ((f32[32,3,512]{2,1,0:T(4,128)}), f32[32,3,512]{2,1,0:T(4,128)S(1)}, u32[]{:S(2)}, u32[]{:S(2)}) async-start(f32[32,3,512]{2,1,0:T(4,128)} %broadcast_in_dim.150), calls=%async_computation.6 | async-start | bytes 524288 | tf_op jit(solution)/shard_map/all_to_all | solution.py:12
  194.8 3.3 %copy-start.7 = (bf16[512,512]{1,0:T(8,128)(2,1)}, bf16[512,512]{1,0:T(8,128)(2,1)S(1)}, u32[]{:S(2)}) copy-start(bf16[512,512]{1,0:T(8,128)(2,1)S(1)} %multiply_convert_fusion) | copy-start | bytes 1572868
  198.1 2.1 copy-start.3
  200.2 4.7 %collective-permute-start.6 = (f32[4,1,4,16,2304]{4,3,0,2,1:T(8,128)S(1)}, f32[4,1,4,16,2304]{4,3,0,2,1:T(8,128)}, u32[]{:S(2)}, u32[]{:S(2)}) collective-permute-start(f32[4,1,4,16,2304]{4,3,0,2,1:T(8,128)S(1)} %dynamic-slice_bitcast_fusion), channel_id=1, source_target_pairs={{0,1},{1,0},{2,3},{3,2},{4,5},{5,4},{6,7},{7,6},{8,9},{9,8},{10,11... | collective-permute-start | bytes 7077896 | tf_op jit(solution)/shard_map/ppermute | solution.py:39
  207.5 1.5 copy-start.8
  208.6 28.3 %collective-permute-start.7 = (f32[2,1,4,16,2304]{4,3,0,2,1:T(8,128)}, f32[2,1,4,16,2304]{4,3,0,2,1:T(8,128)}, u32[]{:S(2)}, u32[]{:S(2)}) collective-permute-start(f32[2,1,4,16,2304]{4,3,0,2,1:T(8,128)} %dynamic-slice_bitcast_fusion.1), channel_id=1, source_target_pairs={{0,2},{1,3},{2,0},{3,1},{4,6},{5,7},{6,4},{7,5},{8,10},{9,11},{10,... | collective-permute-start | bytes 3538952 | tf_op jit(solution)/shard_map/ppermute | solution.py:39
  209.1 34.6 %collective-permute-start.1 = (bf16[512,512]{1,0:T(8,128)(2,1)S(1)}, bf16[512,512]{1,0:T(8,128)(2,1)}, u32[]{:S(2)}, u32[]{:S(2)}) collective-permute-start(bf16[512,512]{1,0:T(8,128)(2,1)S(1)} %copy-done.8), channel_id=1, source_target_pairs={{8,0},{16,8},{24,16},{9,1},{17,9},{25,17},{10,2},{18,10},{26,18},{... | collective-permute-start | bytes 1572872 | tf_op jit(solution)/shard_map/ppermute | solution.py:21
  238.4 1.0 copy-start.4
  239.4 20.3 %collective-permute-start.8 = (f32[1,1,4,16,2304]{4,3,0,2,1:T(8,128)S(1)}, f32[1,1,4,16,2304]{4,3,0,2,1:T(8,128)S(1)}, u32[]{:S(2)}, u32[]{:S(2)}) collective-permute-start(f32[1,1,4,16,2304]{4,3,0,2,1:T(8,128)S(1)} %constant_dynamic-slice_fusion), channel_id=1, source_target_pairs={{0,4},{1,5},{2,6},{3,7},{4,0},{5,1},{6,2},{7,3},{8,12},{9,13},{10,... | collective-permute-start | bytes 1769480 | tf_op jit(solution)/shard_map/ppermute | solution.py:39
  240.4 12.9 %collective-permute-start = (bf16[512,512]{1,0:T(8,128)(2,1)S(1)}, bf16[512,512]{1,0:T(8,128)(2,1)}, u32[]{:S(2)}, u32[]{:S(2)}) collective-permute-start(bf16[512,512]{1,0:T(8,128)(2,1)S(1)} %copy-done.8), channel_id=1, source_target_pairs={{0,8},{8,16},{16,24},{1,9},{9,17},{17,25},{2,10},{10,18},{18,26},{... | collective-permute-start | bytes 1572872 | tf_op jit(solution)/shard_map/ppermute | solution.py:20
  243.7 14.7 %collective-permute-start.2 = (bf16[512,512]{1,0:T(8,128)(2,1)}, bf16[512,512]{1,0:T(8,128)(2,1)}, u32[]{:S(2)}, u32[]{:S(2)}) collective-permute-start(bf16[512,512]{1,0:T(8,128)(2,1)} %collective-permute-done.1), channel_id=1, source_target_pairs={{8,0},{16,8},{9,1},{17,9},{10,2},{18,10},{11,3},{19,11},{12,4},{20... | collective-permute-start | bytes 1572872 | tf_op jit(solution)/shard_map/ppermute | solution.py:21
  253.2 15.8 %collective-permute-start.4 = (bf16[512,512]{1,0:T(8,128)(2,1)}, bf16[512,512]{1,0:T(8,128)(2,1)}, u32[]{:S(2)}, u32[]{:S(2)}) collective-permute-start(bf16[512,512]{1,0:T(8,128)(2,1)} %collective-permute-done), channel_id=1, source_target_pairs={{8,16},{16,24},{9,17},{17,25},{10,18},{18,26},{11,19},{19,27},{12,... | collective-permute-start | bytes 1572872 | tf_op jit(solution)/shard_map/ppermute | solution.py:20
  258.5 20.2 %collective-permute-start.3 = (bf16[512,512]{1,0:T(8,128)(2,1)}, bf16[512,512]{1,0:T(8,128)(2,1)}, u32[]{:S(2)}, u32[]{:S(2)}) collective-permute-start(bf16[512,512]{1,0:T(8,128)(2,1)} %collective-permute-done.2), channel_id=1, source_target_pairs={{8,0},{9,1},{10,2},{11,3},{12,4},{13,5},{14,6},{15,7}} | collective-permute-start | bytes 1572872 | tf_op jit(solution)/shard_map/ppermute | solution.py:21
  261.7 23.2 %all-to-all-start.7 = ((f32[4,16,2304]{2,1,0:T(8,128)}), f32[4,16,2304]{2,1,0:T(8,128)S(1)}, u32[]{:S(2)}, u32[]{:S(2)}) async-start(f32[4,16,2304]{2,1,0:T(8,128)} %add_bitcast_fusion), calls=%async_computation.7 | async-start | bytes 1179648 | tf_op jit(solution)/shard_map/all_to_all | solution.py:147
  266.4 12.3 %copy-start.6 = (bf16[8,4,16,2304]{3,2,0,1:T(8,128)(2,1)S(1)}, bf16[8,4,16,2304]{3,2,0,1:T(8,128)(2,1)}, u32[]{:S(2)}) copy-start(bf16[8,4,16,2304]{3,2,0,1:T(8,128)(2,1)} %copy.30) | copy-start | bytes 7077892
  269.1 13.9 %collective-permute-start.5 = (bf16[512,512]{1,0:T(8,128)(2,1)}, bf16[512,512]{1,0:T(8,128)(2,1)S(1)}, u32[]{:S(2)}, u32[]{:S(2)}) collective-permute-start(bf16[512,512]{1,0:T(8,128)(2,1)} %collective-permute-done.4), channel_id=1, source_target_pairs={{16,24},{17,25},{18,26},{19,27},{20,28},{21,29},{22,30},{23,31}} | collective-permute-start | bytes 1572872 | tf_op jit(solution)/shard_map/ppermute | solution.py:20
  284.9 1.4 copy-start.5

commit v2 on v1

v2 whole, which is shorter than its diff:
```python
import jax
import jax.numpy as jnp
from jax import lax
from jax.sharding import PartitionSpec as P


loss_scale = 8192.0


def exchange(value, axes):
    count = lax.axis_size(axes)
    copies = jnp.broadcast_to(value[None], (count,) + value.shape)
    return lax.all_to_all(copies, axes, split_axis=0, concat_axis=0, tiled=True)


def shift(value, axis, distance):
    size = lax.axis_size(axis)
    return lax.ppermute(value, axis, [(p, (p + distance) % size) for p in range(size)])


def above(axis, distance):
    size = lax.axis_size(axis)
    return lax.rem(lax.axis_index(axis) + size + distance, size)


def spread(value, axis):
    size = lax.axis_size(axis)
    index = lax.axis_index(axis)
    if size != 4:
        return [(above(axis, -d), shift(value, axis, d)) for d in range(1, size)]
    middle = shift(value, axis, 2)
    rising = lax.ppermute(value, axis, [(p, p + 1) for p in range(size - 1)])
    falling = lax.ppermute(value, axis, [(p + 1, p) for p in range(size - 1)])
    relay = lax.ppermute(middle, axis, [(1, 0), (2, 3)])
    first, last = index == 0, index == size - 1
    near = jnp.where(first, falling, rising)
    far = jnp.where(first | last, relay, falling)
    return [
        (jnp.where(first, 1, index - 1), near),
        (lax.rem(index + 2, size), middle),
        (jnp.where(first, size - 1, jnp.where(last, 0, index + 1)), far),
    ]


def direct_sum(part, axis):
    size = lax.axis_size(axis)
    index = lax.axis_index(axis)
    far = lax.ppermute(part(1 - index % 2), axis, [(i, i ^ 1) for i in range(size)])
    value = part(index % 2) + far
    total = lax.dynamic_index_in_dim(value, index // 2, 0, keepdims=False)
    for step in range(1, size // 2):
        send = lax.dynamic_index_in_dim(value, (index // 2) ^ step, 0, keepdims=False)
        send = lax.ppermute(send, axis, [(i, i ^ (2 * step)) for i in range(size)])
        total = total + send
    return total


def in_order(pieces, axis):
    size = len(pieces)
    order = lax.rem(lax.axis_index(axis) + size - jnp.arange(size, dtype=jnp.int32), size)
    return jnp.take(jnp.stack(pieces), order, axis=0, mode="clip")


def shards(teacher_logits, student_hidden, student_head, keep_ids, block_owner, block_count):
    planes = lax.axis_size("dp")
    plane = lax.axis_index("dp")
    shard_count = lax.axis_size("vocab")
    my_shard = lax.axis_index("vocab")
    tok_rows, vocab_rows = teacher_logits.shape
    slab, own_cols = student_head.shape
    width = student_hidden.shape[1]
    lane_count = keep_ids.shape[1]
    kept_blocks = block_owner.shape[0] // shard_count
    part_blocks = kept_blocks // planes
    part_cols = own_cols // planes
    slice_rows = tok_rows // shard_count
    tokens = planes * tok_rows
    capacity = (2 * kept_blocks + shard_count - 1) // shard_count

    pieces = []
    for distance in range(planes):
        piece = lax.dynamic_slice_in_dim(
            student_head, above("dp", distance) * part_cols, part_cols, 1
        )
        pieces.append(shift(piece, "dp", distance) if distance else piece)

    hidden_slice = lax.dynamic_slice_in_dim(student_hidden, my_shard * slice_rows, slice_rows)
    hidden = [shift(hidden_slice, "dp", d) if d else hidden_slice for d in range(planes)]
    hidden = in_order(hidden, "dp")
    hidden = exchange(hidden, "vocab").reshape(tokens, width)

    numbers = jnp.arange(block_owner.shape[0], dtype=jnp.int32)
    lane_index = jnp.arange(lane_count, dtype=jnp.int32)
    source = keep_ids[:, 0] // vocab_rows
    owner_before = (block_owner[None, :] == block_owner[:, None]) & (
        numbers[None, :] < numbers[:, None]
    )
    ordinal = jnp.sum(owner_before.astype(jnp.int32), axis=1)
    pair_rank = jnp.sum(
        (owner_before & (source[None, :] == source[:, None])).astype(jnp.int32), axis=1
    )
    send_slots = jnp.arange(shard_count * capacity, dtype=jnp.int32)
    outgoing = (
        (source == my_shard)[None, :]
        & (block_owner[None, :] == (send_slots // capacity)[:, None])
        & (pair_rank[None, :] == (send_slots % capacity)[:, None])
    )
    chosen = jnp.sum(jnp.where(outgoing, numbers[None, :], 0), axis=1)
    columns = jnp.clip(keep_ids[chosen] - my_shard * vocab_rows, 0, vocab_rows - 1).reshape(-1)
    incoming = (block_owner[None, :] == my_shard) & (
        ordinal[None, :] == jnp.arange(kept_blocks, dtype=jnp.int32)[:, None]
    )
    own_blocks = jnp.sum(jnp.where(incoming, numbers[None, :], 0), axis=1)
    anchor = source[own_blocks] * (capacity + 1) + pair_rank[own_blocks]
    valid = lane_index[None, :] < block_count[own_blocks][:, None]

    values = teacher_logits.astype(jnp.float32)
    local_peak = jnp.max(values, axis=1)
    local_total = jnp.sum(jnp.exp(values - local_peak[:, None]), axis=1)
    terms = [local_peak]
    for _ in range(3):
        terms.append(lax.reduce_precision(local_total, 8, 7))
        local_total = local_total - terms[-1]
    terms = jnp.stack(terms, axis=1).astype(jnp.bfloat16)
    terms = jnp.pad(terms, ((0, 0), (0, lane_count - terms.shape[1])))

    picked = jnp.take(teacher_logits, columns, axis=1, mode="clip")
    picked = picked.reshape(tok_rows, shard_count, capacity, lane_count).transpose(1, 2, 0, 3)
    terms = jnp.broadcast_to(terms, (shard_count, 1, tok_rows, lane_count))
    picked = jnp.concatenate([picked, terms], axis=1)
    hidden, picked = lax.optimization_barrier((hidden, picked))
    arrived = lax.all_to_all(picked, "vocab", split_axis=0, concat_axis=0, tiled=True)
    stats = arrived[:, capacity, :, :4].astype(jnp.float32)
    totals = stats[:, :, 1] + stats[:, :, 2] + stats[:, :, 3]
    peak = jnp.max(stats[:, :, 0], axis=0)
    total = jnp.sum(totals * jnp.exp(stats[:, :, 0] - peak), axis=0)

    arrived = arrived.reshape(shard_count * (capacity + 1), tok_rows, lane_count)
    target = jnp.take(arrived, anchor, axis=0, mode="clip").astype(jnp.float32)
    target = jnp.where(
        valid[:, None, :], jnp.exp(target - peak[None, :, None]) / total[None, :, None], 0.0
    ).astype(jnp.bfloat16)
    mass_part = jnp.sum(target.astype(jnp.float32), axis=(0, 2))

    target = target.reshape(planes, part_blocks, tok_rows, lane_count)
    kept = []
    for distance in range(planes):
        piece = lax.dynamic_index_in_dim(target, above("dp", distance), 0, keepdims=False)
        kept.append(shift(piece, "dp", distance) if distance else piece)
    valid_cols = lax.dynamic_slice_in_dim(valid, plane * part_blocks, part_blocks).reshape(1, -1)

    scores = sum(
        jnp.dot(
            lax.dynamic_slice_in_dim(hidden, above("dp", -distance) * slab, slab, axis=1),
            piece, preferred_element_type=jnp.float32,
        )
        for distance, piece in enumerate(pieces)
    )
    masked = jnp.where(valid_cols, scores, -jnp.inf)
    local_top = jnp.max(masked, axis=1)
    weight = jnp.where(valid_cols, jnp.exp(masked - local_top[:, None]), 0.0)
    student = jnp.concatenate([local_top, jnp.sum(weight, axis=1), mass_part])
    pieces, kept, student = lax.optimization_barrier((pieces, kept, student))
    kept = in_order(kept, "dp").reshape(
        planes, part_blocks, shard_count, slice_rows, lane_count
    ).transpose(2, 0, 3, 1, 4).reshape(tokens, part_cols).astype(jnp.float32)
    student = exchange(student.reshape(-1, tok_rows), ("dp", "vocab")).reshape(
        planes * shard_count, 2 * planes + 1, tok_rows
    )
    tops, norms = student[:, :planes], student[:, planes : 2 * planes]
    student_top = jnp.max(tops, axis=0)
    exp_norm = jnp.sum(norms * jnp.exp(tops - student_top), axis=0)
    kept_mass = jnp.sum(student[:, 2 * planes].reshape(planes, shard_count, tok_rows), axis=1)
    kept_mass = kept_mass.reshape(planes, shard_count, slice_rows).transpose(1, 0, 2).reshape(-1)
    factor = jnp.exp(local_top - student_top.reshape(-1)) / exp_norm.reshape(-1) * kept_mass
    gradient = (loss_scale * (weight * factor[:, None] - kept)).astype(jnp.bfloat16)

    gradients = [(plane, gradient)] + spread(gradient, "dp")

    head = in_order(pieces, "dp").reshape(width, part_cols)
    by_pair = gradient.reshape(shard_count // 2, 2, planes * slice_rows, part_cols)

    def part(last_bit):
        rows = lax.dynamic_index_in_dim(by_pair, last_bit, 1, keepdims=False)
        product = lax.dot_general(
            rows.reshape(-1, part_cols), head, (((1,), (1,)), ((), ())),
            preferred_element_type=jnp.float32,
        )
        return product.reshape(shard_count // 2, planes, slice_rows, width)

    sums = direct_sum(part, "vocab")
    sums = lax.all_to_all(sums, "dp", split_axis=0, concat_axis=0, tiled=True)
    hidden_grad = jnp.sum(sums, axis=0).astype(jnp.bfloat16)

    own_hidden = lax.dynamic_slice_in_dim(hidden, plane * slab, slab, axis=1)
    head_grad = jnp.zeros((slab, own_cols), jnp.bfloat16)
    for origin, columns_part in gradients:
        block = lax.dot_general(
            own_hidden, columns_part, (((0,), (0,)), ((), ())), preferred_element_type=jnp.float32
        ).astype(jnp.bfloat16)
        head_grad = lax.dynamic_update_slice_in_dim(head_grad, block, origin * part_cols, axis=1)
    return (head_grad, hidden_grad)


def solution(mesh):
    return jax.shard_map(
        shards,
        mesh=mesh,
        in_specs=(P("dp", "vocab"), P("dp", None), P("dp", "vocab"), P(), P(), P()),
        out_specs=(P("dp", "vocab"), P(("dp", "vocab"), None)),
        check_vma=False,
    )
```

time: 291 us -> 192 us (0.66); the launches traced: 286 us -> 191 us
  waiting for transfers between devices: 157 us -> 62.7 us
  blocking collectives: 13.6 us -> 0 us
  matrix products: 15.6 us -> 21.1 us
  starting transfers between devices: 47.7 us -> 51.6 us
    all_to_all x3 -> x2, waiting for transfers between devices: 62.5 us -> 6.48 us  [the longest x1 6.48 us: shards(): lax.all_to_all(picked, 'vocab', split_axis=0, concat_axis=0, tiled=True)]
    all_to_all x4 -> x2, waiting for transfers between devices: 42.2 us -> 8.69 us  [exchange(): return lax.all_to_all(copies, axes, split_axis=0, concat_axis=0, tiled=True)]
    ppermute x9 -> x17, starting transfers between devices: 10.7 us -> 28.9 us  [the longest x10 18.7 us: shift(): lax.ppermute(value, axis, [(p, (p + distance) % size) for p in range(size)])]
    all_to_all x1 -> x0, blocking collectives: 13.6 us -> none  [shards(): lax.all_to_all(jnp.take(arrived, anchor, axis=0), 'dp', split_axis=0, con...]
    all_to_all x4 -> x2, starting transfers between devices: 23.8 us -> 12.2 us  [exchange(): return lax.all_to_all(copies, axes, split_axis=0, concat_axis=0, tiled=True)]
    dot_general x2 -> x6, matrix products: 7.11 us -> 12.3 us  [the longest x4 7.63 us: shards(): jnp.dot(lax.dynamic_slice_in_dim(hidden, above('dp', -distance) * slab, s...]
    ppermute x9 -> x17, waiting for transfers between devices: 52.1 us -> 47.5 us  [the longest x10 26.5 us: shift(): lax.ppermute(value, axis, [(p, (p + distance) % size) for p in range(size)])]
    dynamic_slice x0 -> x2, local copies, waits for them, and re-layouts: none -> 3.95 us  [the longest x1 2.88 us: shards(): lax.dynamic_slice_in_dim(student_head, above('dp', distance) * part_cols,...]
  transfers between devices with their start and end apart: 16 -> 21, of which waited for: 10 -> 10; matrix products, arithmetic and copies ran while one was open for 14% -> 29% of each run, Pallas kernels for 0% -> 0%
where the time goes in v2:
time: 192 us; the launch traced here: 191 us
  waiting for transfers between devices  62.7 us (33%)
  starting transfers between devices  51.6 us (27%)
  local copies, waits for them, and re-layouts  37.5 us (20%)
  matrix products  21.1 us (11%)
  other arithmetic  17.3 us (9%)
    ppermute x10, waiting for transfers between devices, shift(): lax.ppermute(value, axis, [(p, (p + distance) % size) for p in range(size)])  26.5 us
    ppermute x10, starting transfers between devices, shift(): lax.ppermute(value, axis, [(p, (p + distance) % size) for p in range(size)])  18.7 us
    gather x1, local copies, waits for them, and re-layouts, shards(): picked = jnp.take(teacher_logits, columns, axis=1, mode='clip')  14.9 us
    all_to_all x2, starting transfers between devices, exchange(): return lax.all_to_all(copies, axes, split_axis=0, concat_axis=0, tiled=True)  12.2 us
    ppermute x1, waiting for transfers between devices, spread(): relay = lax.ppermute(middle, axis, [(1, 0), (2, 3)])  10.3 us
    dot_general x4, matrix products, shards(): lax.dot_general(own_hidden, columns_part, (((0,), (0,)), ((), ())), prefe...  8.75 us
    all_to_all x2, waiting for transfers between devices, exchange(): return lax.all_to_all(copies, axes, split_axis=0, concat_axis=0, tiled=True)  8.69 us
    dot_general x4, matrix products, shards(): jnp.dot(lax.dynamic_slice_in_dim(hidden, above('dp', -distance) * slab, s...  7.63 us
  transfers between devices with their start and end apart: 21, of which 10 were waited for; matrix products, arithmetic and copies ran while one was open for 29% of the time, Pallas kernels for 0%

profile of v2, /device:TPU:0, one launch (start us, length us, event | category | flops | bytes accessed | tf_op | source)
XLA Modules:
  0.0 191.3 jit_solution(17533988415222404083)
XLA Ops:
  1.7 3.1 %collective-permute-start = (bf16[16,2304]{1,0:T(8,128)(2,1)S(1)}, bf16[16,2304]{1,0:T(8,128)(2,1)S(1)}, u32[]{:S(2)}, u32[]{:S(2)}) collective-permute-start(bf16[16,2304]{1,0:T(8,128)(2,1)S(1)} %constant_dynamic-slice_fusion.7), channel_id=1, source_target_pairs={{0,8},{8,16},{16,24},{24,0},{1,9},{9,17},{17,25},{25,1},{2,10},{10... | collective-permute-start | bytes 221192 | tf_op jit(solution)/shard_map/ppermute | solution.py:18
  4.8 2.6 %collective-permute-start.1 = (bf16[16,2304]{1,0:T(8,128)(2,1)S(1)}, bf16[16,2304]{1,0:T(8,128)(2,1)S(1)}, u32[]{:S(2)}, u32[]{:S(2)}) collective-permute-start(bf16[16,2304]{1,0:T(8,128)(2,1)S(1)} %constant_dynamic-slice_fusion.7), channel_id=1, source_target_pairs={{0,16},{8,24},{16,0},{24,8},{1,17},{9,25},{17,1},{25,9},{2,18},{10... | collective-permute-start | bytes 221192 | tf_op jit(solution)/shard_map/ppermute | solution.py:18
  8.7 2.9 %constant_dynamic-slice_fusion.2 = (bf16[576,512]{1,0:T(8,128)(2,1)}, bf16[576,512]{1,0:T(8,128)(2,1)}, bf16[576,512]{1,0:T(8,128)(2,1)S(1)}, bf16[576,512]{1,0:T(8,128)(2,1)}) fusion(bf16[576,2048]{1,0:T(8,128)(2,1)} %param.8, s32[]{:T(128)S(6)} %select_n.214, s32[]{:T(128)S(6)} %select_n.210, s32[]{:T(128)S(6)} %select_n.208, s32[]{:T(128)S(6)} %select_n.212), kind=kLoop, calls=%fused_computation.99 | loop fusion | bytes 4718608 | tf_op jit(solution)/shard_map/dynamic_slice | solution.py:82
  12.3 3.1 %collective-permute-start.5 = (bf16[576,512]{1,0:T(8,128)(2,1)}, bf16[576,512]{1,0:T(8,128)(2,1)}, u32[]{:S(2)}, u32[]{:S(2)}) collective-permute-start(bf16[576,512]{1,0:T(8,128)(2,1)} %get-tuple-element.35), channel_id=1, source_target_pairs={{0,24},{8,0},{16,8},{24,16},{1,25},{9,1},{17,9},{25,17},{2,26},{10... | collective-permute-start | bytes 1769480 | tf_op jit(solution)/shard_map/ppermute | solution.py:18
  18.6 4.5 %all-to-all-start = ((bf16[8,4,16,2304]{3,2,1,0:T(8,128)(2,1)}), bf16[8,4,16,2304]{3,2,1,0:T(8,128)(2,1)}, u32[]{:S(2)}, u32[]{:S(2)}) async-start(bf16[8,4,16,2304]{3,2,1,0:T(8,128)(2,1)} %broadcast_in_dim.76), calls=%async_computation | async-start | bytes 4718592 | tf_op jit(solution)/shard_map/all_to_all | solution.py:13
  25.1 14.9 %gather_fusion.2 = bf16[4096,128]{1,0:T(8,128)(2,1)} fusion(bf16[128,8000]{0,1:T(8,128)(2,1)S(1)} %copy-done.2, s32[4096]{0:T(1024)S(1)} %bitcast_clamp_fusion), kind=kCustom, calls=%fused_computation.2 | custom fusion | bytes 2113536 | tf_op jit(solution)/shard_map/jit(_take)/gather | solution.py:127
  44.4 8.1 %all-to-all-done = bf16[8,4,16,2304]{3,2,1,0:T(8,128)(2,1)} async-done(((bf16[8,4,16,2304]{3,2,1,0:T(8,128)(2,1)}), bf16[8,4,16,2304]{3,2,1,0:T(8,128)(2,1)}, u32[]{:S(2)}, u32[]{:S(2)}) %all-to-all-start) | async-done | bytes 2359328 | tf_op jit(solution)/shard_map/all_to_all | solution.py:13
  52.5 3.6 %all-to-all-start.1 = ((bf16[8,5,128,128]{2,3,1,0:T(8,128)(2,1)}), bf16[8,5,128,128]{2,3,1,0:T(8,128)(2,1)S(1)}, u32[]{:S(2)}, u32[]{:S(2)}) async-start(bf16[8,5,128,128]{2,3,1,0:T(8,128)(2,1)} %pad_maximum_fusion.1), calls=%async_computation.1 | async-start | bytes 2621440 | tf_op jit(solution)/shard_map/all_to_all | solution.py:132
  61.8 2.7 %collective-permute-done.4 = bf16[576,512]{1,0:T(8,128)(2,1)} collective-permute-done((bf16[576,512]{1,0:T(8,128)(2,1)}, bf16[576,512]{1,0:T(8,128)(2,1)}, u32[]{:S(2)}, u32[]{:S(2)}) %collective-permute-start.4) | collective-permute-done | bytes 589856 | tf_op jit(solution)/shard_map/ppermute | solution.py:18
  64.5 2.0 %fusion.59 = (f32[512]{0:T(512)S(1)}, f32[512,512]{1,0:T(8,128)S(1)}) fusion(f32[512,512]{1,0:T(8,128)S(1)} %fusion.9, f32[512,512]{1,0:T(8,128)S(1)} %convolution_add_fusion.2, bf16[576,512]{1,0:T(8,128)(2,1)} %collective-permute-done.4, bf16[512,2304]{1,0:T(8,128)(2,1)} %bitcast.5, s32[]{:T(128)S(6)} %select_n.211, pred[512]{0:T(512)(128)(4,1)S(1)} %fusion.49), kind=kOutput, calls=%fused_computation.146 | convolution fusion | flops 303037952 | bytes 4393476 | tf_op jit(solution)/shard_map/dot_general | solution.py:153
  67.8 6.5 %all-to-all-done.1 = bf16[8,5,128,128]{2,3,1,0:T(8,128)(2,1)S(1)} async-done(((bf16[8,5,128,128]{2,3,1,0:T(8,128)(2,1)}), bf16[8,5,128,128]{2,3,1,0:T(8,128)(2,1)S(1)}, u32[]{:S(2)}, u32[]{:S(2)}) %all-to-all-start.1) | async-done | bytes 1310752 | tf_op jit(solution)/shard_map/all_to_all | solution.py:132
  76.4 2.4 %collective-permute-start.7 = (bf16[4,128,128]{2,1,0:T(8,128)(2,1)S(1)}, bf16[4,128,128]{2,1,0:T(8,128)(2,1)S(1)}, u32[]{:S(2)}, u32[]{:S(2)}) collective-permute-start(bf16[4,128,128]{2,1,0:T(8,128)(2,1)S(1)} %get-tuple-element.42), channel_id=1, source_target_pairs={{0,16},{8,24},{16,0},{24,8},{1,17},{9,25},{17,1},{25,9},{2,18},{10... | collective-permute-start | bytes 393224 | tf_op jit(solution)/shard_map/ppermute | solution.py:18
  78.8 2.8 %collective-permute-start.8 = (bf16[4,128,128]{2,1,0:T(8,128)(2,1)S(1)}, bf16[4,128,128]{2,1,0:T(8,128)(2,1)S(1)}, u32[]{:S(2)}, u32[]{:S(2)}) collective-permute-start(bf16[4,128,128]{2,1,0:T(8,128)(2,1)S(1)} %get-tuple-element.41), channel_id=1, source_target_pairs={{0,24},{8,0},{16,8},{24,16},{1,25},{9,1},{17,9},{25,17},{2,26},{10... | collective-permute-start | bytes 393224 | tf_op jit(solution)/shard_map/ppermute | solution.py:18
  83.4 3.1 %collective-permute-done.7 = bf16[4,128,128]{2,1,0:T(8,128)(2,1)S(1)} collective-permute-done((bf16[4,128,128]{2,1,0:T(8,128)(2,1)S(1)}, bf16[4,128,128]{2,1,0:T(8,128)(2,1)S(1)}, u32[]{:S(2)}, u32[]{:S(2)}) %collective-permute-start.7) | collective-permute-done | bytes 131104 | tf_op jit(solution)/shard_map/ppermute | solution.py:18
  87.2 7.7 %all-to-all-start.2 = ((f32[32,9,128]{2,1,0:T(8,128)}), f32[32,9,128]{2,1,0:T(8,128)}, u32[]{:S(2)}, u32[]{:S(2)}) async-start(f32[32,9,128]{2,1,0:T(8,128)} %broadcast_in_dim.129), calls=%async_computation.2 | async-start | bytes 524288 | tf_op jit(solution)/shard_map/all_to_all | solution.py:13
  94.9 3.1 %pad_maximum_fusion = bf16[4,576,512]{2,1,0:T(8,128)(2,1)} fusion(bf16[1,576,512]{2,1,0:T(8,128)(2,1)} %bitcast.43, bf16[1,576,512]{2,1,0:T(8,128)(2,1)} %bitcast.42, bf16[1,576,512]{2,1,0:T(8,128)(2,1)} %bitcast.41, bf16[1,576,512]{2,1,0:T(8,128)(2,1)S(1)} %bitcast.119), kind=kLoop, calls=%fused_computation.11 | loop fusion | flops 3538944 | bytes 4718592 | tf_op jit(solution)/shard_map/stack | solution.py:61
  98.9 2.4 %gather_fusion.8 = bf16[4,576,512]{2,1,0:T(8,128)(2,1)S(1)} fusion(bf16[4,576,512]{2,1,0:T(8,128)(2,1)} %pad_maximum_fusion, s32[1024]{0:T(1024)S(1)} %pad_clamp_fusion.3), kind=kCustom, calls=%fused_computation.8 | custom fusion | bytes 4718608 | tf_op jit(solution)/shard_map/jit(_take)/gather | solution.py:61
  108.4 2.7 %fusion.7 = bf16[512,512]{1,0:T(8,128)(2,1)} fusion(f32[64,8,4,128]{3,2,1,0:T(4,128)} %bitcast.121, f32[512,512]{1,0:T(8,128)} %copy-done.4, f32[512]{0:T(512)S(1)} %fusion.47, f32[512]{0:T(512)S(1)} %get-tuple-element.50, pred[512]{0:T(512)(128)(4,1)S(1)} %fusion.49), kind=kLoop, calls=%fused_computation.27 | loop fusion | flops 1572864 | bytes 2626048 | tf_op jit(solution)/shard_map/convert_element_type | solution.py:176
  112.1 2.2 %fusion.60 = f32[4,4,16,2304]{3,2,1,0:T(8,128)} fusion(bf16[4,4,16,512]{3,2,1,0:T(8,128)(2,1)S(1)} %bitcast.126, bf16[2304,512,1,1]{1,0,3,2:T(8,128)(2,1)S(1)} %bitcast.117), kind=kOutput, calls=%fused_computation.147 | convolution fusion | flops 603979776 | bytes 4980736 | tf_op jit(solution)/shard_map/dot_general | solution.py:185
  114.3 4.9 %collective-permute-done.13 = f32[4,4,16,2304]{3,2,1,0:T(8,128)} collective-permute-done((f32[4,4,16,2304]{3,2,1,0:T(8,128)}, f32[4,4,16,2304]{3,2,1,0:T(8,128)}, u32[]{:S(2)}, u32[]{:S(2)}) %collective-permute-start.13) | collective-permute-done | bytes 2359328 | tf_op jit(solution)/shard_map/ppermute | solution.py:48
  119.2 2.5 %convolution_add_fusion = f32[4,4,16,2304]{3,2,1,0:T(8,128)S(1)} fusion(f32[4,4,16,2304]{3,2,1,0:T(8,128)} %collective-permute-done.13, bf16[4,4,16,512]{3,2,1,0:T(8,128)(2,1)S(1)} %bitcast.125, bf16[2304,512,1,1]{1,0,3,2:T(8,128)(2,1)S(1)} %bitcast.118), kind=kOutput, calls=%fused_computation.9 | convolution fusion | flops 604569600 | bytes 7340032 | tf_op jit(solution)/shard_map/dot_general | solution.py:185
  127.5 1.9 %collective-permute-start.11 = (bf16[512,512]{1,0:T(8,128)(2,1)}, bf16[512,512]{1,0:T(8,128)(2,1)}, u32[]{:S(2)}, u32[]{:S(2)}) collective-permute-start(bf16[512,512]{1,0:T(8,128)(2,1)} %fusion.7), channel_id=1, source_target_pairs={{0,16},{8,24},{16,0},{24,8},{1,17},{9,25},{17,1},{25,9},{2,18},{10... | collective-permute-start | bytes 1572872 | tf_op jit(solution)/shard_map/ppermute | solution.py:18
  129.5 4.2 %collective-permute-start.10 = (bf16[512,512]{1,0:T(8,128)(2,1)}, bf16[512,512]{1,0:T(8,128)(2,1)}, u32[]{:S(2)}, u32[]{:S(2)}) collective-permute-start(bf16[512,512]{1,0:T(8,128)(2,1)} %fusion.7), channel_id=1, source_target_pairs={{0,8},{8,16},{16,24},{1,9},{9,17},{17,25},{2,10},{10,18},{18,26},{... | collective-permute-start | bytes 1572872 | tf_op jit(solution)/shard_map/ppermute | solution.py:32
  133.6 19.5 %collective-permute-done.11 = bf16[512,512]{1,0:T(8,128)(2,1)} collective-permute-done((bf16[512,512]{1,0:T(8,128)(2,1)}, bf16[512,512]{1,0:T(8,128)(2,1)}, u32[]{:S(2)}, u32[]{:S(2)}) %collective-permute-start.11) | collective-permute-done | bytes 524320 | tf_op jit(solution)/shard_map/ppermute | solution.py:18
  155.8 2.0 %fusion.16 = f32[4,16,2304]{2,1,0:T(8,128)} fusion(f32[4,16,2304]{2,1,0:T(8,128)S(1)} %collective-permute-done.16, f32[4,16,2304]{2,1,0:T(8,128)S(1)} %collective-permute-done.15, f32[4,16,2304]{2,1,0:T(8,128)S(1)} %collective-permute-done.14, f32[4,4,16,2304]{3,2,1,0:T(8,128)} %copy-done.3, s32[]{:T(128)S(6)} %select_n.238), kind=kLoop, calls=%fused_computation.42 | loop fusion | flops 442368 | bytes 2949124 | tf_op jit(solution)/shard_map/add | solution.py:54
  157.8 6.9 %all-to-all-start.3 = ((f32[4,16,2304]{2,1,0:T(8,128)}), f32[4,16,2304]{2,1,0:T(8,128)S(1)}, u32[]{:S(2)}, u32[]{:S(2)}) async-start(f32[4,16,2304]{2,1,0:T(8,128)} %fusion.16), calls=%async_computation.3 | async-start | bytes 1179648 | tf_op jit(solution)/shard_map/all_to_all | solution.py:192
  165.0 2.2 %fusion.5 = bf16[576,2048]{1,0:T(8,128)(2,1)S(1)} fusion(bf16[576,2048]{1,0:T(8,128)(2,1)S(1)} %broadcast_in_dim.75, s32[]{:T(128)S(6)} %select_n.223, bf16[512,512]{1,0:T(8,128)(2,1)} %fusion.7, bf16[512,2304]{1,0:T(8,128)(2,1)} %bitcast.5, s32[]{:T(128)S(6)} %select_n.203), kind=kOutput, calls=%fused_computation.23 | convolution fusion | flops 302284800 | bytes 1769480 | tf_op jit(solution)/shard_map/dot_general | solution.py:198
  167.2 5.8 %collective-permute-done.9 = bf16[512,512]{1,0:T(8,128)(2,1)} collective-permute-done((bf16[512,512]{1,0:T(8,128)(2,1)}, bf16[512,512]{1,0:T(8,128)(2,1)}, u32[]{:S(2)}, u32[]{:S(2)}) %collective-permute-start.9) | collective-permute-done | bytes 524320 | tf_op jit(solution)/shard_map/ppermute | solution.py:33
  173.0 2.2 %fusion.4 = bf16[576,2048]{1,0:T(8,128)(2,1)S(1)} fusion(bf16[576,2048]{1,0:T(8,128)(2,1)S(1)} %fusion.5, s32[]{:T(128)S(6)} %select_n.227, bf16[512,512]{1,0:T(8,128)(2,1)} %collective-permute-done.9, bf16[512,512]{1,0:T(8,128)(2,1)} %collective-permute-done.10, pred[]{:T(512)S(6)} %eq.112, bf16[512,2304]{1,0:T(8,128)(2,1)} %bitcast.5, s32[]{:T(128)S(6)} %select_n.203), kind=kOutput, calls=%fused_computation.21 | convolution fusion | flops 302546944 | bytes 2293769 | tf_op jit(solution)/shard_map/dot_general | solution.py:198
  175.2 2.2 %fusion.3 = bf16[576,2048]{1,0:T(8,128)(2,1)S(1)} fusion(bf16[576,2048]{1,0:T(8,128)(2,1)S(1)} %fusion.4, s32[]{:T(128)S(6)} %select_n.228, bf16[512,512]{1,0:T(8,128)(2,1)} %collective-permute-done.11, bf16[512,2304]{1,0:T(8,128)(2,1)} %bitcast.5, s32[]{:T(128)S(6)} %select_n.203), kind=kOutput, calls=%fused_computation.19 | convolution fusion | flops 302284800 | bytes 1769480 | tf_op jit(solution)/shard_map/dot_general | solution.py:198
  177.4 10.3 %collective-permute-done.12 = bf16[512,512]{1,0:T(8,128)(2,1)} collective-permute-done((bf16[512,512]{1,0:T(8,128)(2,1)}, bf16[512,512]{1,0:T(8,128)(2,1)}, u32[]{:S(2)}, u32[]{:S(2)}) %collective-permute-start.12) | collective-permute-done | bytes 524320 | tf_op jit(solution)/shard_map/ppermute | solution.py:34
  187.7 2.2 %fusion.2 = bf16[576,2048]{1,0:T(8,128)(2,1)S(1)} fusion(bf16[576,2048]{1,0:T(8,128)(2,1)S(1)} %fusion.3, s32[]{:T(128)S(6)} %select_n.233, bf16[512,512]{1,0:T(8,128)(2,1)} %collective-permute-done.12, bf16[512,512]{1,0:T(8,128)(2,1)} %collective-permute-done.9, pred[]{:T(512)S(6)} %or.3, bf16[512,2304]{1,0:T(8,128)(2,1)} %bitcast.5, s32[]{:T(128)S(6)} %select_n.203), kind=kOutput, calls=%fused_computation.17 | convolution fusion | flops 302546944 | bytes 2293769 | tf_op jit(solution)/shard_map/dot_general | solution.py:198
  (108 shorter events, 43.1 us)
Async XLA Ops:
  0.6 1.1 copy-start
  1.7 14.6 %collective-permute-start = (bf16[16,2304]{1,0:T(8,128)(2,1)S(1)}, bf16[16,2304]{1,0:T(8,128)(2,1)S(1)}, u32[]{:S(2)}, u32[]{:S(2)}) collective-permute-start(bf16[16,2304]{1,0:T(8,128)(2,1)S(1)} %constant_dynamic-slice_fusion.7), channel_id=1, source_target_pairs={{0,8},{8,16},{16,24},{24,0},{1,9},{9,17},{17,25},{25,1},{2,10},{10... | collective-permute-start | bytes 221192 | tf_op jit(solution)/shard_map/ppermute | solution.py:18
  4.8 11.6 %collective-permute-start.1 = (bf16[16,2304]{1,0:T(8,128)(2,1)S(1)}, bf16[16,2304]{1,0:T(8,128)(2,1)S(1)}, u32[]{:S(2)}, u32[]{:S(2)}) collective-permute-start(bf16[16,2304]{1,0:T(8,128)(2,1)S(1)} %constant_dynamic-slice_fusion.7), channel_id=1, source_target_pairs={{0,16},{8,24},{16,0},{24,8},{1,17},{9,25},{17,1},{25,9},{2,18},{10... | collective-permute-start | bytes 221192 | tf_op jit(solution)/shard_map/ppermute | solution.py:18
  7.3 9.0 %collective-permute-start.2 = (bf16[16,2304]{1,0:T(8,128)(2,1)S(1)}, bf16[16,2304]{1,0:T(8,128)(2,1)S(1)}, u32[]{:S(2)}, u32[]{:S(2)}) collective-permute-start(bf16[16,2304]{1,0:T(8,128)(2,1)S(1)} %constant_dynamic-slice_fusion.7), channel_id=1, source_target_pairs={{0,24},{8,0},{16,8},{24,16},{1,25},{9,1},{17,9},{25,17},{2,26},{10... | collective-permute-start | bytes 221192 | tf_op jit(solution)/shard_map/ppermute | solution.py:18
  8.7 6.8 %copy-start.7 = (s32[128,128]{1,0:T(8,128)S(1)}, s32[128,128]{1,0:T(8,128)}, u32[]{:S(2)}) copy-start(s32[128,128]{1,0:T(8,128)} %param.9) | copy-start | bytes 196612
  8.7 7.0 %copy-start.8 = (s32[128]{0:T(128)S(1)}, s32[128]{0:T(128)}, u32[]{:S(2)}) copy-start(s32[128]{0:T(128)} %param.10) | copy-start | bytes 1540
  11.6 48.3 %collective-permute-start.3 = (bf16[576,512]{1,0:T(8,128)(2,1)}, bf16[576,512]{1,0:T(8,128)(2,1)}, u32[]{:S(2)}, u32[]{:S(2)}) collective-permute-start(bf16[576,512]{1,0:T(8,128)(2,1)} %get-tuple-element.36), channel_id=1, source_target_pairs={{0,8},{8,16},{16,24},{24,0},{1,9},{9,17},{17,25},{25,1},{2,10},{10... | collective-permute-start | bytes 1769480 | tf_op jit(solution)/shard_map/ppermute | solution.py:18
  12.3 45.6 %collective-permute-start.5 = (bf16[576,512]{1,0:T(8,128)(2,1)}, bf16[576,512]{1,0:T(8,128)(2,1)}, u32[]{:S(2)}, u32[]{:S(2)}) collective-permute-start(bf16[576,512]{1,0:T(8,128)(2,1)} %get-tuple-element.35), channel_id=1, source_target_pairs={{0,24},{8,0},{16,8},{24,16},{1,25},{9,1},{17,9},{25,17},{2,26},{10... | collective-permute-start | bytes 1769480 | tf_op jit(solution)/shard_map/ppermute | solution.py:18
  16.3 48.2 %collective-permute-start.4 = (bf16[576,512]{1,0:T(8,128)(2,1)}, bf16[576,512]{1,0:T(8,128)(2,1)}, u32[]{:S(2)}, u32[]{:S(2)}) collective-permute-start(bf16[576,512]{1,0:T(8,128)(2,1)} %get-tuple-element.38), channel_id=1, source_target_pairs={{0,16},{8,24},{16,0},{24,8},{1,17},{9,25},{17,1},{25,9},{2,18},{10... | collective-permute-start | bytes 1769480 | tf_op jit(solution)/shard_map/ppermute | solution.py:18
  18.6 6.5 %copy-start.2 = (bf16[128,8000]{0,1:T(8,128)(2,1)S(1)}, bf16[128,8000]{0,1:T(8,128)(2,1)}, u32[]{:S(2)}) copy-start(bf16[128,8000]{0,1:T(8,128)(2,1)} %param.6) | copy-start | bytes 6144004
  18.6 33.9 %all-to-all-start = ((bf16[8,4,16,2304]{3,2,1,0:T(8,128)(2,1)}), bf16[8,4,16,2304]{3,2,1,0:T(8,128)(2,1)}, u32[]{:S(2)}, u32[]{:S(2)}) async-start(bf16[8,4,16,2304]{3,2,1,0:T(8,128)(2,1)} %broadcast_in_dim.76), calls=%async_computation | async-start | bytes 4718592 | tf_op jit(solution)/shard_map/all_to_all | solution.py:13
  40.0 1.1 copy-start.1
  41.8 1.2 copy-start.5
  52.5 21.7 %all-to-all-start.1 = ((bf16[8,5,128,128]{2,3,1,0:T(8,128)(2,1)}), bf16[8,5,128,128]{2,3,1,0:T(8,128)(2,1)S(1)}, u32[]{:S(2)}, u32[]{:S(2)}) async-start(bf16[8,5,128,128]{2,3,1,0:T(8,128)(2,1)} %pad_maximum_fusion.1), calls=%async_computation.1 | async-start | bytes 2621440 | tf_op jit(solution)/shard_map/all_to_all | solution.py:132
  66.5 1.0 copy-start.4
  75.8 7.6 %collective-permute-start.6 = (bf16[4,128,128]{2,1,0:T(8,128)(2,1)S(1)}, bf16[4,128,128]{2,1,0:T(8,128)(2,1)S(1)}, u32[]{:S(2)}, u32[]{:S(2)}) collective-permute-start(bf16[4,128,128]{2,1,0:T(8,128)(2,1)S(1)} %get-tuple-element.43), channel_id=1, source_target_pairs={{0,8},{8,16},{16,24},{24,0},{1,9},{9,17},{17,25},{25,1},{2,10},{10... | collective-permute-start | bytes 393224 | tf_op jit(solution)/shard_map/ppermute | solution.py:18
  76.4 10.1 %collective-permute-start.7 = (bf16[4,128,128]{2,1,0:T(8,128)(2,1)S(1)}, bf16[4,128,128]{2,1,0:T(8,128)(2,1)S(1)}, u32[]{:S(2)}, u32[]{:S(2)}) collective-permute-start(bf16[4,128,128]{2,1,0:T(8,128)(2,1)S(1)} %get-tuple-element.42), channel_id=1, source_target_pairs={{0,16},{8,24},{16,0},{24,8},{1,17},{9,25},{17,1},{25,9},{2,18},{10... | collective-permute-start | bytes 393224 | tf_op jit(solution)/shard_map/ppermute | solution.py:18
  78.8 7.7 %collective-permute-start.8 = (bf16[4,128,128]{2,1,0:T(8,128)(2,1)S(1)}, bf16[4,128,128]{2,1,0:T(8,128)(2,1)S(1)}, u32[]{:S(2)}, u32[]{:S(2)}) collective-permute-start(bf16[4,128,128]{2,1,0:T(8,128)(2,1)S(1)} %get-tuple-element.41), channel_id=1, source_target_pairs={{0,24},{8,0},{16,8},{24,16},{1,25},{9,1},{17,9},{25,17},{2,26},{10... | collective-permute-start | bytes 393224 | tf_op jit(solution)/shard_map/ppermute | solution.py:18
  87.2 18.0 %all-to-all-start.2 = ((f32[32,9,128]{2,1,0:T(8,128)}), f32[32,9,128]{2,1,0:T(8,128)}, u32[]{:S(2)}, u32[]{:S(2)}) async-start(f32[32,9,128]{2,1,0:T(8,128)} %broadcast_in_dim.129), calls=%async_computation.2 | async-start | bytes 524288 | tf_op jit(solution)/shard_map/all_to_all | solution.py:13
  114.3 4.9 %collective-permute-start.13 = (f32[4,4,16,2304]{3,2,1,0:T(8,128)}, f32[4,4,16,2304]{3,2,1,0:T(8,128)}, u32[]{:S(2)}, u32[]{:S(2)}) collective-permute-start(f32[4,4,16,2304]{3,2,1,0:T(8,128)} %fusion.60), channel_id=1, source_target_pairs={{0,1},{1,0},{2,3},{3,2},{4,5},{5,4},{6,7},{7,6},{8,9},{9,8},{10,11... | collective-permute-start | bytes 7077896 | tf_op jit(solution)/shard_map/ppermute | solution.py:48
  121.7 1.4 copy-start.3
  124.1 30.4 %collective-permute-start.14 = (f32[4,16,2304]{2,1,0:T(8,128)}, f32[4,16,2304]{2,1,0:T(8,128)S(1)}, u32[]{:S(2)}, u32[]{:S(2)}) collective-permute-start(f32[4,16,2304]{2,1,0:T(8,128)} %get-tuple-element.32), channel_id=1, source_target_pairs={{0,2},{1,3},{2,0},{3,1},{4,6},{5,7},{6,4},{7,5},{8,10},{9,11},{10,... | collective-permute-start | bytes 1769480 | tf_op jit(solution)/shard_map/ppermute | solution.py:53
  125.0 30.7 %collective-permute-start.15 = (f32[4,16,2304]{2,1,0:T(8,128)S(1)}, f32[4,16,2304]{2,1,0:T(8,128)S(1)}, u32[]{:S(2)}, u32[]{:S(2)}) collective-permute-start(f32[4,16,2304]{2,1,0:T(8,128)S(1)} %get-tuple-element.34), channel_id=1, source_target_pairs={{0,4},{1,5},{2,6},{3,7},{4,0},{5,1},{6,2},{7,3},{8,12},{9,13},{10,... | collective-permute-start | bytes 1769480 | tf_op jit(solution)/shard_map/ppermute | solution.py:53
  126.5 29.3 %collective-permute-start.16 = (f32[4,16,2304]{2,1,0:T(8,128)S(1)}, f32[4,16,2304]{2,1,0:T(8,128)S(1)}, u32[]{:S(2)}, u32[]{:S(2)}) collective-permute-start(f32[4,16,2304]{2,1,0:T(8,128)S(1)} %get-tuple-element.33), channel_id=1, source_target_pairs={{0,6},{1,7},{2,4},{3,5},{4,2},{5,3},{6,0},{7,1},{8,14},{9,15},{10,... | collective-permute-start | bytes 1769480 | tf_op jit(solution)/shard_map/ppermute | solution.py:53
  127.5 25.6 %collective-permute-start.11 = (bf16[512,512]{1,0:T(8,128)(2,1)}, bf16[512,512]{1,0:T(8,128)(2,1)}, u32[]{:S(2)}, u32[]{:S(2)}) collective-permute-start(bf16[512,512]{1,0:T(8,128)(2,1)} %fusion.7), channel_id=1, source_target_pairs={{0,16},{8,24},{16,0},{24,8},{1,17},{9,25},{17,1},{25,9},{2,18},{10... | collective-permute-start | bytes 1572872 | tf_op jit(solution)/shard_map/ppermute | solution.py:18
  129.5 37.7 %collective-permute-start.10 = (bf16[512,512]{1,0:T(8,128)(2,1)}, bf16[512,512]{1,0:T(8,128)(2,1)}, u32[]{:S(2)}, u32[]{:S(2)}) collective-permute-start(bf16[512,512]{1,0:T(8,128)(2,1)} %fusion.7), channel_id=1, source_target_pairs={{0,8},{8,16},{16,24},{1,9},{9,17},{17,25},{2,10},{10,18},{18,26},{... | collective-permute-start | bytes 1572872 | tf_op jit(solution)/shard_map/ppermute | solution.py:32
  153.1 19.8 %collective-permute-start.9 = (bf16[512,512]{1,0:T(8,128)(2,1)}, bf16[512,512]{1,0:T(8,128)(2,1)}, u32[]{:S(2)}, u32[]{:S(2)}) collective-permute-start(bf16[512,512]{1,0:T(8,128)(2,1)} %fusion.7), channel_id=1, source_target_pairs={{8,0},{16,8},{24,16},{9,1},{17,9},{25,17},{10,2},{18,10},{26,18},{... | collective-permute-start | bytes 1572872 | tf_op jit(solution)/shard_map/ppermute | solution.py:33
  154.4 33.2 %collective-permute-start.12 = (bf16[512,512]{1,0:T(8,128)(2,1)}, bf16[512,512]{1,0:T(8,128)(2,1)}, u32[]{:S(2)}, u32[]{:S(2)}) collective-permute-start(bf16[512,512]{1,0:T(8,128)(2,1)} %collective-permute-done.11), channel_id=1, source_target_pairs={{8,0},{16,24},{9,1},{17,25},{10,2},{18,26},{11,3},{19,27},{12,4},{... | collective-permute-start | bytes 1572872 | tf_op jit(solution)/shard_map/ppermute | solution.py:34
  157.8 32.1 %all-to-all-start.3 = ((f32[4,16,2304]{2,1,0:T(8,128)}), f32[4,16,2304]{2,1,0:T(8,128)S(1)}, u32[]{:S(2)}, u32[]{:S(2)}) async-start(f32[4,16,2304]{2,1,0:T(8,128)} %fusion.16), calls=%async_computation.3 | async-start | bytes 1179648 | tf_op jit(solution)/shard_map/all_to_all | solution.py:192
  189.9 1.4 copy-start.6

commit v3 on v2

--- a/solution.py
+++ b/solution.py
@@ -1,6 +1,10 @@
+import functools
+
 import jax
 import jax.numpy as jnp
 from jax import lax
+from jax.experimental import pallas as pl
+from jax.experimental.pallas import tpu as pltpu
 from jax.sharding import PartitionSpec as P
 
 
@@ -21,6 +25,19 @@
 def above(axis, distance):
     size = lax.axis_size(axis)
     return lax.rem(lax.axis_index(axis) + size + distance, size)
+
+
+def chip_gather(value, axis):
+    size = lax.axis_size(axis)
+    index = lax.axis_index(axis)
+    like = [value]
+    for step in range(1, size // 2):
+        like.append(lax.ppermute(value, axis, [(i, i ^ (2 * step)) for i in range(size)]))
+    like = jnp.stack(like)
+    other = lax.ppermute(like, axis, [(i, i ^ 1) for i in range(size)])
+    both = jnp.stack([like, other], axis=1).reshape((size,) + value.shape)
+    order = jnp.bitwise_xor(jnp.arange(size, dtype=jnp.int32), index)
+    return jnp.take(both, order, axis=0, mode="clip")
 
 
 def spread(value, axis):
@@ -61,6 +78,111 @@
     return jnp.take(jnp.stack(pieces), order, axis=0, mode="clip")
 
 
+def pick_kernel(capacity, ids_ref, count_ref, logits_ref, out_ref, wide_ref, rows_ref):
+    vocab_rows, tok_rows = logits_ref.shape
+    lanes = out_ref.shape[2]
+    step = next(s for s in (400, 320, 160, 80, 16) if vocab_rows % s == 0)
+
+    def widen(i, peak):
+        rows = pl.ds(pl.multiple_of(i * step, step), step)
+        part = logits_ref[rows, :].astype(jnp.float32)
+        wide_ref[rows, :] = part
+        return jnp.maximum(peak, jnp.max(part, axis=0, keepdims=True))
+
+    peak = lax.fori_loop(0, vocab_rows // step, widen, jnp.full((1, tok_rows), -jnp.inf, jnp.float32))
+
+    def add(i, total):
+        rows = pl.ds(pl.multiple_of(i * step, step), step)
+        return total + jnp.sum(jnp.exp(wide_ref[rows, :] - peak), axis=0, keepdims=True)
+
+    total = lax.fori_loop(0, vocab_rows // step, add, jnp.zeros((1, tok_rows), jnp.float32))
+    rows_ref[...] = jnp.zeros_like(rows_ref)
+    first = total.astype(jnp.bfloat16).astype(jnp.float32)
+    second = (total - first).astype(jnp.bfloat16).astype(jnp.float32)
+    rows_ref[0:1, :] = peak
+    rows_ref[1:2, :] = first
+    rows_ref[2:3, :] = second
+    rows_ref[3:4, :] = total - first - second
+    terms = rows_ref[...].astype(out_ref.dtype)
+    for shard in range(out_ref.shape[0]):
+        out_ref[shard, capacity] = terms
+
+    def slot(s, _):
+        def eight(g, _):
+            for j in range(8):
+                row = ids_ref[s * lanes + g * 8 + j]
+                rows_ref[pl.ds(g * 8 + j, 1), :] = wide_ref[pl.ds(row, 1), :]
+            return 0
+
+        @pl.when(count_ref[s] > 0)
+        def _():
+            lax.fori_loop(0, (count_ref[s] + 7) // 8, eight, 0)
+            out_ref[s // capacity, s % capacity] = rows_ref[...].astype(out_ref.dtype)
+
+        return 0
+
+    lax.fori_loop(0, out_ref.shape[0] * capacity, slot, 0)
+
+
+def pick(teacher_logits, ids, counts, shards, capacity):
+    tok_rows, vocab_rows = teacher_logits.shape
+    lanes = ids.shape[1]
+    return pl.pallas_call(
+        functools.partial(pick_kernel, capacity),
+        out_shape=jax.ShapeDtypeStruct(
+            (shards, capacity + 1, lanes, tok_rows), teacher_logits.dtype
+        ),
+        in_specs=[
+            pl.BlockSpec(memory_space=pltpu.SMEM),
+            pl.BlockSpec(memory_space=pltpu.SMEM),
+            pl.BlockSpec(memory_space=pltpu.VMEM),
+        ],
+        out_specs=pl.BlockSpec(memory_space=pltpu.VMEM),
+        scratch_shapes=[
+            pltpu.VMEM((vocab_rows, tok_rows), jnp.float32),
+            pltpu.VMEM((lanes, tok_rows), jnp.float32),
+        ],
+    )(ids.reshape(-1), counts, teacher_logits.T)
+
+
+def kept_kernel(capacity, anchor_ref, count_ref, arrived_ref, kept_ref, mass_ref):
+    shards = arrived_ref.shape[0] // (capacity + 1)
+    tops, sums = [], []
+    for shard in range(shards):
+        terms = arrived_ref[shard * (capacity + 1) + capacity, 0:16, :].astype(jnp.float32)
+        tops.append(terms[0:1])
+        sums.append(terms[1:2] + terms[2:3] + terms[3:4])
+    peak = functools.reduce(jnp.maximum, tops)
+    total = sum(part * jnp.exp(top - peak) for top, part in zip(tops, sums))
+    lane = lax.broadcasted_iota(jnp.int32, kept_ref.shape[1:], 0)
+
+    def block(b, mass):
+        logits = arrived_ref[anchor_ref[b]].astype(jnp.float32)
+        probs = jnp.where(lane < count_ref[b], jnp.exp(logits - peak) / total, 0.0)
+        kept = probs.astype(kept_ref.dtype)
+        kept_ref[b] = kept
+        return mass + jnp.sum(kept.astype(jnp.float32), axis=0, keepdims=True)
+
+    mass_ref[...] = lax.fori_loop(0, kept_ref.shape[0], block, jnp.zeros(mass_ref.shape, jnp.float32))
+
+
+def kept_probabilities(arrived, anchor, counts, capacity):
+    lanes, tok_rows = arrived.shape[2:]
+    return pl.pallas_call(
+        functools.partial(kept_kernel, capacity),
+        out_shape=(
+            jax.ShapeDtypeStruct((anchor.shape[0], lanes, tok_rows), arrived.dtype),
+            jax.ShapeDtypeStruct((1, tok_rows), jnp.float32),
+        ),
+        in_specs=[
+            pl.BlockSpec(memory_space=pltpu.SMEM),
+            pl.BlockSpec(memory_space=pltpu.SMEM),
+            pl.BlockSpec(memory_space=pltpu.VMEM),
+        ],
+        out_specs=[pl.BlockSpec(memory_space=pltpu.VMEM)] * 2,
+    )(anchor, counts, arrived.reshape(-1, lanes, tok_rows))
+
+
 def shards(teacher_logits, student_hidden, student_head, keep_ids, block_owner, block_count):
     planes = lax.axis_size("dp")
     plane = lax.axis_index("dp")
@@ -86,8 +208,7 @@
 
     hidden_slice = lax.dynamic_slice_in_dim(student_hidden, my_shard * slice_rows, slice_rows)
     hidden = [shift(hidden_slice, "dp", d) if d else hidden_slice for d in range(planes)]
-    hidden = in_order(hidden, "dp")
-    hidden = exchange(hidden, "vocab").reshape(tokens, width)
+    hidden = chip_gather(in_order(hidden, "dp"), "vocab").reshape(tokens, width)
 
     numbers = jnp.arange(block_owner.shape[0], dtype=jnp.int32)
     lane_index = jnp.arange(lane_count, dtype=jnp.int32)
@@ -106,43 +227,23 @@
         & (pair_rank[None, :] == (send_slots % capacity)[:, None])
     )
     chosen = jnp.sum(jnp.where(outgoing, numbers[None, :], 0), axis=1)
-    columns = jnp.clip(keep_ids[chosen] - my_shard * vocab_rows, 0, vocab_rows - 1).reshape(-1)
+    columns = jnp.clip(keep_ids[chosen] - my_shard * vocab_rows, 0, vocab_rows - 1)
+    slot_counts = jnp.sum(jnp.where(outgoing, block_count[None, :], 0), axis=1)
     incoming = (block_owner[None, :] == my_shard) & (
         ordinal[None, :] == jnp.arange(kept_blocks, dtype=jnp.int32)[:, None]
     )
     own_blocks = jnp.sum(jnp.where(incoming, numbers[None, :], 0), axis=1)
     anchor = source[own_blocks] * (capacity + 1) + pair_rank[own_blocks]
-    valid = lane_index[None, :] < block_count[own_blocks][:, None]
-
-    values = teacher_logits.astype(jnp.float32)
-    local_peak = jnp.max(values, axis=1)
-    local_total = jnp.sum(jnp.exp(values - local_peak[:, None]), axis=1)
-    terms = [local_peak]
-    for _ in range(3):
-        terms.append(lax.reduce_precision(local_total, 8, 7))
-        local_total = local_total - terms[-1]
-    terms = jnp.stack(terms, axis=1).astype(jnp.bfloat16)
-    terms = jnp.pad(terms, ((0, 0), (0, lane_count - terms.shape[1])))
-
-    picked = jnp.take(teacher_logits, columns, axis=1, mode="clip")
-    picked = picked.reshape(tok_rows, shard_count, capacity, lane_count).transpose(1, 2, 0, 3)
-    terms = jnp.broadcast_to(terms, (shard_count, 1, tok_rows, lane_count))
-    picked = jnp.concatenate([picked, terms], axis=1)
-    hidden, picked = lax.optimization_barrier((hidden, picked))
+    own_counts = block_count[own_blocks]
+    valid = lane_index[None, :] < own_counts[:, None]
+
+    picked = pick(teacher_logits, columns, slot_counts, shard_count, capacity)
     arrived = lax.all_to_all(picked, "vocab", split_axis=0, concat_axis=0, tiled=True)
-    stats = arrived[:, capacity, :, :4].astype(jnp.float32)
-    totals = stats[:, :, 1] + stats[:, :, 2] + stats[:, :, 3]
-    peak = jnp.max(stats[:, :, 0], axis=0)
-    total = jnp.sum(totals * jnp.exp(stats[:, :, 0] - peak), axis=0)
-
-    arrived = arrived.reshape(shard_count * (capacity + 1), tok_rows, lane_count)
-    target = jnp.take(arrived, anchor, axis=0, mode="clip").astype(jnp.float32)
-    target = jnp.where(
-        valid[:, None, :], jnp.exp(target - peak[None, :, None]) / total[None, :, None], 0.0
-    ).astype(jnp.bfloat16)
-    mass_part = jnp.sum(target.astype(jnp.float32), axis=(0, 2))
-
-    target = target.reshape(planes, part_blocks, tok_rows, lane_count)
+    arrived, hidden = lax.optimization_barrier((arrived, hidden))
+    target, mass_part = kept_probabilities(arrived, anchor, own_counts, capacity)
+    mass_part = mass_part.reshape(-1)
+
+    target = target.reshape(planes, part_blocks, lane_count, tok_rows)
     kept = []
     for distance in range(planes):
         piece = lax.dynamic_index_in_dim(target, above("dp", distance), 0, keepdims=False)
@@ -162,8 +263,9 @@
     student = jnp.concatenate([local_top, jnp.sum(weight, axis=1), mass_part])
     pieces, kept, student = lax.optimization_barrier((pieces, kept, student))
     kept = in_order(kept, "dp").reshape(
-        planes, part_blocks, shard_count, slice_rows, lane_count
-    ).transpose(2, 0, 3, 1, 4).reshape(tokens, part_cols).astype(jnp.float32)
+        planes, part_cols, tok_rows
+    ).transpose(0, 2, 1).reshape(planes, shard_count, slice_rows, part_cols)
+    kept = kept.transpose(1, 0, 2, 3).reshape(tokens, part_cols).astype(jnp.float32)
     student = exchange(student.reshape(-1, tok_rows), ("dp", "vocab")).reshape(
         planes * shard_count, 2 * planes + 1, tok_rows
     )
@@ -196,7 +298,8 @@
     head_grad = jnp.zeros((slab, own_cols), jnp.bfloat16)
     for origin, columns_part in gradients:
         block = lax.dot_general(
-            own_hidden, columns_part, (((0,), (0,)), ((), ())), preferred_element_type=jnp.float32
+            own_hidden, columns_part, (((0,), (0,)), ((), ())),
+            preferred_element_type=jnp.float32,
         ).astype(jnp.bfloat16)
         head_grad = lax.dynamic_update_slice_in_dim(head_grad, block, origin * part_cols, axis=1)
     return (head_grad, hidden_grad)

time: 192 us -> 206 us (1.073)
  the two profiles are of different devices: /device:TPU:0 before, /device:TPU:26 now
where the time goes in v3:
time: 206 us; the launch traced here: 205 us
  waiting for transfers between devices  71.6 us (35%)
  starting transfers between devices  47.3 us (23%)
  local copies, waits for them, and re-layouts  30.3 us (15%)
  other arithmetic  24.4 us (12%)
  matrix products  21.6 us (10%)
  Pallas kernels  8.64 us (4%)
    ppermute x10, waiting for transfers between devices, shift(): lax.ppermute(value, axis, [(p, (p + distance) % size) for p in range(size)])  53.8 us
    ppermute x10, starting transfers between devices, shift(): lax.ppermute(value, axis, [(p, (p + distance) % size) for p in range(size)])  12.5 us
    dot_general x4, matrix products, shards(): lax.dot_general(own_hidden, columns_part, (((0,), (0,)), ((), ())), prefe...  11.1 us
    ppermute x1, waiting for transfers between devices, spread(): relay = lax.ppermute(middle, axis, [(1, 0), (2, 3)])  10.8 us
    all_to_all x1, starting transfers between devices, shards(): lax.all_to_all(picked, 'vocab', split_axis=0, concat_axis=0, tiled=True)  8.69 us
    all_to_all x1, starting transfers between devices, shards(): sums = lax.all_to_all(sums, 'dp', split_axis=0, concat_axis=0, tiled=True)  7.25 us
    all_to_all x1, starting transfers between devices, exchange(): return lax.all_to_all(copies, axes, split_axis=0, concat_axis=0, tiled=True)  5.88 us
    dot_general x4, matrix products, shards(): jnp.dot(lax.dynamic_slice_in_dim(hidden, above('dp', -distance) * slab, s...  5.8 us
  transfers between devices with their start and end apart: 24, of which 9 were waited for; matrix products, arithmetic and copies ran while one was open for 28% of the time, Pallas kernels for 4%

profile of v3, /device:TPU:26, one launch (start us, length us, event | category | flops | bytes accessed | tf_op | source)
XLA Modules:
  0.0 204.9 jit_solution(13127899276897926911)
XLA Ops:
  15.4 5.0 %shard_map.77 = bf16[8,5,128,128]{3,2,1,0:T(8,128)(2,1)} custom-call(s32[4096]{0:T(1024)} %clamp_bitcast_fusion.ids_ref, s32[32]{0:T(128)} %get-tuple-element.30.count_ref, bf16[8000,128]{1,0:T(8,128)(2,1)} %bitcast.124), custom_call_target="tpu_custom_call" | custom-call | tf_op jit(solution)/shard_map/pallas_call | solution.py:130
  20.4 8.7 %all-to-all-start = ((bf16[8,5,128,128]{3,2,1,0:T(8,128)(2,1)}), bf16[8,5,128,128]{3,2,1,0:T(8,128)(2,1)}, u32[]{:S(2)}, u32[]{:S(2)}) async-start(bf16[8,5,128,128]{3,2,1,0:T(8,128)(2,1)} %shard_map.77), calls=%async_computation | async-start | bytes 2621440 | tf_op jit(solution)/shard_map/all_to_all | solution.py:241
  29.1 2.9 %constant_dynamic-slice_fusion.2 = (bf16[576,512]{1,0:T(8,128)(2,1)}, bf16[576,512]{1,0:T(8,128)(2,1)}, bf16[576,512]{1,0:T(8,128)(2,1)S(1)}, bf16[576,512]{1,0:T(8,128)(2,1)}) fusion(bf16[576,2048]{1,0:T(8,128)(2,1)} %param.8, s32[]{:T(128)S(6)} %select_n.211, s32[]{:T(128)S(6)} %select_n.207, s32[]{:T(128)S(6)} %select_n.205, s32[]{:T(128)S(6)} %select_n.209), kind=kLoop, calls=%fused_computation.85 | loop fusion | bytes 4718608 | tf_op jit(solution)/shard_map/dynamic_slice | solution.py:204
  32.0 2.5 %collective-permute-start.7 = (bf16[576,512]{1,0:T(8,128)(2,1)}, bf16[576,512]{1,0:T(8,128)(2,1)}, u32[]{:S(2)}, u32[]{:S(2)}) collective-permute-start(bf16[576,512]{1,0:T(8,128)(2,1)} %get-tuple-element.42), channel_id=1, source_target_pairs={{0,8},{8,16},{16,24},{24,0},{1,9},{9,17},{17,25},{25,1},{2,10},{10... | collective-permute-start | bytes 1769480 | tf_op jit(solution)/shard_map/ppermute | solution.py:22
  36.5 2.2 %fusion.46 = (bf16[4,1,4,16,2304]{4,3,2,1,0:T(8,128)(2,1)S(1)}, bf16[4,4,16,2304]{3,2,1,0:T(8,128)(2,1)}) fusion(bf16[1,4,16,2304]{3,2,1,0:T(8,128)(2,1)} %bitcast.132, bf16[1,4,16,2304]{3,2,1,0:T(8,128)(2,1)S(1)} %bitcast.131, bf16[1,4,16,2304]{3,2,1,0:T(8,128)(2,1)S(1)} %bitcast.130, bf16[1,4,16,2304]{3,2,1,0:T(8,128)(2,1)S(1)} %bitcast.125), kind=kLoop, calls=%fused_computation.122 | loop fusion | flops 1769472 | bytes 3538944 | tf_op jit(solution)/shard_map/stack | solution.py:38
  41.9 2.9 %pad_maximum_fusion = bf16[4,2,4,16,2304]{4,3,2,1,0:T(8,128)(2,1)} fusion(bf16[4,1,4,16,2304]{4,3,2,1,0:T(8,128)(2,1)} %bitcast.15, bf16[4,1,4,16,2304]{4,3,2,1,0:T(8,128)(2,1)S(1)} %get-tuple-element.45), kind=kLoop, calls=%fused_computation.9 | loop fusion | flops 1179648 | bytes 4718592 | tf_op jit(solution)/shard_map/stack | solution.py:38
  44.8 2.4 %gather_fusion.2 = bf16[8,4,16,2304]{3,2,1,0:T(8,128)(2,1)S(1)} fusion(bf16[8,4,16,2304]{3,2,1,0:T(8,128)(2,1)} %bitcast.121, s32[1024]{0:T(1024)S(1)} %pad_clamp_fusion.1), kind=kCustom, calls=%fused_computation.2 | custom fusion | bytes 4718624 | tf_op jit(solution)/shard_map/jit(_take)/gather | solution.py:40
  47.1 3.6 %shard_map.78 = (bf16[16,128,128]{2,1,0:T(8,128)(2,1)}, f32[1,128]{1,0:T(1,128)}) custom-call(s32[16]{0:T(128)} %multiply_add_fusion.anchor_ref, s32[16]{0:T(128)} %copy-done.11, bf16[40,128,128]{2,1,0:T(8,128)(2,1)} %bitcast.22.arrived_ref), custom_call_target="tpu_custom_call" | custom-call | tf_op jit(solution)/shard_map/pallas_call | solution.py:171
  52.6 2.6 %collective-permute-start.10 = (bf16[4,128,128]{2,1,0:T(8,128)(2,1)S(1)}, bf16[4,128,128]{2,1,0:T(8,128)(2,1)}, u32[]{:S(2)}, u32[]{:S(2)}) collective-permute-start(bf16[4,128,128]{2,1,0:T(8,128)(2,1)S(1)} %get-tuple-element.51), channel_id=1, source_target_pairs={{0,8},{8,16},{16,24},{24,0},{1,9},{9,17},{17,25},{25,1},{2,10},{10... | collective-permute-start | bytes 393224 | tf_op jit(solution)/shard_map/ppermute | solution.py:22
  55.2 2.0 collective-permute-start.11
  57.8 4.6 %collective-permute-done.9 = bf16[576,512]{1,0:T(8,128)(2,1)} collective-permute-done((bf16[576,512]{1,0:T(8,128)(2,1)}, bf16[576,512]{1,0:T(8,128)(2,1)}, u32[]{:S(2)}, u32[]{:S(2)}) %collective-permute-start.9) | collective-permute-done | bytes 589856 | tf_op jit(solution)/shard_map/ppermute | solution.py:22
  67.2 24.7 %collective-permute-done.8 = bf16[576,512]{1,0:T(8,128)(2,1)} collective-permute-done((bf16[576,512]{1,0:T(8,128)(2,1)}, bf16[576,512]{1,0:T(8,128)(2,1)}, u32[]{:S(2)}, u32[]{:S(2)}) %collective-permute-start.8) | collective-permute-done | bytes 589856 | tf_op jit(solution)/shard_map/ppermute | solution.py:22
  95.0 1.8 collective-permute-done.11
  98.2 5.9 %all-to-all-start.1 = ((f32[32,9,128]{2,1,0:T(8,128)}), f32[32,9,128]{2,1,0:T(8,128)}, u32[]{:S(2)}, u32[]{:S(2)}) async-start(f32[32,9,128]{2,1,0:T(8,128)} %broadcast_in_dim.99), calls=%async_computation.1 | async-start | bytes 524288 | tf_op jit(solution)/shard_map/all_to_all | solution.py:17
  104.1 3.2 %pad_maximum_fusion.1 = bf16[4,576,512]{2,1,0:T(8,128)(2,1)} fusion(bf16[1,576,512]{2,1,0:T(8,128)(2,1)} %bitcast.48, bf16[1,576,512]{2,1,0:T(8,128)(2,1)} %bitcast.47, bf16[1,576,512]{2,1,0:T(8,128)(2,1)} %bitcast.46, bf16[1,576,512]{2,1,0:T(8,128)(2,1)S(1)} %bitcast.122), kind=kLoop, calls=%fused_computation.10 | loop fusion | flops 3538944 | bytes 4718592 | tf_op jit(solution)/shard_map/stack | solution.py:78
  109.1 2.4 %gather_fusion.7 = bf16[4,576,512]{2,1,0:T(8,128)(2,1)S(1)} fusion(bf16[4,576,512]{2,1,0:T(8,128)(2,1)} %pad_maximum_fusion.1, s32[1024]{0:T(1024)S(1)} %pad_clamp_fusion.2), kind=kCustom, calls=%fused_computation.7 | custom fusion | bytes 4718608 | tf_op jit(solution)/shard_map/jit(_take)/gather | solution.py:78
  114.3 2.5 %copy.22 = f32[4,512,128]{1,2,0:T(8,128)} copy(f32[4,512,128]{2,1,0:T(8,128)} %bitcast_convert_fusion) | data formatting | bytes 2097152 | tf_op jit(solution)/shard_map/convert_element_type | solution.py:268
  116.8 2.3 %copy.23 = f32[8,4,16,512]{3,2,1,0:T(8,128)} copy(f32[8,4,16,512]{3,2,0,1:T(8,128)} %bitcast.123) | data formatting | bytes 2097152 | tf_op jit(solution)/shard_map/convert_element_type | solution.py:268
  122.2 2.7 %fusion.7 = bf16[512,512]{1,0:T(8,128)(2,1)} fusion(f32[8,4,16,512]{3,2,1,0:T(8,128)} %copy.23, f32[512,512]{1,0:T(8,128)} %copy-done.5, f32[512]{0:T(512)S(1)} %fusion.39, f32[512]{0:T(512)S(1)} %get-tuple-element.53, pred[512]{0:T(512)(128)(4,1)S(1)} %fusion.41), kind=kLoop, calls=%fused_computation.26 | loop fusion | flops 1572864 | bytes 2626048 | tf_op jit(solution)/shard_map/convert_element_type | solution.py:278
  125.9 2.2 %fusion.50 = f32[4,4,16,2304]{3,2,1,0:T(8,128)} fusion(bf16[4,4,16,512]{3,2,1,0:T(8,128)(2,1)S(1)} %bitcast.127, bf16[2304,512,1,1]{1,0,3,2:T(8,128)(2,1)S(1)} %bitcast.111), kind=kOutput, calls=%fused_computation.125 | convolution fusion | flops 603979776 | bytes 4980736 | tf_op jit(solution)/shard_map/dot_general | solution.py:287
  128.3 4.8 %collective-permute-done.17 = f32[4,4,16,2304]{3,2,1,0:T(8,128)} collective-permute-done((f32[4,4,16,2304]{3,2,1,0:T(8,128)}, f32[4,4,16,2304]{3,2,1,0:T(8,128)}, u32[]{:S(2)}, u32[]{:S(2)}) %collective-permute-start.17) | collective-permute-done | bytes 2359328 | tf_op jit(solution)/shard_map/ppermute | solution.py:65
  133.0 2.5 %convolution_add_fusion = f32[4,4,16,2304]{3,2,1,0:T(8,128)S(1)} fusion(f32[4,4,16,2304]{3,2,1,0:T(8,128)} %collective-permute-done.17, bf16[4,4,16,512]{3,2,1,0:T(8,128)(2,1)S(1)} %bitcast.126, bf16[2304,512,1,1]{1,0,3,2:T(8,128)(2,1)S(1)} %bitcast.112), kind=kOutput, calls=%fused_computation.8 | convolution fusion | flops 604569600 | bytes 7340032 | tf_op jit(solution)/shard_map/dot_general | solution.py:287
  141.9 3.2 %collective-permute-start.13 = (bf16[512,512]{1,0:T(8,128)(2,1)}, bf16[512,512]{1,0:T(8,128)(2,1)}, u32[]{:S(2)}, u32[]{:S(2)}) collective-permute-start(bf16[512,512]{1,0:T(8,128)(2,1)} %fusion.7), channel_id=1, source_target_pairs={{8,0},{16,8},{24,16},{9,1},{17,9},{25,17},{10,2},{18,10},{26,18},{... | collective-permute-start | bytes 1572872 | tf_op jit(solution)/shard_map/ppermute | solution.py:50
  145.1 21.8 %collective-permute-done.15 = bf16[512,512]{1,0:T(8,128)(2,1)} collective-permute-done((bf16[512,512]{1,0:T(8,128)(2,1)}, bf16[512,512]{1,0:T(8,128)(2,1)}, u32[]{:S(2)}, u32[]{:S(2)}) %collective-permute-start.15) | collective-permute-done | bytes 524320 | tf_op jit(solution)/shard_map/ppermute | solution.py:22
  169.6 2.0 fusion.16
  171.6 7.2 %all-to-all-start.2 = ((f32[4,16,2304]{2,1,0:T(8,128)}), f32[4,16,2304]{2,1,0:T(8,128)S(1)}, u32[]{:S(2)}, u32[]{:S(2)}) async-start(f32[4,16,2304]{2,1,0:T(8,128)} %fusion.16), calls=%async_computation.2 | async-start | bytes 1179648 | tf_op jit(solution)/shard_map/all_to_all | solution.py:294
  180.5 2.8 %fusion.5 = bf16[576,2048]{1,0:T(8,128)(2,1)} fusion(bf16[576,2048]{1,0:T(8,128)(2,1)} %broadcast_in_dim.59, s32[]{:T(128)S(6)} %select_n.218, bf16[512,512]{1,0:T(8,128)(2,1)} %fusion.7, bf16[512,2304]{1,0:T(8,128)(2,1)S(1)} %bitcast.117, s32[]{:T(128)S(6)} %select_n.200), kind=kOutput, calls=%fused_computation.22 | convolution fusion | flops 302284800 | bytes 1769480 | tf_op jit(solution)/shard_map/dot_general | solution.py:300
  183.3 1.9 collective-permute-done.14
  185.2 2.8 %fusion.4 = bf16[576,2048]{1,0:T(8,128)(2,1)} fusion(bf16[576,2048]{1,0:T(8,128)(2,1)} %fusion.5, s32[]{:T(128)S(6)} %select_n.222, bf16[512,512]{1,0:T(8,128)(2,1)} %collective-permute-done.13, bf16[512,512]{1,0:T(8,128)(2,1)} %collective-permute-done.14, pred[]{:T(512)S(6)} %eq.112, bf16[512,2304]{1,0:T(8,128)(2,1)S(1)} %bitcast.118, s32[]{:T(128)S(6)} %select_n.200), kind=kOutput, calls=%fused_computation.20 | convolution fusion | flops 302546944 | bytes 2293769 | tf_op jit(solution)/shard_map/dot_general | solution.py:300
  188.0 2.8 %fusion.3 = bf16[576,2048]{1,0:T(8,128)(2,1)} fusion(bf16[576,2048]{1,0:T(8,128)(2,1)} %fusion.4, s32[]{:T(128)S(6)} %select_n.223, bf16[512,512]{1,0:T(8,128)(2,1)} %collective-permute-done.15, bf16[512,2304]{1,0:T(8,128)(2,1)S(1)} %bitcast.119, s32[]{:T(128)S(6)} %select_n.200), kind=kOutput, calls=%fused_computation.18 | convolution fusion | flops 302284800 | bytes 1769480 | tf_op jit(solution)/shard_map/dot_general | solution.py:300
  190.7 10.8 %collective-permute-done.16 = bf16[512,512]{1,0:T(8,128)(2,1)} collective-permute-done((bf16[512,512]{1,0:T(8,128)(2,1)}, bf16[512,512]{1,0:T(8,128)(2,1)}, u32[]{:S(2)}, u32[]{:S(2)}) %collective-permute-start.16) | collective-permute-done | bytes 524320 | tf_op jit(solution)/shard_map/ppermute | solution.py:51
  201.5 2.8 %fusion.2 = bf16[576,2048]{1,0:T(8,128)(2,1)} fusion(bf16[576,2048]{1,0:T(8,128)(2,1)} %fusion.3, s32[]{:T(128)S(6)} %select_n.228, bf16[512,512]{1,0:T(8,128)(2,1)} %collective-permute-done.16, bf16[512,512]{1,0:T(8,128)(2,1)} %collective-permute-done.13, pred[]{:T(512)S(6)} %or.3, bf16[512,2304]{1,0:T(8,128)(2,1)S(1)} %bitcast.120, s32[]{:T(128)S(6)} %select_n.200), kind=kOutput, calls=%fused_computation.16 | convolution fusion | flops 302546944 | bytes 2293769 | tf_op jit(solution)/shard_map/dot_general | solution.py:300
  (111 shorter events, 51.5 us)
Async XLA Ops:
  1.7 8.1 %collective-permute-start = (bf16[16,2304]{1,0:T(8,128)(2,1)S(1)}, bf16[16,2304]{1,0:T(8,128)(2,1)S(1)}, u32[]{:S(2)}, u32[]{:S(2)}) collective-permute-start(bf16[16,2304]{1,0:T(8,128)(2,1)S(1)} %constant_dynamic-slice_fusion.6), channel_id=1, source_target_pairs={{0,8},{8,16},{16,24},{24,0},{1,9},{9,17},{17,25},{25,1},{2,10},{10... | collective-permute-start | bytes 221192 | tf_op jit(solution)/shard_map/ppermute | solution.py:22
  1.9 8.7 %collective-permute-start.1 = (bf16[16,2304]{1,0:T(8,128)(2,1)S(1)}, bf16[16,2304]{1,0:T(8,128)(2,1)S(1)}, u32[]{:S(2)}, u32[]{:S(2)}) collective-permute-start(bf16[16,2304]{1,0:T(8,128)(2,1)S(1)} %constant_dynamic-slice_fusion.6), channel_id=1, source_target_pairs={{0,16},{8,24},{16,0},{24,8},{1,17},{9,25},{17,1},{25,9},{2,18},{10... | collective-permute-start | bytes 221192 | tf_op jit(solution)/shard_map/ppermute | solution.py:22
  3.6 7.0 %collective-permute-start.2 = (bf16[16,2304]{1,0:T(8,128)(2,1)S(1)}, bf16[16,2304]{1,0:T(8,128)(2,1)S(1)}, u32[]{:S(2)}, u32[]{:S(2)}) collective-permute-start(bf16[16,2304]{1,0:T(8,128)(2,1)S(1)} %constant_dynamic-slice_fusion.6), channel_id=1, source_target_pairs={{0,24},{8,0},{16,8},{24,16},{1,25},{9,1},{17,9},{25,17},{2,26},{10... | collective-permute-start | bytes 221192 | tf_op jit(solution)/shard_map/ppermute | solution.py:22
  11.3 23.3 %collective-permute-start.3 = (bf16[4,16,2304]{2,1,0:T(8,128)(2,1)S(1)}, bf16[4,16,2304]{2,1,0:T(8,128)(2,1)S(1)}, u32[]{:S(2)}, u32[]{:S(2)}) collective-permute-start(bf16[4,16,2304]{2,1,0:T(8,128)(2,1)S(1)} %gather_fusion.1), channel_id=1, source_target_pairs={{0,2},{1,3},{2,0},{3,1},{4,6},{5,7},{6,4},{7,5},{8,10},{9,11},{10,... | collective-permute-start | bytes 884744 | tf_op jit(solution)/shard_map/ppermute | solution.py:35
  11.9 23.9 %collective-permute-start.4 = (bf16[4,16,2304]{2,1,0:T(8,128)(2,1)S(1)}, bf16[4,16,2304]{2,1,0:T(8,128)(2,1)S(1)}, u32[]{:S(2)}, u32[]{:S(2)}) collective-permute-start(bf16[4,16,2304]{2,1,0:T(8,128)(2,1)S(1)} %gather_fusion.1), channel_id=1, source_target_pairs={{0,4},{1,5},{2,6},{3,7},{4,0},{5,1},{6,2},{7,3},{8,12},{9,13},{10,... | collective-permute-start | bytes 884744 | tf_op jit(solution)/shard_map/ppermute | solution.py:35
  13.4 22.4 %collective-permute-start.5 = (bf16[4,16,2304]{2,1,0:T(8,128)(2,1)S(1)}, bf16[4,16,2304]{2,1,0:T(8,128)(2,1)S(1)}, u32[]{:S(2)}, u32[]{:S(2)}) collective-permute-start(bf16[4,16,2304]{2,1,0:T(8,128)(2,1)S(1)} %gather_fusion.1), channel_id=1, source_target_pairs={{0,6},{1,7},{2,4},{3,5},{4,2},{5,3},{6,0},{7,1},{8,14},{9,15},{10,... | collective-permute-start | bytes 884744 | tf_op jit(solution)/shard_map/ppermute | solution.py:35
  20.4 26.7 %all-to-all-start = ((bf16[8,5,128,128]{3,2,1,0:T(8,128)(2,1)}), bf16[8,5,128,128]{3,2,1,0:T(8,128)(2,1)}, u32[]{:S(2)}, u32[]{:S(2)}) async-start(bf16[8,5,128,128]{3,2,1,0:T(8,128)(2,1)} %shard_map.77), calls=%async_computation | async-start | bytes 2621440 | tf_op jit(solution)/shard_map/all_to_all | solution.py:241
  32.0 6.7 %copy-start.10 = (s32[128]{0:T(128)S(1)}, s32[128]{0:T(128)}, u32[]{:S(2)}) copy-start(s32[128]{0:T(128)} %param.10) | copy-start | bytes 1540
  32.0 6.9 %copy-start.1 = (s32[128]{0:T(128)S(1)}, s32[128]{0:T(128)}, u32[]{:S(2)}) copy-start(s32[128]{0:T(128)} %param.11) | copy-start | bytes 1540
  32.0 33.4 %collective-permute-start.7 = (bf16[576,512]{1,0:T(8,128)(2,1)}, bf16[576,512]{1,0:T(8,128)(2,1)}, u32[]{:S(2)}, u32[]{:S(2)}) collective-permute-start(bf16[576,512]{1,0:T(8,128)(2,1)} %get-tuple-element.42), channel_id=1, source_target_pairs={{0,8},{8,16},{16,24},{24,0},{1,9},{9,17},{17,25},{25,1},{2,10},{10... | collective-permute-start | bytes 1769480 | tf_op jit(solution)/shard_map/ppermute | solution.py:22
  34.5 27.9 %collective-permute-start.9 = (bf16[576,512]{1,0:T(8,128)(2,1)}, bf16[576,512]{1,0:T(8,128)(2,1)}, u32[]{:S(2)}, u32[]{:S(2)}) collective-permute-start(bf16[576,512]{1,0:T(8,128)(2,1)} %get-tuple-element.41), channel_id=1, source_target_pairs={{0,24},{8,0},{16,8},{24,16},{1,25},{9,1},{17,9},{25,17},{2,26},{10... | collective-permute-start | bytes 1769480 | tf_op jit(solution)/shard_map/ppermute | solution.py:22
  34.5 57.3 %collective-permute-start.8 = (bf16[576,512]{1,0:T(8,128)(2,1)}, bf16[576,512]{1,0:T(8,128)(2,1)}, u32[]{:S(2)}, u32[]{:S(2)}) collective-permute-start(bf16[576,512]{1,0:T(8,128)(2,1)} %get-tuple-element.44), channel_id=1, source_target_pairs={{0,16},{8,24},{16,0},{24,8},{1,17},{9,25},{17,1},{25,9},{2,18},{10... | collective-permute-start | bytes 1769480 | tf_op jit(solution)/shard_map/ppermute | solution.py:22
  38.7 3.2 %collective-permute-start.6 = (bf16[4,4,16,2304]{3,2,1,0:T(8,128)(2,1)}, bf16[4,4,16,2304]{3,2,1,0:T(8,128)(2,1)}, u32[]{:S(2)}, u32[]{:S(2)}) collective-permute-start(bf16[4,4,16,2304]{3,2,1,0:T(8,128)(2,1)} %get-tuple-element.46), channel_id=1, source_target_pairs={{0,1},{1,0},{2,3},{3,2},{4,5},{5,4},{6,7},{7,6},{8,9},{9,8},{10,11... | collective-permute-start | bytes 3538952 | tf_op jit(solution)/shard_map/ppermute | solution.py:37
  39.5 5.2 %copy-start.11 = (s32[16]{0:T(128)}, s32[16]{0:T(128)S(1)}, u32[]{:S(2)}) copy-start(s32[16]{0:T(128)S(1)} %gather_fusion.3) | copy-start | bytes 196
  47.1 44.7 %copy-start.2 = (bf16[8,4,16,2304]{3,2,1,0:T(8,128)(2,1)}, bf16[8,4,16,2304]{3,2,1,0:T(8,128)(2,1)S(1)}, u32[]{:S(2)}) copy-start(bf16[8,4,16,2304]{3,2,1,0:T(8,128)(2,1)S(1)} %gather_fusion.2) | copy-start | bytes 7077892
  52.6 42.4 %collective-permute-start.10 = (bf16[4,128,128]{2,1,0:T(8,128)(2,1)S(1)}, bf16[4,128,128]{2,1,0:T(8,128)(2,1)}, u32[]{:S(2)}, u32[]{:S(2)}) collective-permute-start(bf16[4,128,128]{2,1,0:T(8,128)(2,1)S(1)} %get-tuple-element.51), channel_id=1, source_target_pairs={{0,8},{8,16},{16,24},{24,0},{1,9},{9,17},{17,25},{25,1},{2,10},{10... | collective-permute-start | bytes 393224 | tf_op jit(solution)/shard_map/ppermute | solution.py:22
  55.2 41.7 %collective-permute-start.11 = (bf16[4,128,128]{2,1,0:T(8,128)(2,1)S(1)}, bf16[4,128,128]{2,1,0:T(8,128)(2,1)}, u32[]{:S(2)}, u32[]{:S(2)}) collective-permute-start(bf16[4,128,128]{2,1,0:T(8,128)(2,1)S(1)} %get-tuple-element.50), channel_id=1, source_target_pairs={{0,16},{8,24},{16,0},{24,8},{1,17},{9,25},{17,1},{25,9},{2,18},{10... | collective-permute-start | bytes 393224 | tf_op jit(solution)/shard_map/ppermute | solution.py:22
  62.5 34.4 %collective-permute-start.12 = (bf16[4,128,128]{2,1,0:T(8,128)(2,1)S(1)}, bf16[4,128,128]{2,1,0:T(8,128)(2,1)S(1)}, u32[]{:S(2)}, u32[]{:S(2)}) collective-permute-start(bf16[4,128,128]{2,1,0:T(8,128)(2,1)S(1)} %get-tuple-element.49), channel_id=1, source_target_pairs={{0,24},{8,0},{16,8},{24,16},{1,25},{9,1},{17,9},{25,17},{2,26},{10... | collective-permute-start | bytes 393224 | tf_op jit(solution)/shard_map/ppermute | solution.py:22
  67.2 27.8 %copy-start.12 = (f32[1,128]{1,0:T(1,128)S(1)}, f32[1,128]{1,0:T(1,128)}, u32[]{:S(2)}) copy-start(f32[1,128]{1,0:T(1,128)} %get-tuple-element.18) | copy-start | bytes 1540
  98.2 20.9 %all-to-all-start.1 = ((f32[32,9,128]{2,1,0:T(8,128)}), f32[32,9,128]{2,1,0:T(8,128)}, u32[]{:S(2)}, u32[]{:S(2)}) async-start(f32[32,9,128]{2,1,0:T(8,128)} %broadcast_in_dim.99), calls=%async_computation.1 | async-start | bytes 524288 | tf_op jit(solution)/shard_map/all_to_all | solution.py:17
  104.1 3.2 %copy-start.6 = (bf16[4,128,128]{2,1,0:T(8,128)(2,1)S(1)}, bf16[4,128,128]{2,1,0:T(8,128)(2,1)}, u32[]{:S(2)}) copy-start(bf16[4,128,128]{2,1,0:T(8,128)(2,1)} %get-tuple-element.20) | copy-start | bytes 393220
  104.1 3.2 %copy-start.9 = (bf16[4,128,128]{2,1,0:T(8,128)(2,1)S(1)}, bf16[4,128,128]{2,1,0:T(8,128)(2,1)}, u32[]{:S(2)}) copy-start(bf16[4,128,128]{2,1,0:T(8,128)(2,1)} %copy-done.8) | copy-start | bytes 393220
  128.2 4.9 %collective-permute-start.17 = (f32[4,4,16,2304]{3,2,1,0:T(8,128)}, f32[4,4,16,2304]{3,2,1,0:T(8,128)}, u32[]{:S(2)}, u32[]{:S(2)}) collective-permute-start(f32[4,4,16,2304]{3,2,1,0:T(8,128)} %fusion.50), channel_id=1, source_target_pairs={{0,1},{1,0},{2,3},{3,2},{4,5},{5,4},{6,7},{7,6},{8,9},{9,8},{10,11... | collective-permute-start | bytes 7077896 | tf_op jit(solution)/shard_map/ppermute | solution.py:65
  137.9 30.3 %collective-permute-start.18 = (f32[4,16,2304]{2,1,0:T(8,128)}, f32[4,16,2304]{2,1,0:T(8,128)S(1)}, u32[]{:S(2)}, u32[]{:S(2)}) collective-permute-start(f32[4,16,2304]{2,1,0:T(8,128)} %get-tuple-element.38), channel_id=1, source_target_pairs={{0,2},{1,3},{2,0},{3,1},{4,6},{5,7},{6,4},{7,5},{8,10},{9,11},{10,... | collective-permute-start | bytes 1769480 | tf_op jit(solution)/shard_map/ppermute | solution.py:70
  138.4 31.1 %collective-permute-start.19 = (f32[4,16,2304]{2,1,0:T(8,128)S(1)}, f32[4,16,2304]{2,1,0:T(8,128)S(1)}, u32[]{:S(2)}, u32[]{:S(2)}) collective-permute-start(f32[4,16,2304]{2,1,0:T(8,128)S(1)} %get-tuple-element.40), channel_id=1, source_target_pairs={{0,4},{1,5},{2,6},{3,7},{4,0},{5,1},{6,2},{7,3},{8,12},{9,13},{10,... | collective-permute-start | bytes 1769480 | tf_op jit(solution)/shard_map/ppermute | solution.py:70
  139.9 29.6 %collective-permute-start.20 = (f32[4,16,2304]{2,1,0:T(8,128)S(1)}, f32[4,16,2304]{2,1,0:T(8,128)S(1)}, u32[]{:S(2)}, u32[]{:S(2)}) collective-permute-start(f32[4,16,2304]{2,1,0:T(8,128)S(1)} %get-tuple-element.39), channel_id=1, source_target_pairs={{0,6},{1,7},{2,4},{3,5},{4,2},{5,3},{6,0},{7,1},{8,14},{9,15},{10,... | collective-permute-start | bytes 1769480 | tf_op jit(solution)/shard_map/ppermute | solution.py:70
  141.4 25.5 %collective-permute-start.15 = (bf16[512,512]{1,0:T(8,128)(2,1)}, bf16[512,512]{1,0:T(8,128)(2,1)}, u32[]{:S(2)}, u32[]{:S(2)}) collective-permute-start(bf16[512,512]{1,0:T(8,128)(2,1)} %fusion.7), channel_id=1, source_target_pairs={{0,16},{8,24},{16,0},{24,8},{1,17},{9,25},{17,1},{25,9},{2,18},{10... | collective-permute-start | bytes 1572872 | tf_op jit(solution)/shard_map/ppermute | solution.py:22
  141.9 41.4 %collective-permute-start.13 = (bf16[512,512]{1,0:T(8,128)(2,1)}, bf16[512,512]{1,0:T(8,128)(2,1)}, u32[]{:S(2)}, u32[]{:S(2)}) collective-permute-start(bf16[512,512]{1,0:T(8,128)(2,1)} %fusion.7), channel_id=1, source_target_pairs={{8,0},{16,8},{24,16},{9,1},{17,9},{25,17},{10,2},{18,10},{26,18},{... | collective-permute-start | bytes 1572872 | tf_op jit(solution)/shard_map/ppermute | solution.py:50
  166.9 18.2 %collective-permute-start.14 = (bf16[512,512]{1,0:T(8,128)(2,1)}, bf16[512,512]{1,0:T(8,128)(2,1)}, u32[]{:S(2)}, u32[]{:S(2)}) collective-permute-start(bf16[512,512]{1,0:T(8,128)(2,1)} %fusion.7), channel_id=1, source_target_pairs={{0,8},{8,16},{16,24},{1,9},{9,17},{17,25},{2,10},{10,18},{18,26},{... | collective-permute-start | bytes 1572872 | tf_op jit(solution)/shard_map/ppermute | solution.py:49
  168.2 33.2 %collective-permute-start.16 = (bf16[512,512]{1,0:T(8,128)(2,1)}, bf16[512,512]{1,0:T(8,128)(2,1)}, u32[]{:S(2)}, u32[]{:S(2)}) collective-permute-start(bf16[512,512]{1,0:T(8,128)(2,1)} %collective-permute-done.15), channel_id=1, source_target_pairs={{8,0},{16,24},{9,1},{17,25},{10,2},{18,26},{11,3},{19,27},{12,4},{... | collective-permute-start | bytes 1572872 | tf_op jit(solution)/shard_map/ppermute | solution.py:51
  171.6 8.9 %copy-start.3 = (bf16[8,4,16,2304]{3,2,1,0:T(8,128)(2,1)S(1)}, bf16[8,4,16,2304]{3,2,1,0:T(8,128)(2,1)}, u32[]{:S(2)}) copy-start(bf16[8,4,16,2304]{3,2,1,0:T(8,128)(2,1)} %copy-done.2) | copy-start | bytes 7077892
  171.6 32.7 %all-to-all-start.2 = ((f32[4,16,2304]{2,1,0:T(8,128)}), f32[4,16,2304]{2,1,0:T(8,128)S(1)}, u32[]{:S(2)}, u32[]{:S(2)}) async-start(f32[4,16,2304]{2,1,0:T(8,128)} %fusion.16), calls=%async_computation.2 | async-start | bytes 1179648 | tf_op jit(solution)/shard_map/all_to_all | solution.py:294
  (5 other events, 4.8 us)

commit v4 on v3

--- a/solution.py
+++ b/solution.py
@@ -183,6 +183,38 @@
     )(anchor, counts, arrived.reshape(-1, lanes, tok_rows))
 
 
+def place_kernel(planes, origin_ref, *refs):
+    heads, kepts, (head_ref, kept_ref) = refs[:planes], refs[planes : 2 * planes], refs[2 * planes :]
+    shards, _, rows, _ = kept_ref.shape
+    for distance in range(planes):
+        origin = origin_ref[distance]
+        slab, _ = heads[distance].shape
+        head_ref[pl.ds(pl.multiple_of(origin * slab, 16), slab), :] = heads[distance][...]
+        blocks, lanes, _ = kepts[distance].shape
+        for block in range(blocks):
+            tile = kepts[distance][block].astype(jnp.float32).T
+            for shard in range(shards):
+                kept_ref[shard, pl.ds(origin, 1), :, block * lanes : (block + 1) * lanes] = tile[
+                    None, shard * rows : (shard + 1) * rows
+                ]
+
+
+def place(origins, heads, kepts, shards):
+    planes = len(heads)
+    slab, part_cols = heads[0].shape
+    rows = kepts[0].shape[2] // shards
+    vmem = pl.BlockSpec(memory_space=pltpu.VMEM)
+    return pl.pallas_call(
+        functools.partial(place_kernel, planes),
+        out_shape=(
+            jax.ShapeDtypeStruct((planes * slab, part_cols), heads[0].dtype),
+            jax.ShapeDtypeStruct((shards, planes, rows, part_cols), jnp.float32),
+        ),
+        in_specs=[pl.BlockSpec(memory_space=pltpu.SMEM)] + [vmem] * (2 * planes),
+        out_specs=[vmem] * 2,
+    )(origins, *heads, *kepts)
+
+
 def shards(teacher_logits, student_hidden, student_head, keep_ids, block_owner, block_count):
     planes = lax.axis_size("dp")
     plane = lax.axis_index("dp")
@@ -260,26 +292,24 @@
     masked = jnp.where(valid_cols, scores, -jnp.inf)
     local_top = jnp.max(masked, axis=1)
     weight = jnp.where(valid_cols, jnp.exp(masked - local_top[:, None]), 0.0)
-    student = jnp.concatenate([local_top, jnp.sum(weight, axis=1), mass_part])
+    mass = jnp.where(
+        jnp.arange(planes, dtype=jnp.int32)[None, :, None] == plane,
+        mass_part.reshape(shard_count, 1, slice_rows), 0.0,
+    ).reshape(tokens)
+    student = jnp.stack([local_top, jnp.sum(weight, axis=1), mass])
     pieces, kept, student = lax.optimization_barrier((pieces, kept, student))
-    kept = in_order(kept, "dp").reshape(
-        planes, part_cols, tok_rows
-    ).transpose(0, 2, 1).reshape(planes, shard_count, slice_rows, part_cols)
-    kept = kept.transpose(1, 0, 2, 3).reshape(tokens, part_cols).astype(jnp.float32)
-    student = exchange(student.reshape(-1, tok_rows), ("dp", "vocab")).reshape(
-        planes * shard_count, 2 * planes + 1, tok_rows
-    )
-    tops, norms = student[:, :planes], student[:, planes : 2 * planes]
-    student_top = jnp.max(tops, axis=0)
-    exp_norm = jnp.sum(norms * jnp.exp(tops - student_top), axis=0)
-    kept_mass = jnp.sum(student[:, 2 * planes].reshape(planes, shard_count, tok_rows), axis=1)
-    kept_mass = kept_mass.reshape(planes, shard_count, slice_rows).transpose(1, 0, 2).reshape(-1)
-    factor = jnp.exp(local_top - student_top.reshape(-1)) / exp_norm.reshape(-1) * kept_mass
+    origins = jnp.stack([above("dp", -distance) for distance in range(planes)])
+    head, kept = place(origins, pieces, kept, shard_count)
+    kept = kept.reshape(tokens, part_cols)
+    student = exchange(student, ("dp", "vocab")).reshape(planes * shard_count, 3, tokens)
+    student_top = jnp.max(student[:, 0], axis=0)
+    exp_norm = jnp.sum(student[:, 1] * jnp.exp(student[:, 0] - student_top), axis=0)
+    kept_mass = jnp.sum(student[:, 2], axis=0)
+    factor = jnp.exp(local_top - student_top) / exp_norm * kept_mass
     gradient = (loss_scale * (weight * factor[:, None] - kept)).astype(jnp.bfloat16)
 
     gradients = [(plane, gradient)] + spread(gradient, "dp")
 
-    head = in_order(pieces, "dp").reshape(width, part_cols)
     by_pair = gradient.reshape(shard_count // 2, 2, planes * slice_rows, part_cols)
 
     def part(last_bit):

time: 206 us -> 197 us (0.956)
  the two profiles are of different devices: /device:TPU:26 before, /device:TPU:24 now
where the time goes in v4:
time: 197 us; the launch traced here: 196 us
  waiting for transfers between devices  70.1 us (36%)
  starting transfers between devices  47 us (24%)
  matrix products  23.3 us (12%)
  local copies, waits for them, and re-layouts  20.7 us (11%)
  other arithmetic  18.5 us (9%)
  Pallas kernels  15.6 us (8%)
    ppermute x10, waiting for transfers between devices, shift(): lax.ppermute(value, axis, [(p, (p + distance) % size) for p in range(size)])  32.4 us
    ppermute x3, waiting for transfers between devices, chip_gather(): lax.ppermute(value, axis, [(i, i ^ 2 * step) for i in range(size)])  17.6 us
    ppermute x10, starting transfers between devices, shift(): lax.ppermute(value, axis, [(p, (p + distance) % size) for p in range(size)])  14.9 us
    dot_general x4, matrix products, shards(): lax.dot_general(own_hidden, columns_part, (((0,), (0,)), ((), ())), prefe...  11.1 us
    ppermute x1, waiting for transfers between devices, spread(): relay = lax.ppermute(middle, axis, [(1, 0), (2, 3)])  10.9 us
    pallas_call x1, Pallas kernels, pick(): pl.pallas_call(functools.partial(pick_kernel, capacity), out_shape=jax.Sh...  8.99 us
    all_to_all x1, starting transfers between devices, shards(): sums = lax.all_to_all(sums, 'dp', split_axis=0, concat_axis=0, tiled=True)  8.44 us
    dot_general x4, matrix products, shards(): jnp.dot(lax.dynamic_slice_in_dim(hidden, above('dp', -distance) * slab, s...  6.77 us
  transfers between devices with their start and end apart: 24, of which 9 were waited for; matrix products, arithmetic and copies ran while one was open for 24% of the time, Pallas kernels for 8%

profile of v4, /device:TPU:24, one launch (start us, length us, event | category | flops | bytes accessed | tf_op | source)
XLA Modules:
  0.0 196.1 jit_solution(1182853669618976527)
XLA Ops:
  10.3 9.0 %shard_map.77 = bf16[8,5,128,128]{3,2,1,0:T(8,128)(2,1)} custom-call(s32[4096]{0:T(1024)} %clamp_bitcast_fusion.ids_ref, s32[32]{0:T(128)} %get-tuple-element.36.count_ref, bf16[8000,128]{1,0:T(8,128)(2,1)} %bitcast.106), custom_call_target="tpu_custom_call" | custom-call | tf_op jit(solution)/shard_map/pallas_call | solution.py:130
  19.3 4.3 %all-to-all-start = ((bf16[8,5,128,128]{3,2,1,0:T(8,128)(2,1)}), bf16[8,5,128,128]{3,2,1,0:T(8,128)(2,1)}, u32[]{:S(2)}, u32[]{:S(2)}) async-start(bf16[8,5,128,128]{3,2,1,0:T(8,128)(2,1)} %shard_map.77), calls=%async_computation | async-start | bytes 2621440 | tf_op jit(solution)/shard_map/all_to_all | solution.py:273
  24.4 2.0 collective-permute-start.3
  27.9 2.8 %constant_dynamic-slice_fusion.2 = (bf16[576,512]{1,0:T(8,128)(2,1)}, bf16[576,512]{1,0:T(8,128)(2,1)}, bf16[576,512]{1,0:T(8,128)(2,1)S(1)}, bf16[576,512]{1,0:T(8,128)(2,1)}) fusion(bf16[576,2048]{1,0:T(8,128)(2,1)} %param.8, s32[]{:T(128)S(6)} %select_n.225, s32[]{:T(128)S(6)} %select_n.221, s32[]{:T(128)S(6)} %select_n.219, s32[]{:T(128)S(6)} %select_n.223), kind=kLoop, calls=%fused_computation.86 | loop fusion | bytes 4718608 | tf_op jit(solution)/shard_map/dynamic_slice | solution.py:236
  30.8 3.4 %collective-permute-start.7 = (bf16[576,512]{1,0:T(8,128)(2,1)}, bf16[576,512]{1,0:T(8,128)(2,1)}, u32[]{:S(2)}, u32[]{:S(2)}) collective-permute-start(bf16[576,512]{1,0:T(8,128)(2,1)} %get-tuple-element.48), channel_id=1, source_target_pairs={{0,8},{8,16},{16,24},{24,0},{1,9},{9,17},{17,25},{25,1},{2,10},{10... | collective-permute-start | bytes 1769480 | tf_op jit(solution)/shard_map/ppermute | solution.py:22
  34.2 13.6 %collective-permute-done.3 = bf16[4,16,2304]{2,1,0:T(8,128)(2,1)S(1)} collective-permute-done((bf16[4,16,2304]{2,1,0:T(8,128)(2,1)S(1)}, bf16[4,16,2304]{2,1,0:T(8,128)(2,1)S(1)}, u32[]{:S(2)}, u32[]{:S(2)}) %collective-permute-start.3) | collective-permute-done | bytes 294944 | tf_op jit(solution)/shard_map/ppermute | solution.py:35
  47.7 2.6 %collective-permute-start.8 = (bf16[576,512]{1,0:T(8,128)(2,1)}, bf16[576,512]{1,0:T(8,128)(2,1)}, u32[]{:S(2)}, u32[]{:S(2)}) collective-permute-start(bf16[576,512]{1,0:T(8,128)(2,1)} %get-tuple-element.50), channel_id=1, source_target_pairs={{0,16},{8,24},{16,0},{24,8},{1,17},{9,25},{17,1},{25,9},{2,18},{10... | collective-permute-start | bytes 1769480 | tf_op jit(solution)/shard_map/ppermute | solution.py:22
  50.3 4.1 %collective-permute-done.5 = bf16[4,16,2304]{2,1,0:T(8,128)(2,1)S(1)} collective-permute-done((bf16[4,16,2304]{2,1,0:T(8,128)(2,1)S(1)}, bf16[4,16,2304]{2,1,0:T(8,128)(2,1)S(1)}, u32[]{:S(2)}, u32[]{:S(2)}) %collective-permute-start.5) | collective-permute-done | bytes 294944 | tf_op jit(solution)/shard_map/ppermute | solution.py:35
  55.1 2.2 %fusion.50 = (bf16[4,1,4,16,2304]{4,3,2,1,0:T(8,128)(2,1)S(1)}, bf16[4,4,16,2304]{3,2,1,0:T(8,128)(2,1)}) fusion(bf16[1,4,16,2304]{3,2,1,0:T(8,128)(2,1)} %bitcast.113, bf16[1,4,16,2304]{3,2,1,0:T(8,128)(2,1)S(1)} %bitcast.112, bf16[1,4,16,2304]{3,2,1,0:T(8,128)(2,1)S(1)} %bitcast.111, bf16[1,4,16,2304]{3,2,1,0:T(8,128)(2,1)S(1)} %bitcast.107), kind=kLoop, calls=%fused_computation.123 | loop fusion | flops 1769472 | bytes 3538944 | tf_op jit(solution)/shard_map/stack | solution.py:38
  60.5 2.9 %pad_maximum_fusion = bf16[4,2,4,16,2304]{4,3,2,1,0:T(8,128)(2,1)} fusion(bf16[4,1,4,16,2304]{4,3,2,1,0:T(8,128)(2,1)} %bitcast.15, bf16[4,1,4,16,2304]{4,3,2,1,0:T(8,128)(2,1)S(1)} %get-tuple-element.51), kind=kLoop, calls=%fused_computation.7 | loop fusion | flops 1179648 | bytes 4718592 | tf_op jit(solution)/shard_map/stack | solution.py:38
  63.4 2.4 %gather_fusion.2 = bf16[8,4,16,2304]{3,2,1,0:T(8,128)(2,1)S(1)} fusion(bf16[8,4,16,2304]{3,2,1,0:T(8,128)(2,1)} %bitcast.105, s32[1024]{0:T(1024)S(1)} %pad_clamp_fusion.1), kind=kCustom, calls=%fused_computation.2 | custom fusion | bytes 4718624 | tf_op jit(solution)/shard_map/jit(_take)/gather | solution.py:40
  65.7 2.8 %shard_map.78 = (bf16[16,128,128]{2,1,0:T(8,128)(2,1)}, f32[1,128]{1,0:T(1,128)}) custom-call(s32[16]{0:T(128)} %multiply_add_fusion.anchor_ref, s32[16]{0:T(128)} %copy-done.10, bf16[40,128,128]{2,1,0:T(8,128)(2,1)} %bitcast.22.arrived_ref), custom_call_target="tpu_custom_call" | custom-call | tf_op jit(solution)/shard_map/pallas_call | solution.py:171
  70.5 3.4 %collective-permute-start.10 = (bf16[4,128,128]{2,1,0:T(8,128)(2,1)}, bf16[4,128,128]{2,1,0:T(8,128)(2,1)}, u32[]{:S(2)}, u32[]{:S(2)}) collective-permute-start(bf16[4,128,128]{2,1,0:T(8,128)(2,1)} %get-tuple-element.57), channel_id=1, source_target_pairs={{0,8},{8,16},{16,24},{24,0},{1,9},{9,17},{17,25},{25,1},{2,10},{10... | collective-permute-start | bytes 393224 | tf_op jit(solution)/shard_map/ppermute | solution.py:22
  81.3 10.2 %collective-permute-done.8.refs_2_ = bf16[576,512]{1,0:T(8,128)(2,1)} collective-permute-done((bf16[576,512]{1,0:T(8,128)(2,1)}, bf16[576,512]{1,0:T(8,128)(2,1)}, u32[]{:S(2)}, u32[]{:S(2)}) %collective-permute-start.8) | collective-permute-done | bytes 589856 | tf_op jit(solution)/shard_map/ppermute | solution.py:22
  94.7 2.3 %collective-permute-done.11.refs_6_ = bf16[4,128,128]{2,1,0:T(8,128)(2,1)} collective-permute-done((bf16[4,128,128]{2,1,0:T(8,128)(2,1)}, bf16[4,128,128]{2,1,0:T(8,128)(2,1)}, u32[]{:S(2)}, u32[]{:S(2)}) %collective-permute-start.11) | collective-permute-done | bytes 131104 | tf_op jit(solution)/shard_map/ppermute | solution.py:22
  97.8 6.0 %all-to-all-start.1 = ((f32[32,3,512]{2,1,0:T(4,128)}), f32[32,3,512]{2,1,0:T(4,128)S(1)}, u32[]{:S(2)}, u32[]{:S(2)}) async-start(f32[32,3,512]{2,1,0:T(4,128)} %broadcast_in_dim.120), calls=%async_computation.1 | async-start | bytes 524288 | tf_op jit(solution)/shard_map/all_to_all | solution.py:17
  104.4 3.8 %shard_map.79 = (bf16[2304,512]{1,0:T(8,128)(2,1)}, f32[8,4,16,512]{3,2,1,0:T(8,128)}) custom-call(s32[4]{0:T(128)} %pad_add_fusion.origin_ref, bf16[576,512]{1,0:T(8,128)(2,1)} %copy-done.5, bf16[576,512]{1,0:T(8,128)(2,1)} %collective-permute-done.7.refs_1_, bf16[576,512]{1,0:T(8,128)(2,1)} %collective-permute-done.8.refs_2_, ...), custom_call_target="tpu_custom_call" | custom-call | tf_op jit(solution)/shard_map/pallas_call | solution.py:207
  108.2 3.9 %all-to-all-done.1 = f32[32,3,512]{2,1,0:T(4,128)S(1)} async-done(((f32[32,3,512]{2,1,0:T(4,128)}), f32[32,3,512]{2,1,0:T(4,128)S(1)}, u32[]{:S(2)}, u32[]{:S(2)}) %all-to-all-start.1) | async-done | bytes 196640 | tf_op jit(solution)/shard_map/all_to_all | solution.py:17
  112.3 2.8 %fusion.10 = bf16[512,512]{1,0:T(8,128)(2,1)} fusion(f32[8,4,16,512]{3,2,1,0:T(8,128)} %get-tuple-element.30, f32[512,512]{1,0:T(8,128)} %copy-done.4, f32[512]{0:T(512)S(1)} %divide_multiply_fusion, f32[512]{0:T(512)S(1)} %get-tuple-element.61, pred[512]{0:T(512)(128)(4,1)S(1)} %fusion.45), kind=kLoop, calls=%fused_computation.26 | loop fusion | flops 1572864 | bytes 2626048 | tf_op jit(solution)/shard_map/convert_element_type | solution.py:309
  116.2 2.2 %fusion = f32[4,4,16,2304]{3,2,1,0:T(8,128)} fusion(bf16[4,4,16,512]{3,2,1,0:T(8,128)(2,1)S(1)} %bitcast.109, bf16[2304,512]{1,0:T(8,128)(2,1)S(1)} %copy-done.2), kind=kOutput, calls=%fused_computation.8 | convolution fusion | flops 603979776 | bytes 4980736 | tf_op jit(solution)/shard_map/dot_general | solution.py:317
  118.4 4.9 %collective-permute-done.17 = f32[4,4,16,2304]{3,2,1,0:T(8,128)} collective-permute-done((f32[4,4,16,2304]{3,2,1,0:T(8,128)}, f32[4,4,16,2304]{3,2,1,0:T(8,128)}, u32[]{:S(2)}, u32[]{:S(2)}) %collective-permute-start.17) | collective-permute-done | bytes 2359328 | tf_op jit(solution)/shard_map/ppermute | solution.py:65
  123.3 3.2 %convolution_add_fusion = f32[4,4,16,2304]{3,2,1,0:T(8,128)S(1)} fusion(f32[4,4,16,2304]{3,2,1,0:T(8,128)} %collective-permute-done.17, bf16[4,4,16,512]{3,2,1,0:T(8,128)(2,1)S(1)} %bitcast.108, bf16[2304,512]{1,0:T(8,128)(2,1)} %get-tuple-element.31), kind=kOutput, calls=%fused_computation.6 | convolution fusion | flops 604569600 | bytes 7340032 | tf_op jit(solution)/shard_map/dot_general | solution.py:317
  132.6 2.0 collective-permute-start.15
  134.5 3.8 %collective-permute-start.13 = (bf16[512,512]{1,0:T(8,128)(2,1)}, bf16[512,512]{1,0:T(8,128)(2,1)}, u32[]{:S(2)}, u32[]{:S(2)}) collective-permute-start(bf16[512,512]{1,0:T(8,128)(2,1)} %fusion.10), channel_id=1, source_target_pairs={{8,0},{16,8},{24,16},{9,1},{17,9},{25,17},{10,2},{18,10},{26,18},{... | collective-permute-start | bytes 1572872 | tf_op jit(solution)/shard_map/ppermute | solution.py:50
  138.3 19.8 %collective-permute-done.15 = bf16[512,512]{1,0:T(8,128)(2,1)} collective-permute-done((bf16[512,512]{1,0:T(8,128)(2,1)}, bf16[512,512]{1,0:T(8,128)(2,1)}, u32[]{:S(2)}, u32[]{:S(2)}) %collective-permute-start.15) | collective-permute-done | bytes 524320 | tf_op jit(solution)/shard_map/ppermute | solution.py:22
  160.7 2.5 %fusion.19 = f32[4,16,2304]{2,1,0:T(8,128)} fusion(f32[4,16,2304]{2,1,0:T(8,128)} %collective-permute-done.20, f32[4,16,2304]{2,1,0:T(8,128)} %collective-permute-done.19, f32[4,16,2304]{2,1,0:T(8,128)} %collective-permute-done.18, f32[4,4,16,2304]{3,2,1,0:T(8,128)} %copy-done.3, s32[]{:T(128)S(6)} %select_n.249), kind=kLoop, calls=%fused_computation.37 | loop fusion | flops 442368 | bytes 2949124 | tf_op jit(solution)/shard_map/add | solution.py:71
  163.3 8.4 %all-to-all-start.2 = ((f32[4,16,2304]{2,1,0:T(8,128)}), f32[4,16,2304]{2,1,0:T(8,128)S(1)}, u32[]{:S(2)}, u32[]{:S(2)}) async-start(f32[4,16,2304]{2,1,0:T(8,128)} %fusion.19), calls=%async_computation.2 | async-start | bytes 1179648 | tf_op jit(solution)/shard_map/all_to_all | solution.py:324
  173.4 2.8 %fusion.8 = bf16[576,2048]{1,0:T(8,128)(2,1)} fusion(bf16[576,2048]{1,0:T(8,128)(2,1)} %broadcast_in_dim.108, s32[]{:T(128)S(6)} %select_n.234, bf16[512,512]{1,0:T(8,128)(2,1)} %fusion.10, bf16[512,2304]{1,0:T(8,128)(2,1)S(1)} %bitcast.101, s32[]{:T(128)S(6)} %select_n.214), kind=kOutput, calls=%fused_computation.22 | convolution fusion | flops 302284800 | bytes 1769480 | tf_op jit(solution)/shard_map/dot_general | solution.py:330
  176.2 2.8 %fusion.7 = bf16[576,2048]{1,0:T(8,128)(2,1)} fusion(bf16[576,2048]{1,0:T(8,128)(2,1)} %fusion.8, s32[]{:T(128)S(6)} %select_n.238, bf16[512,512]{1,0:T(8,128)(2,1)} %collective-permute-done.13, bf16[512,512]{1,0:T(8,128)(2,1)} %collective-permute-done.14, pred[]{:T(512)S(6)} %eq.125, bf16[512,2304]{1,0:T(8,128)(2,1)S(1)} %bitcast.102, s32[]{:T(128)S(6)} %select_n.214), kind=kOutput, calls=%fused_computation.20 | convolution fusion | flops 302546944 | bytes 2293769 | tf_op jit(solution)/shard_map/dot_general | solution.py:330
  178.9 2.8 %fusion.6 = bf16[576,2048]{1,0:T(8,128)(2,1)} fusion(bf16[576,2048]{1,0:T(8,128)(2,1)} %fusion.7, s32[]{:T(128)S(6)} %select_n.239, bf16[512,512]{1,0:T(8,128)(2,1)} %collective-permute-done.15, bf16[512,2304]{1,0:T(8,128)(2,1)S(1)} %bitcast.103, s32[]{:T(128)S(6)} %select_n.214), kind=kOutput, calls=%fused_computation.18 | convolution fusion | flops 302284800 | bytes 1769480 | tf_op jit(solution)/shard_map/dot_general | solution.py:330
  181.7 10.9 %collective-permute-done.16 = bf16[512,512]{1,0:T(8,128)(2,1)} collective-permute-done((bf16[512,512]{1,0:T(8,128)(2,1)}, bf16[512,512]{1,0:T(8,128)(2,1)}, u32[]{:S(2)}, u32[]{:S(2)}) %collective-permute-start.16) | collective-permute-done | bytes 524320 | tf_op jit(solution)/shard_map/ppermute | solution.py:51
  192.7 2.8 %fusion.5 = bf16[576,2048]{1,0:T(8,128)(2,1)} fusion(bf16[576,2048]{1,0:T(8,128)(2,1)} %fusion.6, s32[]{:T(128)S(6)} %select_n.244, bf16[512,512]{1,0:T(8,128)(2,1)} %collective-permute-done.16, bf16[512,512]{1,0:T(8,128)(2,1)} %collective-permute-done.13, pred[]{:T(512)S(6)} %or.3, bf16[512,2304]{1,0:T(8,128)(2,1)S(1)} %bitcast.104, s32[]{:T(128)S(6)} %select_n.214), kind=kOutput, calls=%fused_computation.16 | convolution fusion | flops 302546944 | bytes 2293769 | tf_op jit(solution)/shard_map/dot_general | solution.py:330
  (105 shorter events, 42.0 us)
Async XLA Ops:
  1.7 22.0 %collective-permute-start = (bf16[16,2304]{1,0:T(8,128)(2,1)S(1)}, bf16[16,2304]{1,0:T(8,128)(2,1)S(1)}, u32[]{:S(2)}, u32[]{:S(2)}) collective-permute-start(bf16[16,2304]{1,0:T(8,128)(2,1)S(1)} %constant_dynamic-slice_fusion.6), channel_id=1, source_target_pairs={{0,8},{8,16},{16,24},{24,0},{1,9},{9,17},{17,25},{25,1},{2,10},{10... | collective-permute-start | bytes 221192 | tf_op jit(solution)/shard_map/ppermute | solution.py:22
  1.7 22.0 %collective-permute-start.1 = (bf16[16,2304]{1,0:T(8,128)(2,1)S(1)}, bf16[16,2304]{1,0:T(8,128)(2,1)S(1)}, u32[]{:S(2)}, u32[]{:S(2)}) collective-permute-start(bf16[16,2304]{1,0:T(8,128)(2,1)S(1)} %constant_dynamic-slice_fusion.6), channel_id=1, source_target_pairs={{0,16},{8,24},{16,0},{24,8},{1,17},{9,25},{17,1},{25,9},{2,18},{10... | collective-permute-start | bytes 221192 | tf_op jit(solution)/shard_map/ppermute | solution.py:22
  3.6 20.1 %collective-permute-start.2 = (bf16[16,2304]{1,0:T(8,128)(2,1)S(1)}, bf16[16,2304]{1,0:T(8,128)(2,1)S(1)}, u32[]{:S(2)}, u32[]{:S(2)}) collective-permute-start(bf16[16,2304]{1,0:T(8,128)(2,1)S(1)} %constant_dynamic-slice_fusion.6), channel_id=1, source_target_pairs={{0,24},{8,0},{16,8},{24,16},{1,25},{9,1},{17,9},{25,17},{2,26},{10... | collective-permute-start | bytes 221192 | tf_op jit(solution)/shard_map/ppermute | solution.py:22
  19.3 46.4 %all-to-all-start = ((bf16[8,5,128,128]{3,2,1,0:T(8,128)(2,1)}), bf16[8,5,128,128]{3,2,1,0:T(8,128)(2,1)}, u32[]{:S(2)}, u32[]{:S(2)}) async-start(bf16[8,5,128,128]{3,2,1,0:T(8,128)(2,1)} %shard_map.77), calls=%async_computation | async-start | bytes 2621440 | tf_op jit(solution)/shard_map/all_to_all | solution.py:273
  24.3 9.8 %copy-start.9 = (s32[128]{0:T(128)S(1)}, s32[128]{0:T(128)}, u32[]{:S(2)}) copy-start(s32[128]{0:T(128)} %param.10) | copy-start | bytes 1540
  24.4 23.3 %collective-permute-start.3 = (bf16[4,16,2304]{2,1,0:T(8,128)(2,1)S(1)}, bf16[4,16,2304]{2,1,0:T(8,128)(2,1)S(1)}, u32[]{:S(2)}, u32[]{:S(2)}) collective-permute-start(bf16[4,16,2304]{2,1,0:T(8,128)(2,1)S(1)} %gather_fusion.1), channel_id=1, source_target_pairs={{0,2},{1,3},{2,0},{3,1},{4,6},{5,7},{6,4},{7,5},{8,10},{9,11},{10,... | collective-permute-start | bytes 884744 | tf_op jit(solution)/shard_map/ppermute | solution.py:35
  26.3 24.0 %collective-permute-start.4 = (bf16[4,16,2304]{2,1,0:T(8,128)(2,1)S(1)}, bf16[4,16,2304]{2,1,0:T(8,128)(2,1)S(1)}, u32[]{:S(2)}, u32[]{:S(2)}) collective-permute-start(bf16[4,16,2304]{2,1,0:T(8,128)(2,1)S(1)} %gather_fusion.1), channel_id=1, source_target_pairs={{0,4},{1,5},{2,6},{3,7},{4,0},{5,1},{6,2},{7,3},{8,12},{9,13},{10,... | collective-permute-start | bytes 884744 | tf_op jit(solution)/shard_map/ppermute | solution.py:35
  27.8 26.6 %collective-permute-start.5 = (bf16[4,16,2304]{2,1,0:T(8,128)(2,1)S(1)}, bf16[4,16,2304]{2,1,0:T(8,128)(2,1)S(1)}, u32[]{:S(2)}, u32[]{:S(2)}) collective-permute-start(bf16[4,16,2304]{2,1,0:T(8,128)(2,1)S(1)} %gather_fusion.1), channel_id=1, source_target_pairs={{0,6},{1,7},{2,4},{3,5},{4,2},{5,3},{6,0},{7,1},{8,14},{9,15},{10,... | collective-permute-start | bytes 884744 | tf_op jit(solution)/shard_map/ppermute | solution.py:35
  30.8 43.1 %copy-start.5 = (bf16[576,512]{1,0:T(8,128)(2,1)}, bf16[576,512]{1,0:T(8,128)(2,1)S(1)}, u32[]{:S(2)}) copy-start(bf16[576,512]{1,0:T(8,128)(2,1)S(1)} %get-tuple-element.22.refs_0_) | copy-start | bytes 1769476
  30.8 26.6 %copy-start.1 = (s32[128]{0:T(128)S(1)}, s32[128]{0:T(128)}, u32[]{:S(2)}) copy-start(s32[128]{0:T(128)} %param.11) | copy-start | bytes 1540
  30.8 48.8 %collective-permute-start.7 = (bf16[576,512]{1,0:T(8,128)(2,1)}, bf16[576,512]{1,0:T(8,128)(2,1)}, u32[]{:S(2)}, u32[]{:S(2)}) collective-permute-start(bf16[576,512]{1,0:T(8,128)(2,1)} %get-tuple-element.48), channel_id=1, source_target_pairs={{0,8},{8,16},{16,24},{24,0},{1,9},{9,17},{17,25},{25,1},{2,10},{10... | collective-permute-start | bytes 1769480 | tf_op jit(solution)/shard_map/ppermute | solution.py:22
  34.1 42.5 %collective-permute-start.9 = (bf16[576,512]{1,0:T(8,128)(2,1)}, bf16[576,512]{1,0:T(8,128)(2,1)}, u32[]{:S(2)}, u32[]{:S(2)}) collective-permute-start(bf16[576,512]{1,0:T(8,128)(2,1)} %get-tuple-element.47), channel_id=1, source_target_pairs={{0,24},{8,0},{16,8},{24,16},{1,25},{9,1},{17,9},{25,17},{2,26},{10... | collective-permute-start | bytes 1769480 | tf_op jit(solution)/shard_map/ppermute | solution.py:22
  47.7 43.8 %collective-permute-start.8 = (bf16[576,512]{1,0:T(8,128)(2,1)}, bf16[576,512]{1,0:T(8,128)(2,1)}, u32[]{:S(2)}, u32[]{:S(2)}) collective-permute-start(bf16[576,512]{1,0:T(8,128)(2,1)} %get-tuple-element.50), channel_id=1, source_target_pairs={{0,16},{8,24},{16,0},{24,8},{1,17},{9,25},{17,1},{25,9},{2,18},{10... | collective-permute-start | bytes 1769480 | tf_op jit(solution)/shard_map/ppermute | solution.py:22
  57.3 3.2 %collective-permute-start.6 = (bf16[4,4,16,2304]{3,2,1,0:T(8,128)(2,1)}, bf16[4,4,16,2304]{3,2,1,0:T(8,128)(2,1)}, u32[]{:S(2)}, u32[]{:S(2)}) collective-permute-start(bf16[4,4,16,2304]{3,2,1,0:T(8,128)(2,1)} %get-tuple-element.52), channel_id=1, source_target_pairs={{0,1},{1,0},{2,3},{3,2},{4,5},{5,4},{6,7},{7,6},{8,9},{9,8},{10,11... | collective-permute-start | bytes 3538952 | tf_op jit(solution)/shard_map/ppermute | solution.py:37
  58.1 5.3 %copy-start.10 = (s32[16]{0:T(128)}, s32[16]{0:T(128)S(1)}, u32[]{:S(2)}) copy-start(s32[16]{0:T(128)S(1)} %gather_fusion.3) | copy-start | bytes 196
  68.5 7.4 %copy-start.11 = (f32[1,128]{1,0:T(1,128)S(1)}, f32[1,128]{1,0:T(1,128)}, u32[]{:S(2)}) copy-start(f32[1,128]{1,0:T(1,128)} %get-tuple-element.20) | copy-start | bytes 1540
  70.5 24.3 %collective-permute-start.10 = (bf16[4,128,128]{2,1,0:T(8,128)(2,1)}, bf16[4,128,128]{2,1,0:T(8,128)(2,1)}, u32[]{:S(2)}, u32[]{:S(2)}) collective-permute-start(bf16[4,128,128]{2,1,0:T(8,128)(2,1)} %get-tuple-element.57), channel_id=1, source_target_pairs={{0,8},{8,16},{16,24},{24,0},{1,9},{9,17},{17,25},{25,1},{2,10},{10... | collective-permute-start | bytes 393224 | tf_op jit(solution)/shard_map/ppermute | solution.py:22
  73.8 23.2 %collective-permute-start.11 = (bf16[4,128,128]{2,1,0:T(8,128)(2,1)}, bf16[4,128,128]{2,1,0:T(8,128)(2,1)}, u32[]{:S(2)}, u32[]{:S(2)}) collective-permute-start(bf16[4,128,128]{2,1,0:T(8,128)(2,1)} %get-tuple-element.56), channel_id=1, source_target_pairs={{0,16},{8,24},{16,0},{24,8},{1,17},{9,25},{17,1},{25,9},{2,18},{10... | collective-permute-start | bytes 393224 | tf_op jit(solution)/shard_map/ppermute | solution.py:22
  76.6 3.0 %copy-start.6 = (f32[512,512]{1,0:T(8,128)S(1)}, f32[512,512]{1,0:T(8,128)}, u32[]{:S(2)}) copy-start(f32[512,512]{1,0:T(8,128)} %fusion.16) | copy-start | bytes 3145732
  76.7 20.4 %collective-permute-start.12 = (bf16[4,128,128]{2,1,0:T(8,128)(2,1)}, bf16[4,128,128]{2,1,0:T(8,128)(2,1)S(1)}, u32[]{:S(2)}, u32[]{:S(2)}) collective-permute-start(bf16[4,128,128]{2,1,0:T(8,128)(2,1)} %get-tuple-element.55), channel_id=1, source_target_pairs={{0,24},{8,0},{16,8},{24,16},{1,25},{9,1},{17,9},{25,17},{2,26},{10... | collective-permute-start | bytes 393224 | tf_op jit(solution)/shard_map/ppermute | solution.py:22
  97.1 7.3 %copy-start.8 = (bf16[4,128,128]{2,1,0:T(8,128)(2,1)}, bf16[4,128,128]{2,1,0:T(8,128)(2,1)S(1)}, u32[]{:S(2)}) copy-start(bf16[4,128,128]{2,1,0:T(8,128)(2,1)S(1)} %collective-permute-done.12.refs_7_) | copy-start | bytes 393220
  97.8 14.3 %all-to-all-start.1 = ((f32[32,3,512]{2,1,0:T(4,128)}), f32[32,3,512]{2,1,0:T(4,128)S(1)}, u32[]{:S(2)}, u32[]{:S(2)}) async-start(f32[32,3,512]{2,1,0:T(4,128)} %broadcast_in_dim.120), calls=%async_computation.1 | async-start | bytes 524288 | tf_op jit(solution)/shard_map/all_to_all | solution.py:17
  112.1 4.1 %copy-start.2 = (bf16[2304,512]{1,0:T(8,128)(2,1)S(1)}, bf16[2304,512]{1,0:T(8,128)(2,1)}, u32[]{:S(2)}) copy-start(bf16[2304,512]{1,0:T(8,128)(2,1)} %get-tuple-element.31) | copy-start | bytes 7077892
  118.4 4.9 %collective-permute-start.17 = (f32[4,4,16,2304]{3,2,1,0:T(8,128)}, f32[4,4,16,2304]{3,2,1,0:T(8,128)}, u32[]{:S(2)}, u32[]{:S(2)}) collective-permute-start(f32[4,4,16,2304]{3,2,1,0:T(8,128)} %fusion), channel_id=1, source_target_pairs={{0,1},{1,0},{2,3},{3,2},{4,5},{5,4},{6,7},{7,6},{8,9},{9,8},{10,11... | collective-permute-start | bytes 7077896 | tf_op jit(solution)/shard_map/ppermute | solution.py:65
  129.1 30.3 %collective-permute-start.18 = (f32[4,16,2304]{2,1,0:T(8,128)}, f32[4,16,2304]{2,1,0:T(8,128)}, u32[]{:S(2)}, u32[]{:S(2)}) collective-permute-start(f32[4,16,2304]{2,1,0:T(8,128)} %get-tuple-element.44), channel_id=1, source_target_pairs={{0,2},{1,3},{2,0},{3,1},{4,6},{5,7},{6,4},{7,5},{8,10},{9,11},{10,... | collective-permute-start | bytes 1769480 | tf_op jit(solution)/shard_map/ppermute | solution.py:70
  129.6 31.1 %collective-permute-start.19 = (f32[4,16,2304]{2,1,0:T(8,128)}, f32[4,16,2304]{2,1,0:T(8,128)}, u32[]{:S(2)}, u32[]{:S(2)}) collective-permute-start(f32[4,16,2304]{2,1,0:T(8,128)} %get-tuple-element.46), channel_id=1, source_target_pairs={{0,4},{1,5},{2,6},{3,7},{4,0},{5,1},{6,2},{7,3},{8,12},{9,13},{10,... | collective-permute-start | bytes 1769480 | tf_op jit(solution)/shard_map/ppermute | solution.py:70
  130.9 29.8 %collective-permute-start.20 = (f32[4,16,2304]{2,1,0:T(8,128)S(1)}, f32[4,16,2304]{2,1,0:T(8,128)}, u32[]{:S(2)}, u32[]{:S(2)}) collective-permute-start(f32[4,16,2304]{2,1,0:T(8,128)S(1)} %get-tuple-element.45), channel_id=1, source_target_pairs={{0,6},{1,7},{2,4},{3,5},{4,2},{5,3},{6,0},{7,1},{8,14},{9,15},{10,... | collective-permute-start | bytes 1769480 | tf_op jit(solution)/shard_map/ppermute | solution.py:70
  132.6 25.5 %collective-permute-start.15 = (bf16[512,512]{1,0:T(8,128)(2,1)}, bf16[512,512]{1,0:T(8,128)(2,1)}, u32[]{:S(2)}, u32[]{:S(2)}) collective-permute-start(bf16[512,512]{1,0:T(8,128)(2,1)} %fusion.10), channel_id=1, source_target_pairs={{0,16},{8,24},{16,0},{24,8},{1,17},{9,25},{17,1},{25,9},{2,18},{10... | collective-permute-start | bytes 1572872 | tf_op jit(solution)/shard_map/ppermute | solution.py:22
  134.5 41.6 %collective-permute-start.13 = (bf16[512,512]{1,0:T(8,128)(2,1)}, bf16[512,512]{1,0:T(8,128)(2,1)}, u32[]{:S(2)}, u32[]{:S(2)}) collective-permute-start(bf16[512,512]{1,0:T(8,128)(2,1)} %fusion.10), channel_id=1, source_target_pairs={{8,0},{16,8},{24,16},{9,1},{17,9},{25,17},{10,2},{18,10},{26,18},{... | collective-permute-start | bytes 1572872 | tf_op jit(solution)/shard_map/ppermute | solution.py:50
  158.1 18.1 %collective-permute-start.14 = (bf16[512,512]{1,0:T(8,128)(2,1)}, bf16[512,512]{1,0:T(8,128)(2,1)}, u32[]{:S(2)}, u32[]{:S(2)}) collective-permute-start(bf16[512,512]{1,0:T(8,128)(2,1)} %fusion.10), channel_id=1, source_target_pairs={{0,8},{8,16},{16,24},{1,9},{9,17},{17,25},{2,10},{10,18},{18,26},{... | collective-permute-start | bytes 1572872 | tf_op jit(solution)/shard_map/ppermute | solution.py:49
  159.4 33.2 %collective-permute-start.16 = (bf16[512,512]{1,0:T(8,128)(2,1)}, bf16[512,512]{1,0:T(8,128)(2,1)}, u32[]{:S(2)}, u32[]{:S(2)}) collective-permute-start(bf16[512,512]{1,0:T(8,128)(2,1)} %collective-permute-done.15), channel_id=1, source_target_pairs={{8,0},{16,24},{9,1},{17,25},{10,2},{18,26},{11,3},{19,27},{12,4},{... | collective-permute-start | bytes 1572872 | tf_op jit(solution)/shard_map/ppermute | solution.py:51
  163.3 32.2 %all-to-all-start.2 = ((f32[4,16,2304]{2,1,0:T(8,128)}), f32[4,16,2304]{2,1,0:T(8,128)S(1)}, u32[]{:S(2)}, u32[]{:S(2)}) async-start(f32[4,16,2304]{2,1,0:T(8,128)} %fusion.19), calls=%async_computation.2 | async-start | bytes 1179648 | tf_op jit(solution)/shard_map/all_to_all | solution.py:324
  (4 other events, 4.2 us)

commit v5 on v4

--- a/solution.py
+++ b/solution.py
@@ -37,7 +37,10 @@
     other = lax.ppermute(like, axis, [(i, i ^ 1) for i in range(size)])
     both = jnp.stack([like, other], axis=1).reshape((size,) + value.shape)
     order = jnp.bitwise_xor(jnp.arange(size, dtype=jnp.int32), index)
-    return jnp.take(both, order, axis=0, mode="clip")
+    planes = value.shape[0]
+    order = order[None, :] * planes + jnp.arange(planes, dtype=jnp.int32)[:, None]
+    both = both.reshape((size * planes,) + value.shape[1:])
+    return jnp.take(both, order.reshape(-1), axis=0, mode="clip")
 
 
 def spread(value, axis):
@@ -59,16 +62,31 @@
     ]
 
 
-def direct_sum(part, axis):
+def direct_sum(gradient, head, axis):
     size = lax.axis_size(axis)
     index = lax.axis_index(axis)
-    far = lax.ppermute(part(1 - index % 2), axis, [(i, i ^ 1) for i in range(size)])
-    value = part(index % 2) + far
-    total = lax.dynamic_index_in_dim(value, index // 2, 0, keepdims=False)
-    for step in range(1, size // 2):
-        send = lax.dynamic_index_in_dim(value, (index // 2) ^ step, 0, keepdims=False)
-        send = lax.ppermute(send, axis, [(i, i ^ (2 * step)) for i in range(size)])
-        total = total + send
+    planes, _, rows, part_cols = gradient.shape
+    pairs = gradient.reshape(planes, size // 2, 2, rows, part_cols).transpose(2, 1, 0, 3, 4)
+
+    def product(part):
+        out = lax.dot_general(
+            part.reshape(-1, part_cols), head, (((1,), (1,)), ((), ())),
+            preferred_element_type=jnp.float32,
+        )
+        return out.reshape(part.shape[:-1] + (head.shape[0],))
+
+    away = product(lax.dynamic_index_in_dim(pairs, 1 - index % 2, 0, keepdims=False))
+    near = lax.ppermute(away, axis, [(i, i ^ 1) for i in range(size)])
+    own = lax.dynamic_index_in_dim(pairs, index % 2, 0, keepdims=False)
+
+    def chip(place):
+        part = product(lax.dynamic_index_in_dim(own, place, 0, keepdims=False))
+        return part + lax.dynamic_index_in_dim(near, place, 0, keepdims=False)
+
+    sends = [chip((index // 2) ^ step) for step in range(1, size // 2)]
+    total = chip(index // 2)
+    for step, send in enumerate(sends, 1):
+        total = total + lax.ppermute(send, axis, [(i, i ^ (2 * step)) for i in range(size)])
     return total
 
 
@@ -185,7 +203,6 @@
 
 def place_kernel(planes, origin_ref, *refs):
     heads, kepts, (head_ref, kept_ref) = refs[:planes], refs[planes : 2 * planes], refs[2 * planes :]
-    shards, _, rows, _ = kept_ref.shape
     for distance in range(planes):
         origin = origin_ref[distance]
         slab, _ = heads[distance].shape
@@ -193,22 +210,19 @@
         blocks, lanes, _ = kepts[distance].shape
         for block in range(blocks):
             tile = kepts[distance][block].astype(jnp.float32).T
-            for shard in range(shards):
-                kept_ref[shard, pl.ds(origin, 1), :, block * lanes : (block + 1) * lanes] = tile[
-                    None, shard * rows : (shard + 1) * rows
-                ]
-
-
-def place(origins, heads, kepts, shards):
+            columns = slice(block * lanes, (block + 1) * lanes)
+            kept_ref[pl.ds(origin, 1), :, columns] = tile[None]
+
+
+def place(origins, heads, kepts):
     planes = len(heads)
     slab, part_cols = heads[0].shape
-    rows = kepts[0].shape[2] // shards
     vmem = pl.BlockSpec(memory_space=pltpu.VMEM)
     return pl.pallas_call(
         functools.partial(place_kernel, planes),
         out_shape=(
             jax.ShapeDtypeStruct((planes * slab, part_cols), heads[0].dtype),
-            jax.ShapeDtypeStruct((shards, planes, rows, part_cols), jnp.float32),
+            jax.ShapeDtypeStruct((planes, kepts[0].shape[2], part_cols), jnp.float32),
         ),
         in_specs=[pl.BlockSpec(memory_space=pltpu.SMEM)] + [vmem] * (2 * planes),
         out_specs=[vmem] * 2,
@@ -292,14 +306,13 @@
     masked = jnp.where(valid_cols, scores, -jnp.inf)
     local_top = jnp.max(masked, axis=1)
     weight = jnp.where(valid_cols, jnp.exp(masked - local_top[:, None]), 0.0)
-    mass = jnp.where(
-        jnp.arange(planes, dtype=jnp.int32)[None, :, None] == plane,
-        mass_part.reshape(shard_count, 1, slice_rows), 0.0,
-    ).reshape(tokens)
+    mass = lax.dynamic_update_slice_in_dim(
+        jnp.zeros((tokens,), jnp.float32), mass_part, plane * tok_rows, 0
+    )
     student = jnp.stack([local_top, jnp.sum(weight, axis=1), mass])
     pieces, kept, student = lax.optimization_barrier((pieces, kept, student))
     origins = jnp.stack([above("dp", -distance) for distance in range(planes)])
-    head, kept = place(origins, pieces, kept, shard_count)
+    head, kept = place(origins, pieces, kept)
     kept = kept.reshape(tokens, part_cols)
     student = exchange(student, ("dp", "vocab")).reshape(planes * shard_count, 3, tokens)
     student_top = jnp.max(student[:, 0], axis=0)
@@ -310,17 +323,9 @@
 
     gradients = [(plane, gradient)] + spread(gradient, "dp")
 
-    by_pair = gradient.reshape(shard_count // 2, 2, planes * slice_rows, part_cols)
-
-    def part(last_bit):
-        rows = lax.dynamic_index_in_dim(by_pair, last_bit, 1, keepdims=False)
-        product = lax.dot_general(
-            rows.reshape(-1, part_cols), head, (((1,), (1,)), ((), ())),
-            preferred_element_type=jnp.float32,
-        )
-        return product.reshape(shard_count // 2, planes, slice_rows, width)
-
-    sums = direct_sum(part, "vocab")
+    sums = direct_sum(
+        gradient.reshape(planes, shard_count, slice_rows, part_cols), head, "vocab"
+    )
     sums = lax.all_to_all(sums, "dp", split_axis=0, concat_axis=0, tiled=True)
     hidden_grad = jnp.sum(sums, axis=0).astype(jnp.bfloat16)
 

time: 197 us -> 195 us (0.990)
  matrix products: 23.3 us -> 29.2 us
  waiting for transfers between devices: 70.1 us -> 65.1 us
  local copies, waits for them, and re-layouts: 20.7 us -> 17.1 us
    dot_general x2 -> x5, matrix products: 5.43 us -> 12.3 us  [product(): lax.dot_general(part.reshape(-1, part_cols), head, (((1,), (1,)), ((), ()...]
    ppermute x10, waiting for transfers between devices: 32.4 us -> 27.6 us  [shift(): lax.ppermute(value, axis, [(p, (p + distance) % size) for p in range(size)])]
    another operation x2, other arithmetic: 5.06 us -> 2.83 us  [chip_gather(): both = jnp.stack([like, other], axis=1).reshape((size,) + value.shape)]
    unnamed x24 -> x22, local copies, waits for them, and re-layouts: 4.18 us -> 2.09 us
  transfers between devices with their start and end apart: 24 -> 24, of which waited for: 9 -> 8; matrix products, arithmetic and copies ran while one was open for 24% -> 26% of each run, Pallas kernels for 8% -> 9%
where the time goes in v5:
time: 195 us; the launch traced here: 194 us
  waiting for transfers between devices  65.1 us (33%)
  starting transfers between devices  47.4 us (24%)
  matrix products  29.2 us (15%)
  other arithmetic  17.2 us (9%)
  local copies, waits for them, and re-layouts  17.1 us (9%)
  Pallas kernels  16.6 us (9%)
    ppermute x10, waiting for transfers between devices, shift(): lax.ppermute(value, axis, [(p, (p + distance) % size) for p in range(size)])  27.6 us
    ppermute x3, waiting for transfers between devices, chip_gather(): lax.ppermute(value, axis, [(i, i ^ 2 * step) for i in range(size)])  18.1 us
    ppermute x10, starting transfers between devices, shift(): lax.ppermute(value, axis, [(p, (p + distance) % size) for p in range(size)])  14.9 us
    dot_general x5, matrix products, product(): lax.dot_general(part.reshape(-1, part_cols), head, (((1,), (1,)), ((), ()...  12.3 us
    dot_general x4, matrix products, shards(): lax.dot_general(own_hidden, columns_part, (((0,), (0,)), ((), ())), prefe...  11.1 us
    ppermute x1, waiting for transfers between devices, spread(): relay = lax.ppermute(middle, axis, [(1, 0), (2, 3)])  10.6 us
    pallas_call x1, Pallas kernels, pick(): pl.pallas_call(functools.partial(pick_kernel, capacity), out_shape=jax.Sh...  9.16 us
    all_to_all x1, starting transfers between devices, shards(): sums = lax.all_to_all(sums, 'dp', split_axis=0, concat_axis=0, tiled=True)  8.65 us
  transfers between devices with their start and end apart: 24, of which 8 were waited for; matrix products, arithmetic and copies ran while one was open for 26% of the time, Pallas kernels for 9%

profile of v5, /device:TPU:24, one launch (start us, length us, event | category | flops | bytes accessed | tf_op | source)
XLA Modules:
  0.0 193.5 jit_solution(8786420739638388095)
XLA Ops:
  2.3 1.9 collective-permute-start.1
  11.0 9.2 %shard_map.77 = bf16[8,5,128,128]{3,2,1,0:T(8,128)(2,1)} custom-call(s32[4096]{0:T(1024)} %clamp_bitcast_fusion.ids_ref, s32[32]{0:T(128)} %get-tuple-element.36.count_ref, bf16[8000,128]{1,0:T(8,128)(2,1)} %bitcast.138), custom_call_target="tpu_custom_call" | custom-call | tf_op jit(solution)/shard_map/pallas_call | solution.py:148
  20.2 4.3 %all-to-all-start = ((bf16[8,5,128,128]{3,2,1,0:T(8,128)(2,1)}), bf16[8,5,128,128]{3,2,1,0:T(8,128)(2,1)}, u32[]{:S(2)}, u32[]{:S(2)}) async-start(bf16[8,5,128,128]{3,2,1,0:T(8,128)(2,1)} %shard_map.77), calls=%async_computation | async-start | bytes 2621440 | tf_op jit(solution)/shard_map/all_to_all | solution.py:287
  25.9 3.4 %collective-permute-start.7 = (bf16[576,512]{1,0:T(8,128)(2,1)}, bf16[576,512]{1,0:T(8,128)(2,1)}, u32[]{:S(2)}, u32[]{:S(2)}) collective-permute-start(bf16[576,512]{1,0:T(8,128)(2,1)} %get-tuple-element.45), channel_id=1, source_target_pairs={{0,8},{8,16},{16,24},{24,0},{1,9},{9,17},{17,25},{25,1},{2,10},{10... | collective-permute-start | bytes 1769480 | tf_op jit(solution)/shard_map/ppermute | solution.py:22
  30.9 1.9 collective-permute-start.3
  34.6 14.0 %collective-permute-done.3 = bf16[4,16,2304]{2,1,0:T(8,128)(2,1)S(1)} collective-permute-done((bf16[4,16,2304]{2,1,0:T(8,128)(2,1)S(1)}, bf16[4,16,2304]{2,1,0:T(8,128)(2,1)S(1)}, u32[]{:S(2)}, u32[]{:S(2)}) %collective-permute-start.3) | collective-permute-done | bytes 294944 | tf_op jit(solution)/shard_map/ppermute | solution.py:35
  48.6 2.6 %collective-permute-start.8 = (bf16[576,512]{1,0:T(8,128)(2,1)}, bf16[576,512]{1,0:T(8,128)(2,1)}, u32[]{:S(2)}, u32[]{:S(2)}) collective-permute-start(bf16[576,512]{1,0:T(8,128)(2,1)} %get-tuple-element.47), channel_id=1, source_target_pairs={{0,16},{8,24},{16,0},{24,8},{1,17},{9,25},{17,1},{25,9},{2,18},{10... | collective-permute-start | bytes 1769480 | tf_op jit(solution)/shard_map/ppermute | solution.py:22
  51.2 4.1 %collective-permute-done.5 = bf16[4,16,2304]{2,1,0:T(8,128)(2,1)S(1)} collective-permute-done((bf16[4,16,2304]{2,1,0:T(8,128)(2,1)S(1)}, bf16[4,16,2304]{2,1,0:T(8,128)(2,1)S(1)}, u32[]{:S(2)}, u32[]{:S(2)}) %collective-permute-start.5) | collective-permute-done | bytes 294944 | tf_op jit(solution)/shard_map/ppermute | solution.py:35
  63.8 2.4 %gather_fusion.2 = bf16[32,16,2304]{2,1,0:T(8,128)(2,1)S(1)} fusion(bf16[32,16,2304]{2,1,0:T(8,128)(2,1)} %bitcast.137, s32[1024]{0:T(1024)S(1)} %pad_clamp_fusion.1), kind=kCustom, calls=%fused_computation.2 | custom fusion | bytes 4718720 | tf_op jit(solution)/shard_map/jit(_take)/gather | solution.py:43
  66.2 3.6 %shard_map.78 = (bf16[16,128,128]{2,1,0:T(8,128)(2,1)}, f32[1,128]{1,0:T(1,128)}) custom-call(s32[16]{0:T(128)} %multiply_add_fusion.anchor_ref, s32[16]{0:T(128)} %gather_fusion.3, bf16[40,128,128]{2,1,0:T(8,128)(2,1)} %bitcast.21.arrived_ref), custom_call_target="tpu_custom_call" | custom-call | tf_op jit(solution)/shard_map/pallas_call | solution.py:189
  71.7 3.4 %collective-permute-start.10 = (bf16[4,128,128]{2,1,0:T(8,128)(2,1)S(1)}, bf16[4,128,128]{2,1,0:T(8,128)(2,1)}, u32[]{:S(2)}, u32[]{:S(2)}) collective-permute-start(bf16[4,128,128]{2,1,0:T(8,128)(2,1)S(1)} %get-tuple-element.52), channel_id=1, source_target_pairs={{0,8},{8,16},{16,24},{24,0},{1,9},{9,17},{17,25},{25,1},{2,10},{10... | collective-permute-start | bytes 393224 | tf_op jit(solution)/shard_map/ppermute | solution.py:22
  80.4 7.0 %collective-permute-done.8.refs_2_ = bf16[576,512]{1,0:T(8,128)(2,1)} collective-permute-done((bf16[576,512]{1,0:T(8,128)(2,1)}, bf16[576,512]{1,0:T(8,128)(2,1)}, u32[]{:S(2)}, u32[]{:S(2)}) %collective-permute-start.8) | collective-permute-done | bytes 589856 | tf_op jit(solution)/shard_map/ppermute | solution.py:22
  90.6 2.4 %collective-permute-done.11.refs_6_ = bf16[4,128,128]{2,1,0:T(8,128)(2,1)} collective-permute-done((bf16[4,128,128]{2,1,0:T(8,128)(2,1)S(1)}, bf16[4,128,128]{2,1,0:T(8,128)(2,1)}, u32[]{:S(2)}, u32[]{:S(2)}) %collective-permute-start.11) | collective-permute-done | bytes 131104 | tf_op jit(solution)/shard_map/ppermute | solution.py:22
  93.7 6.0 %all-to-all-start.1 = ((f32[32,3,512]{2,1,0:T(4,128)}), f32[32,3,512]{2,1,0:T(4,128)S(1)}, u32[]{:S(2)}, u32[]{:S(2)}) async-start(f32[32,3,512]{2,1,0:T(4,128)} %broadcast_in_dim.99), calls=%async_computation.1 | async-start | bytes 524288 | tf_op jit(solution)/shard_map/all_to_all | solution.py:17
  100.3 3.8 %shard_map.79 = (bf16[2304,512]{1,0:T(8,128)(2,1)}, f32[4,128,512]{2,1,0:T(8,128)}) custom-call(s32[4]{0:T(128)} %pad_add_fusion.origin_ref, bf16[576,512]{1,0:T(8,128)(2,1)} %copy-done.6, bf16[576,512]{1,0:T(8,128)(2,1)} %collective-permute-done.7.refs_1_, bf16[576,512]{1,0:T(8,128)(2,1)} %collective-permute-done.8.refs_2_, ...), custom_call_target="tpu_custom_call" | custom-call | tf_op jit(solution)/shard_map/pallas_call | solution.py:221
  104.1 3.9 %all-to-all-done.1 = f32[32,3,512]{2,1,0:T(4,128)S(1)} async-done(((f32[32,3,512]{2,1,0:T(4,128)}), f32[32,3,512]{2,1,0:T(4,128)S(1)}, u32[]{:S(2)}, u32[]{:S(2)}) %all-to-all-start.1) | async-done | bytes 196640 | tf_op jit(solution)/shard_map/all_to_all | solution.py:17
  108.2 2.7 %fusion.17 = bf16[512,512]{1,0:T(8,128)(2,1)} fusion(f32[4,128,512]{2,1,0:T(8,128)} %get-tuple-element.30, f32[512,512]{1,0:T(8,128)} %copy-done.5, f32[512]{0:T(512)S(1)} %divide_multiply_fusion, f32[512]{0:T(512)S(1)} %get-tuple-element.56, pred[512]{0:T(512)(128)(4,1)S(1)} %fusion.77), kind=kLoop, calls=%fused_computation.32 | loop fusion | flops 1572864 | bytes 2626048 | tf_op jit(solution)/shard_map/convert_element_type | solution.py:322
  110.9 3.2 %fusion = f32[4,4,16,2304]{3,2,1,0:T(8,128)} fusion(bf16[2304,512]{1,0:T(8,128)(2,1)S(1)} %copy-done.2, bf16[4,4,2,16,512]{4,3,2,1,0:T(8,128)(2,1)} %bitcast.35, s32[]{:T(128)S(6)} %select_n.254), kind=kOutput, calls=%fused_computation.7 | convolution fusion | flops 603979776 | bytes 4980740 | tf_op jit(solution)/shard_map/dot_general | solution.py:72
  114.1 4.9 %collective-permute-done.17 = f32[4,4,16,2304]{3,2,1,0:T(8,128)} collective-permute-done((f32[4,4,16,2304]{3,2,1,0:T(8,128)}, f32[4,4,16,2304]{3,2,1,0:T(8,128)}, u32[]{:S(2)}, u32[]{:S(2)}) %collective-permute-start.17) | collective-permute-done | bytes 2359328 | tf_op jit(solution)/shard_map/ppermute | solution.py:79
  119.0 2.8 %bitcast_add_fusion.2 = f32[4,16,2304]{2,1,0:T(8,128)} fusion(f32[4,4,16,2304]{3,2,1,0:T(8,128)} %collective-permute-done.17, s32[]{:T(128)S(6)} %select_n.255, bf16[2304,512]{1,0:T(8,128)(2,1)S(1)} %copy-done.2, bf16[4,4,2,16,512]{4,3,2,1,0:T(8,128)(2,1)} %bitcast.35, s32[]{:T(128)S(6)} %select_n.256, s32[]{:T(128)S(6)} %select_n.253), kind=kOutput, calls=%fused_computation.43 | convolution fusion | flops 151142400 | bytes 3604492 | tf_op jit(solution)/shard_map/dot_general | solution.py:72
  122.3 1.9 bitcast_add_fusion.1
  125.5 2.8 %bitcast_add_fusion = f32[4,16,2304]{2,1,0:T(8,128)} fusion(f32[4,4,16,2304]{3,2,1,0:T(8,128)} %collective-permute-done.17, s32[]{:T(128)S(6)} %select_n.259, bf16[2304,512]{1,0:T(8,128)(2,1)S(1)} %copy-done.2, bf16[4,4,2,16,512]{4,3,2,1,0:T(8,128)(2,1)} %bitcast.35, s32[]{:T(128)S(6)} %select_n.260, s32[]{:T(128)S(6)} %select_n.253), kind=kOutput, calls=%fused_computation.41 | convolution fusion | flops 151142400 | bytes 3604492 | tf_op jit(solution)/shard_map/dot_general | solution.py:72
  130.0 2.0 %collective-permute-start.15 = (bf16[512,512]{1,0:T(8,128)(2,1)}, bf16[512,512]{1,0:T(8,128)(2,1)}, u32[]{:S(2)}, u32[]{:S(2)}) collective-permute-start(bf16[512,512]{1,0:T(8,128)(2,1)} %fusion.17), channel_id=1, source_target_pairs={{0,16},{8,24},{16,0},{24,8},{1,17},{9,25},{17,1},{25,9},{2,18},{10... | collective-permute-start | bytes 1572872 | tf_op jit(solution)/shard_map/ppermute | solution.py:22
  131.9 3.8 %collective-permute-start.13 = (bf16[512,512]{1,0:T(8,128)(2,1)}, bf16[512,512]{1,0:T(8,128)(2,1)}, u32[]{:S(2)}, u32[]{:S(2)}) collective-permute-start(bf16[512,512]{1,0:T(8,128)(2,1)} %fusion.17), channel_id=1, source_target_pairs={{8,0},{16,8},{24,16},{9,1},{17,9},{25,17},{10,2},{18,10},{26,18},{... | collective-permute-start | bytes 1572872 | tf_op jit(solution)/shard_map/ppermute | solution.py:53
  137.4 18.1 %collective-permute-done.15 = bf16[512,512]{1,0:T(8,128)(2,1)} collective-permute-done((bf16[512,512]{1,0:T(8,128)(2,1)}, bf16[512,512]{1,0:T(8,128)(2,1)}, u32[]{:S(2)}, u32[]{:S(2)}) %collective-permute-start.15) | collective-permute-done | bytes 524320 | tf_op jit(solution)/shard_map/ppermute | solution.py:22
  158.2 2.6 %fusion.27 = f32[4,16,2304]{2,1,0:T(8,128)} fusion(f32[4,16,2304]{2,1,0:T(8,128)} %collective-permute-done.20, f32[4,16,2304]{2,1,0:T(8,128)} %collective-permute-done.19, f32[4,16,2304]{2,1,0:T(8,128)} %collective-permute-done.18, f32[4,16,2304]{2,1,0:T(8,128)S(1)} %fusion.8, f32[4,4,16,2304]{3,2,1,0:T(8,128)} %collective-permute-done.17, s32[]{:T(128)S(6)} %select_n.249), kind=kLoop, calls=%fused_computation.47 | loop fusion | flops 589824 | bytes 3538948 | tf_op jit(solution)/shard_map/add | solution.py:89
  160.8 8.7 %all-to-all-start.2 = ((f32[4,16,2304]{2,1,0:T(8,128)}), f32[4,16,2304]{2,1,0:T(8,128)S(1)}, u32[]{:S(2)}, u32[]{:S(2)}) async-start(f32[4,16,2304]{2,1,0:T(8,128)} %fusion.27), calls=%async_computation.2 | async-start | bytes 1179648 | tf_op jit(solution)/shard_map/all_to_all | solution.py:329
  171.1 2.8 %fusion.15 = bf16[576,2048]{1,0:T(8,128)(2,1)} fusion(bf16[576,2048]{1,0:T(8,128)(2,1)} %broadcast_in_dim.56, s32[]{:T(128)S(6)} %select_n.237, bf16[512,512]{1,0:T(8,128)(2,1)} %fusion.17, bf16[512,2304]{1,0:T(8,128)(2,1)S(1)} %bitcast.133, s32[]{:T(128)S(6)} %select_n.218), kind=kOutput, calls=%fused_computation.28 | convolution fusion | flops 302284800 | bytes 1769480 | tf_op jit(solution)/shard_map/dot_general | solution.py:335
  173.9 2.8 %fusion.14 = bf16[576,2048]{1,0:T(8,128)(2,1)} fusion(bf16[576,2048]{1,0:T(8,128)(2,1)} %fusion.15, s32[]{:T(128)S(6)} %select_n.241, bf16[512,512]{1,0:T(8,128)(2,1)} %collective-permute-done.13, bf16[512,512]{1,0:T(8,128)(2,1)} %collective-permute-done.14, pred[]{:T(512)S(6)} %eq.112, bf16[512,2304]{1,0:T(8,128)(2,1)S(1)} %bitcast.134, s32[]{:T(128)S(6)} %select_n.218), kind=kOutput, calls=%fused_computation.26 | convolution fusion | flops 302546944 | bytes 2293769 | tf_op jit(solution)/shard_map/dot_general | solution.py:335
  176.7 2.8 %fusion.13 = bf16[576,2048]{1,0:T(8,128)(2,1)} fusion(bf16[576,2048]{1,0:T(8,128)(2,1)} %fusion.14, s32[]{:T(128)S(6)} %select_n.242, bf16[512,512]{1,0:T(8,128)(2,1)} %collective-permute-done.15, bf16[512,2304]{1,0:T(8,128)(2,1)S(1)} %bitcast.135, s32[]{:T(128)S(6)} %select_n.218), kind=kOutput, calls=%fused_computation.24 | convolution fusion | flops 302284800 | bytes 1769480 | tf_op jit(solution)/shard_map/dot_general | solution.py:335
  179.5 10.6 %collective-permute-done.16 = bf16[512,512]{1,0:T(8,128)(2,1)} collective-permute-done((bf16[512,512]{1,0:T(8,128)(2,1)}, bf16[512,512]{1,0:T(8,128)(2,1)}, u32[]{:S(2)}, u32[]{:S(2)}) %collective-permute-start.16) | collective-permute-done | bytes 524320 | tf_op jit(solution)/shard_map/ppermute | solution.py:54
  190.1 2.8 %fusion.12 = bf16[576,2048]{1,0:T(8,128)(2,1)} fusion(bf16[576,2048]{1,0:T(8,128)(2,1)} %fusion.13, s32[]{:T(128)S(6)} %select_n.247, bf16[512,512]{1,0:T(8,128)(2,1)} %collective-permute-done.16, bf16[512,512]{1,0:T(8,128)(2,1)} %collective-permute-done.13, pred[]{:T(512)S(6)} %or.3, bf16[512,2304]{1,0:T(8,128)(2,1)S(1)} %bitcast.136, s32[]{:T(128)S(6)} %select_n.218), kind=kOutput, calls=%fused_computation.22 | convolution fusion | flops 302546944 | bytes 2293769 | tf_op jit(solution)/shard_map/dot_general | solution.py:335
  (102 shorter events, 43.7 us)
Async XLA Ops:
  2.3 27.0 %collective-permute-start = (bf16[16,2304]{1,0:T(8,128)(2,1)}, bf16[16,2304]{1,0:T(8,128)(2,1)}, u32[]{:S(2)}, u32[]{:S(2)}) collective-permute-start(bf16[16,2304]{1,0:T(8,128)(2,1)} %constant_dynamic-slice_fusion.5), channel_id=1, source_target_pairs={{0,8},{8,16},{16,24},{24,0},{1,9},{9,17},{17,25},{25,1},{2,10},{10... | collective-permute-start | bytes 221192 | tf_op jit(solution)/shard_map/ppermute | solution.py:22
  2.3 27.0 %collective-permute-start.1 = (bf16[16,2304]{1,0:T(8,128)(2,1)}, bf16[16,2304]{1,0:T(8,128)(2,1)}, u32[]{:S(2)}, u32[]{:S(2)}) collective-permute-start(bf16[16,2304]{1,0:T(8,128)(2,1)} %constant_dynamic-slice_fusion.5), channel_id=1, source_target_pairs={{0,16},{8,24},{16,0},{24,8},{1,17},{9,25},{17,1},{25,9},{2,18},{10... | collective-permute-start | bytes 221192 | tf_op jit(solution)/shard_map/ppermute | solution.py:22
  4.3 25.1 %collective-permute-start.2 = (bf16[16,2304]{1,0:T(8,128)(2,1)}, bf16[16,2304]{1,0:T(8,128)(2,1)}, u32[]{:S(2)}, u32[]{:S(2)}) collective-permute-start(bf16[16,2304]{1,0:T(8,128)(2,1)} %constant_dynamic-slice_fusion.5), channel_id=1, source_target_pairs={{0,24},{8,0},{16,8},{24,16},{1,25},{9,1},{17,9},{25,17},{2,26},{10... | collective-permute-start | bytes 221192 | tf_op jit(solution)/shard_map/ppermute | solution.py:22
  11.0 13.5 %copy-start.7 = (bf16[576,2048]{1,0:T(8,128)(2,1)S(1)}, bf16[576,2048]{1,0:T(8,128)(2,1)}, u32[]{:S(2)}) copy-start(bf16[576,2048]{1,0:T(8,128)(2,1)} %param.8) | copy-start | bytes 7077892
  20.2 46.0 %all-to-all-start = ((bf16[8,5,128,128]{3,2,1,0:T(8,128)(2,1)}), bf16[8,5,128,128]{3,2,1,0:T(8,128)(2,1)}, u32[]{:S(2)}, u32[]{:S(2)}) async-start(bf16[8,5,128,128]{3,2,1,0:T(8,128)(2,1)} %shard_map.77), calls=%async_computation | async-start | bytes 2621440 | tf_op jit(solution)/shard_map/all_to_all | solution.py:287
  24.5 10.0 %copy-start.9 = (s32[128]{0:T(128)S(1)}, s32[128]{0:T(128)}, u32[]{:S(2)}) copy-start(s32[128]{0:T(128)} %param.10) | copy-start | bytes 1540
  25.9 49.2 %copy-start.6 = (bf16[576,512]{1,0:T(8,128)(2,1)}, bf16[576,512]{1,0:T(8,128)(2,1)S(1)}, u32[]{:S(2)}) copy-start(bf16[576,512]{1,0:T(8,128)(2,1)S(1)} %get-tuple-element.22.refs_0_) | copy-start | bytes 1769476
  25.9 52.8 %collective-permute-start.7 = (bf16[576,512]{1,0:T(8,128)(2,1)}, bf16[576,512]{1,0:T(8,128)(2,1)}, u32[]{:S(2)}, u32[]{:S(2)}) collective-permute-start(bf16[576,512]{1,0:T(8,128)(2,1)} %get-tuple-element.45), channel_id=1, source_target_pairs={{0,8},{8,16},{16,24},{24,0},{1,9},{9,17},{17,25},{25,1},{2,10},{10... | collective-permute-start | bytes 1769480 | tf_op jit(solution)/shard_map/ppermute | solution.py:22
  29.2 46.4 %collective-permute-start.9 = (bf16[576,512]{1,0:T(8,128)(2,1)}, bf16[576,512]{1,0:T(8,128)(2,1)}, u32[]{:S(2)}, u32[]{:S(2)}) collective-permute-start(bf16[576,512]{1,0:T(8,128)(2,1)} %get-tuple-element.44), channel_id=1, source_target_pairs={{0,24},{8,0},{16,8},{24,16},{1,25},{9,1},{17,9},{25,17},{2,26},{10... | collective-permute-start | bytes 1769480 | tf_op jit(solution)/shard_map/ppermute | solution.py:22
  29.3 27.2 %copy-start.1 = (s32[128]{0:T(128)S(1)}, s32[128]{0:T(128)}, u32[]{:S(2)}) copy-start(s32[128]{0:T(128)} %param.11) | copy-start | bytes 1540
  30.9 17.7 %collective-permute-start.3 = (bf16[4,16,2304]{2,1,0:T(8,128)(2,1)S(1)}, bf16[4,16,2304]{2,1,0:T(8,128)(2,1)S(1)}, u32[]{:S(2)}, u32[]{:S(2)}) collective-permute-start(bf16[4,16,2304]{2,1,0:T(8,128)(2,1)S(1)} %gather_fusion.1), channel_id=1, source_target_pairs={{0,2},{1,3},{2,0},{3,1},{4,6},{5,7},{6,4},{7,5},{8,10},{9,11},{10,... | collective-permute-start | bytes 884744 | tf_op jit(solution)/shard_map/ppermute | solution.py:35
  32.8 18.3 %collective-permute-start.4 = (bf16[4,16,2304]{2,1,0:T(8,128)(2,1)S(1)}, bf16[4,16,2304]{2,1,0:T(8,128)(2,1)S(1)}, u32[]{:S(2)}, u32[]{:S(2)}) collective-permute-start(bf16[4,16,2304]{2,1,0:T(8,128)(2,1)S(1)} %gather_fusion.1), channel_id=1, source_target_pairs={{0,4},{1,5},{2,6},{3,7},{4,0},{5,1},{6,2},{7,3},{8,12},{9,13},{10,... | collective-permute-start | bytes 884744 | tf_op jit(solution)/shard_map/ppermute | solution.py:35
  34.3 20.9 %collective-permute-start.5 = (bf16[4,16,2304]{2,1,0:T(8,128)(2,1)S(1)}, bf16[4,16,2304]{2,1,0:T(8,128)(2,1)S(1)}, u32[]{:S(2)}, u32[]{:S(2)}) collective-permute-start(bf16[4,16,2304]{2,1,0:T(8,128)(2,1)S(1)} %gather_fusion.1), channel_id=1, source_target_pairs={{0,6},{1,7},{2,4},{3,5},{4,2},{5,3},{6,0},{7,1},{8,14},{9,15},{10,... | collective-permute-start | bytes 884744 | tf_op jit(solution)/shard_map/ppermute | solution.py:35
  48.6 38.8 %collective-permute-start.8 = (bf16[576,512]{1,0:T(8,128)(2,1)}, bf16[576,512]{1,0:T(8,128)(2,1)}, u32[]{:S(2)}, u32[]{:S(2)}) collective-permute-start(bf16[576,512]{1,0:T(8,128)(2,1)} %get-tuple-element.47), channel_id=1, source_target_pairs={{0,16},{8,24},{16,0},{24,8},{1,17},{9,25},{17,1},{25,9},{2,18},{10... | collective-permute-start | bytes 1769480 | tf_op jit(solution)/shard_map/ppermute | solution.py:22
  56.5 5.7 %collective-permute-start.6 = (bf16[4,4,16,2304]{3,2,1,0:T(8,128)(2,1)}, bf16[4,4,16,2304]{3,2,1,0:T(8,128)(2,1)S(1)}, u32[]{:S(2)}, u32[]{:S(2)}) collective-permute-start(bf16[4,4,16,2304]{3,2,1,0:T(8,128)(2,1)} %get-tuple-element.49), channel_id=1, source_target_pairs={{0,1},{1,0},{2,3},{3,2},{4,5},{5,4},{6,7},{7,6},{8,9},{9,8},{10,11... | collective-permute-start | bytes 3538952 | tf_op jit(solution)/shard_map/ppermute | solution.py:37
  66.2 21.2 %copy-start.3 = (bf16[32,16,2304]{2,1,0:T(8,128)(2,1)}, bf16[32,16,2304]{2,1,0:T(8,128)(2,1)S(1)}, u32[]{:S(2)}) copy-start(bf16[32,16,2304]{2,1,0:T(8,128)(2,1)S(1)} %gather_fusion.2) | copy-start | bytes 7077892
  71.7 18.9 %collective-permute-start.10 = (bf16[4,128,128]{2,1,0:T(8,128)(2,1)S(1)}, bf16[4,128,128]{2,1,0:T(8,128)(2,1)}, u32[]{:S(2)}, u32[]{:S(2)}) collective-permute-start(bf16[4,128,128]{2,1,0:T(8,128)(2,1)S(1)} %get-tuple-element.52), channel_id=1, source_target_pairs={{0,8},{8,16},{16,24},{24,0},{1,9},{9,17},{17,25},{25,1},{2,10},{10... | collective-permute-start | bytes 393224 | tf_op jit(solution)/shard_map/ppermute | solution.py:22
  75.0 17.9 %collective-permute-start.11 = (bf16[4,128,128]{2,1,0:T(8,128)(2,1)S(1)}, bf16[4,128,128]{2,1,0:T(8,128)(2,1)}, u32[]{:S(2)}, u32[]{:S(2)}) collective-permute-start(bf16[4,128,128]{2,1,0:T(8,128)(2,1)S(1)} %get-tuple-element.51), channel_id=1, source_target_pairs={{0,16},{8,24},{16,0},{24,8},{1,17},{9,25},{17,1},{25,9},{2,18},{10... | collective-permute-start | bytes 393224 | tf_op jit(solution)/shard_map/ppermute | solution.py:22
  75.7 17.3 %collective-permute-start.12 = (bf16[4,128,128]{2,1,0:T(8,128)(2,1)S(1)}, bf16[4,128,128]{2,1,0:T(8,128)(2,1)S(1)}, u32[]{:S(2)}, u32[]{:S(2)}) collective-permute-start(bf16[4,128,128]{2,1,0:T(8,128)(2,1)S(1)} %get-tuple-element.50), channel_id=1, source_target_pairs={{0,24},{8,0},{16,8},{24,16},{1,25},{9,1},{17,9},{25,17},{2,26},{10... | collective-permute-start | bytes 393224 | tf_op jit(solution)/shard_map/ppermute | solution.py:22
  80.4 10.2 %copy-start.10 = (f32[1,128]{1,0:T(1,128)S(1)}, f32[1,128]{1,0:T(1,128)}, u32[]{:S(2)}) copy-start(f32[1,128]{1,0:T(1,128)} %get-tuple-element.20) | copy-start | bytes 1540
  93.0 7.4 %copy-start.8 = (bf16[4,128,128]{2,1,0:T(8,128)(2,1)}, bf16[4,128,128]{2,1,0:T(8,128)(2,1)S(1)}, u32[]{:S(2)}) copy-start(bf16[4,128,128]{2,1,0:T(8,128)(2,1)S(1)} %collective-permute-done.12.refs_7_) | copy-start | bytes 393220
  93.7 14.3 %all-to-all-start.1 = ((f32[32,3,512]{2,1,0:T(4,128)}), f32[32,3,512]{2,1,0:T(4,128)S(1)}, u32[]{:S(2)}, u32[]{:S(2)}) async-start(f32[32,3,512]{2,1,0:T(4,128)} %broadcast_in_dim.99), calls=%async_computation.1 | async-start | bytes 524288 | tf_op jit(solution)/shard_map/all_to_all | solution.py:17
  114.1 4.9 %collective-permute-start.17 = (f32[4,4,16,2304]{3,2,1,0:T(8,128)}, f32[4,4,16,2304]{3,2,1,0:T(8,128)}, u32[]{:S(2)}, u32[]{:S(2)}) collective-permute-start(f32[4,4,16,2304]{3,2,1,0:T(8,128)} %fusion), channel_id=1, source_target_pairs={{0,1},{1,0},{2,3},{3,2},{4,5},{5,4},{6,7},{7,6},{8,9},{9,8},{10,11... | collective-permute-start | bytes 7077896 | tf_op jit(solution)/shard_map/ppermute | solution.py:79
  121.7 35.1 %collective-permute-start.18 = (f32[4,16,2304]{2,1,0:T(8,128)}, f32[4,16,2304]{2,1,0:T(8,128)}, u32[]{:S(2)}, u32[]{:S(2)}) collective-permute-start(f32[4,16,2304]{2,1,0:T(8,128)} %bitcast_add_fusion.2), channel_id=1, source_target_pairs={{0,2},{1,3},{2,0},{3,1},{4,6},{5,7},{6,4},{7,5},{8,10},{9,11},{10,... | collective-permute-start | bytes 1769480 | tf_op jit(solution)/shard_map/ppermute | solution.py:89
  124.2 33.9 %collective-permute-start.19 = (f32[4,16,2304]{2,1,0:T(8,128)S(1)}, f32[4,16,2304]{2,1,0:T(8,128)}, u32[]{:S(2)}, u32[]{:S(2)}) collective-permute-start(f32[4,16,2304]{2,1,0:T(8,128)S(1)} %bitcast_add_fusion.1), channel_id=1, source_target_pairs={{0,4},{1,5},{2,6},{3,7},{4,0},{5,1},{6,2},{7,3},{8,12},{9,13},{10,... | collective-permute-start | bytes 1769480 | tf_op jit(solution)/shard_map/ppermute | solution.py:89
  128.3 29.9 %collective-permute-start.20 = (f32[4,16,2304]{2,1,0:T(8,128)}, f32[4,16,2304]{2,1,0:T(8,128)}, u32[]{:S(2)}, u32[]{:S(2)}) collective-permute-start(f32[4,16,2304]{2,1,0:T(8,128)} %bitcast_add_fusion), channel_id=1, source_target_pairs={{0,6},{1,7},{2,4},{3,5},{4,2},{5,3},{6,0},{7,1},{8,14},{9,15},{10,... | collective-permute-start | bytes 1769480 | tf_op jit(solution)/shard_map/ppermute | solution.py:89
  130.0 25.6 %collective-permute-start.15 = (bf16[512,512]{1,0:T(8,128)(2,1)}, bf16[512,512]{1,0:T(8,128)(2,1)}, u32[]{:S(2)}, u32[]{:S(2)}) collective-permute-start(bf16[512,512]{1,0:T(8,128)(2,1)} %fusion.17), channel_id=1, source_target_pairs={{0,16},{8,24},{16,0},{24,8},{1,17},{9,25},{17,1},{25,9},{2,18},{10... | collective-permute-start | bytes 1572872 | tf_op jit(solution)/shard_map/ppermute | solution.py:22
  131.9 42.0 %collective-permute-start.13 = (bf16[512,512]{1,0:T(8,128)(2,1)}, bf16[512,512]{1,0:T(8,128)(2,1)}, u32[]{:S(2)}, u32[]{:S(2)}) collective-permute-start(bf16[512,512]{1,0:T(8,128)(2,1)} %fusion.17), channel_id=1, source_target_pairs={{8,0},{16,8},{24,16},{9,1},{17,9},{25,17},{10,2},{18,10},{26,18},{... | collective-permute-start | bytes 1572872 | tf_op jit(solution)/shard_map/ppermute | solution.py:53
  155.5 18.4 %collective-permute-start.14 = (bf16[512,512]{1,0:T(8,128)(2,1)}, bf16[512,512]{1,0:T(8,128)(2,1)}, u32[]{:S(2)}, u32[]{:S(2)}) collective-permute-start(bf16[512,512]{1,0:T(8,128)(2,1)} %fusion.17), channel_id=1, source_target_pairs={{0,8},{8,16},{16,24},{1,9},{9,17},{17,25},{2,10},{10,18},{18,26},{... | collective-permute-start | bytes 1572872 | tf_op jit(solution)/shard_map/ppermute | solution.py:52
  156.8 33.2 %collective-permute-start.16 = (bf16[512,512]{1,0:T(8,128)(2,1)}, bf16[512,512]{1,0:T(8,128)(2,1)}, u32[]{:S(2)}, u32[]{:S(2)}) collective-permute-start(bf16[512,512]{1,0:T(8,128)(2,1)} %collective-permute-done.15), channel_id=1, source_target_pairs={{8,0},{16,24},{9,1},{17,25},{10,2},{18,26},{11,3},{19,27},{12,4},{... | collective-permute-start | bytes 1572872 | tf_op jit(solution)/shard_map/ppermute | solution.py:54
  160.8 10.4 %copy-start.4 = (bf16[32,16,2304]{2,1,0:T(8,128)(2,1)S(1)}, bf16[32,16,2304]{2,1,0:T(8,128)(2,1)}, u32[]{:S(2)}) copy-start(bf16[32,16,2304]{2,1,0:T(8,128)(2,1)} %copy-done.3) | copy-start | bytes 7077892
  160.8 32.1 %all-to-all-start.2 = ((f32[4,16,2304]{2,1,0:T(8,128)}), f32[4,16,2304]{2,1,0:T(8,128)S(1)}, u32[]{:S(2)}, u32[]{:S(2)}) async-start(f32[4,16,2304]{2,1,0:T(8,128)} %fusion.27), calls=%async_computation.2 | async-start | bytes 1179648 | tf_op jit(solution)/shard_map/all_to_all | solution.py:329
  (3 other events, 8.9 us)

commit v6 on v5

--- a/solution.py
+++ b/solution.py
@@ -245,12 +245,15 @@
     tokens = planes * tok_rows
     capacity = (2 * kept_blocks + shard_count - 1) // shard_count
 
-    pieces = []
-    for distance in range(planes):
-        piece = lax.dynamic_slice_in_dim(
-            student_head, above("dp", distance) * part_cols, part_cols, 1
-        )
-        pieces.append(shift(piece, "dp", distance) if distance else piece)
+    def columns_of(head, distance):
+        return lax.dynamic_slice_in_dim(head, above("dp", distance) * part_cols, part_cols, 1)
+
+    first = columns_of(student_head, 1)
+    first, later = lax.optimization_barrier((first, student_head))
+    pieces = [columns_of(later, 0)]
+    for distance in range(1, planes):
+        piece = columns_of(later, distance) if distance > 1 else first
+        pieces.append(shift(piece, "dp", distance))
 
     hidden_slice = lax.dynamic_slice_in_dim(student_hidden, my_shard * slice_rows, slice_rows)
     hidden = [shift(hidden_slice, "dp", d) if d else hidden_slice for d in range(planes)]
@@ -296,13 +299,10 @@
         kept.append(shift(piece, "dp", distance) if distance else piece)
     valid_cols = lax.dynamic_slice_in_dim(valid, plane * part_blocks, part_blocks).reshape(1, -1)
 
-    scores = sum(
-        jnp.dot(
-            lax.dynamic_slice_in_dim(hidden, above("dp", -distance) * slab, slab, axis=1),
-            piece, preferred_element_type=jnp.float32,
-        )
-        for distance, piece in enumerate(pieces)
-    )
+    scores = 0.0
+    for distance, piece in enumerate(pieces):
+        rows = lax.dynamic_slice_in_dim(hidden, above("dp", -distance) * slab, slab, axis=1)
+        scores = scores + jnp.dot(rows, piece, preferred_element_type=jnp.float32)
     masked = jnp.where(valid_cols, scores, -jnp.inf)
     local_top = jnp.max(masked, axis=1)
     weight = jnp.where(valid_cols, jnp.exp(masked - local_top[:, None]), 0.0)
@@ -310,7 +310,7 @@
         jnp.zeros((tokens,), jnp.float32), mass_part, plane * tok_rows, 0
     )
     student = jnp.stack([local_top, jnp.sum(weight, axis=1), mass])
-    pieces, kept, student = lax.optimization_barrier((pieces, kept, student))
+    pieces, kept, _ = lax.optimization_barrier((pieces, kept, student))
     origins = jnp.stack([above("dp", -distance) for distance in range(planes)])
     head, kept = place(origins, pieces, kept)
     kept = kept.reshape(tokens, part_cols)

time: 195 us -> 203 us (1.041)
  waiting for transfers between devices: 65.1 us -> 76.3 us
  starting transfers between devices: 47.4 us -> 43 us
  local copies, waits for them, and re-layouts: 17.1 us -> 19.3 us
    ppermute x10, waiting for transfers between devices: 27.6 us -> 43.5 us  [shift(): lax.ppermute(value, axis, [(p, (p + distance) % size) for p in range(size)])]
    all_to_all x1, waiting for transfers between devices: 3.9 us -> 0.01 us  [exchange(): return lax.all_to_all(copies, axes, split_axis=0, concat_axis=0, tiled=True)]
    ppermute x10, starting transfers between devices: 14.9 us -> 12.4 us  [shift(): lax.ppermute(value, axis, [(p, (p + distance) % size) for p in range(size)])]
  transfers between devices with their start and end apart: 24 -> 24, of which waited for: 8 -> 9; matrix products, arithmetic and copies ran while one was open for 26% -> 24% of each run, Pallas kernels for 9% -> 6%
where the time goes in v6:
time: 203 us; the launch traced here: 202 us
  waiting for transfers between devices  76.3 us (38%)
  starting transfers between devices  43 us (21%)
  matrix products  29.3 us (14%)
  local copies, waits for them, and re-layouts  19.3 us (10%)
  other arithmetic  17.4 us (9%)
  Pallas kernels  15.7 us (8%)
    ppermute x10, waiting for transfers between devices, shift(): lax.ppermute(value, axis, [(p, (p + distance) % size) for p in range(size)])  43.5 us
    ppermute x3, waiting for transfers between devices, chip_gather(): lax.ppermute(value, axis, [(i, i ^ 2 * step) for i in range(size)])  17.1 us
    ppermute x10, starting transfers between devices, shift(): lax.ppermute(value, axis, [(p, (p + distance) % size) for p in range(size)])  12.4 us
    dot_general x5, matrix products, product(): lax.dot_general(part.reshape(-1, part_cols), head, (((1,), (1,)), ((), ()...  12.3 us
    dot_general x4, matrix products, shards(): lax.dot_general(own_hidden, columns_part, (((0,), (0,)), ((), ())), prefe...  11.1 us
    pallas_call x1, Pallas kernels, pick(): pl.pallas_call(functools.partial(pick_kernel, capacity), out_shape=jax.Sh...  9.16 us
    ppermute x1, waiting for transfers between devices, spread(): relay = lax.ppermute(middle, axis, [(1, 0), (2, 3)])  8.82 us
    all_to_all x1, starting transfers between devices, shards(): sums = lax.all_to_all(sums, 'dp', split_axis=0, concat_axis=0, tiled=True)  8.55 us
  transfers between devices with their start and end apart: 24, of which 9 were waited for; matrix products, arithmetic and copies ran while one was open for 24% of the time, Pallas kernels for 6%

profile of v6, /device:TPU:24, one launch (start us, length us, event | category | flops | bytes accessed | tf_op | source)
XLA Modules:
  0.0 202.0 jit_solution(10692132678865266330)
XLA Ops:
  2.3 1.9 collective-permute-start.1
  11.0 9.2 %shard_map.77 = bf16[8,5,128,128]{3,2,1,0:T(8,128)(2,1)} custom-call(s32[4096]{0:T(1024)} %clamp_bitcast_fusion.ids_ref, s32[32]{0:T(128)} %get-tuple-element.38.count_ref, bf16[8000,128]{1,0:T(8,128)(2,1)} %bitcast.138), custom_call_target="tpu_custom_call" | custom-call | tf_op jit(solution)/shard_map/pallas_call | solution.py:148
  20.2 4.3 %all-to-all-start = ((bf16[8,5,128,128]{3,2,1,0:T(8,128)(2,1)}), bf16[8,5,128,128]{3,2,1,0:T(8,128)(2,1)}, u32[]{:S(2)}, u32[]{:S(2)}) async-start(bf16[8,5,128,128]{3,2,1,0:T(8,128)(2,1)} %shard_map.77), calls=%async_computation | async-start | bytes 2621440 | tf_op jit(solution)/shard_map/all_to_all | solution.py:290
  25.3 3.4 %collective-permute-start.7 = (bf16[576,512]{1,0:T(8,128)(2,1)}, bf16[576,512]{1,0:T(8,128)(2,1)}, u32[]{:S(2)}, u32[]{:S(2)}) collective-permute-start(bf16[576,512]{1,0:T(8,128)(2,1)} %constant_dynamic-slice_fusion.4), channel_id=1, source_target_pairs={{0,8},{8,16},{16,24},{24,0},{1,9},{9,17},{17,25},{25,1},{2,10},{10... | collective-permute-start | bytes 1769480 | tf_op jit(solution)/shard_map/ppermute | solution.py:22
  31.8 1.9 collective-permute-start.3
  35.5 13.1 %collective-permute-done.3 = bf16[4,16,2304]{2,1,0:T(8,128)(2,1)S(1)} collective-permute-done((bf16[4,16,2304]{2,1,0:T(8,128)(2,1)S(1)}, bf16[4,16,2304]{2,1,0:T(8,128)(2,1)S(1)}, u32[]{:S(2)}, u32[]{:S(2)}) %collective-permute-start.3) | collective-permute-done | bytes 294944 | tf_op jit(solution)/shard_map/ppermute | solution.py:35
  48.5 2.6 %collective-permute-start.8 = (bf16[576,512]{1,0:T(8,128)(2,1)}, bf16[576,512]{1,0:T(8,128)(2,1)}, u32[]{:S(2)}, u32[]{:S(2)}) collective-permute-start(bf16[576,512]{1,0:T(8,128)(2,1)} %get-tuple-element.47), channel_id=1, source_target_pairs={{0,16},{8,24},{16,0},{24,8},{1,17},{9,25},{17,1},{25,9},{2,18},{10... | collective-permute-start | bytes 1769480 | tf_op jit(solution)/shard_map/ppermute | solution.py:22
  51.1 4.1 %collective-permute-done.5 = bf16[4,16,2304]{2,1,0:T(8,128)(2,1)S(1)} collective-permute-done((bf16[4,16,2304]{2,1,0:T(8,128)(2,1)S(1)}, bf16[4,16,2304]{2,1,0:T(8,128)(2,1)S(1)}, u32[]{:S(2)}, u32[]{:S(2)}) %collective-permute-start.5) | collective-permute-done | bytes 294944 | tf_op jit(solution)/shard_map/ppermute | solution.py:35
  63.8 2.4 %gather_fusion.2 = bf16[32,16,2304]{2,1,0:T(8,128)(2,1)S(1)} fusion(bf16[32,16,2304]{2,1,0:T(8,128)(2,1)} %bitcast.137, s32[1024]{0:T(1024)S(1)} %pad_clamp_fusion.1), kind=kCustom, calls=%fused_computation.2 | custom fusion | bytes 4718720 | tf_op jit(solution)/shard_map/jit(_take)/gather | solution.py:43
  66.8 1.8 fusion.19
  70.4 10.8 %collective-permute-done.8.refs_2_ = bf16[576,512]{1,0:T(8,128)(2,1)} collective-permute-done((bf16[576,512]{1,0:T(8,128)(2,1)}, bf16[576,512]{1,0:T(8,128)(2,1)}, u32[]{:S(2)}, u32[]{:S(2)}) %collective-permute-start.8) | collective-permute-done | bytes 589856 | tf_op jit(solution)/shard_map/ppermute | solution.py:22
  84.3 2.8 %shard_map.78 = (bf16[16,128,128]{2,1,0:T(8,128)(2,1)}, f32[1,128]{1,0:T(1,128)}) custom-call(s32[16]{0:T(128)} %multiply_add_fusion.anchor_ref, s32[16]{0:T(128)} %gather_fusion.3, bf16[40,128,128]{2,1,0:T(8,128)(2,1)} %bitcast.23.arrived_ref), custom_call_target="tpu_custom_call" | custom-call | tf_op jit(solution)/shard_map/pallas_call | solution.py:189
  88.5 6.0 %all-to-all-start.1 = ((f32[32,3,512]{2,1,0:T(4,128)}), f32[32,3,512]{2,1,0:T(4,128)S(1)}, u32[]{:S(2)}, u32[]{:S(2)}) async-start(f32[32,3,512]{2,1,0:T(4,128)} %broadcast_in_dim.99), calls=%async_computation.1 | async-start | bytes 524288 | tf_op jit(solution)/shard_map/all_to_all | solution.py:17
  99.5 3.6 %collective-permute-done.10.refs_5_ = bf16[4,128,128]{2,1,0:T(8,128)(2,1)S(1)} collective-permute-done((bf16[4,128,128]{2,1,0:T(8,128)(2,1)S(1)}, bf16[4,128,128]{2,1,0:T(8,128)(2,1)S(1)}, u32[]{:S(2)}, u32[]{:S(2)}) %collective-permute-start.10) | collective-permute-done | bytes 131104 | tf_op jit(solution)/shard_map/ppermute | solution.py:22
  103.1 9.7 %collective-permute-done.11.refs_6_ = bf16[4,128,128]{2,1,0:T(8,128)(2,1)S(1)} collective-permute-done((bf16[4,128,128]{2,1,0:T(8,128)(2,1)S(1)}, bf16[4,128,128]{2,1,0:T(8,128)(2,1)S(1)}, u32[]{:S(2)}, u32[]{:S(2)}) %collective-permute-start.11) | collective-permute-done | bytes 131104 | tf_op jit(solution)/shard_map/ppermute | solution.py:22
  113.6 3.8 %shard_map.79 = (bf16[2304,512]{1,0:T(8,128)(2,1)}, f32[4,128,512]{2,1,0:T(8,128)}) custom-call(s32[4]{0:T(128)} %pad_add_fusion.origin_ref, bf16[576,512]{1,0:T(8,128)(2,1)} %copy-done.6, bf16[576,512]{1,0:T(8,128)(2,1)} %collective-permute-done.7.refs_1_, bf16[576,512]{1,0:T(8,128)(2,1)} %collective-permute-done.8.refs_2_, ...), custom_call_target="tpu_custom_call" | custom-call | tf_op jit(solution)/shard_map/pallas_call | solution.py:221
  117.6 2.8 %fusion.17 = bf16[512,512]{1,0:T(8,128)(2,1)} fusion(f32[4,128,512]{2,1,0:T(8,128)} %get-tuple-element.32, f32[512,512]{1,0:T(8,128)} %copy-done.5, f32[512]{0:T(512)S(1)} %divide_multiply_fusion, f32[512]{0:T(512)S(1)} %get-tuple-element.57, pred[512]{0:T(512)(128)(4,1)S(1)} %fusion.77), kind=kLoop, calls=%fused_computation.32 | loop fusion | flops 1572864 | bytes 2626048 | tf_op jit(solution)/shard_map/convert_element_type | solution.py:322
  120.3 3.2 %fusion = f32[4,4,16,2304]{3,2,1,0:T(8,128)} fusion(bf16[2304,512]{1,0:T(8,128)(2,1)S(1)} %copy-done.2, bf16[4,4,2,16,512]{4,3,2,1,0:T(8,128)(2,1)} %bitcast.35, s32[]{:T(128)S(6)} %select_n.254), kind=kOutput, calls=%fused_computation.7 | convolution fusion | flops 603979776 | bytes 4980740 | tf_op jit(solution)/shard_map/dot_general | solution.py:72
  123.5 4.9 %collective-permute-done.17 = f32[4,4,16,2304]{3,2,1,0:T(8,128)} collective-permute-done((f32[4,4,16,2304]{3,2,1,0:T(8,128)}, f32[4,4,16,2304]{3,2,1,0:T(8,128)}, u32[]{:S(2)}, u32[]{:S(2)}) %collective-permute-start.17) | collective-permute-done | bytes 2359328 | tf_op jit(solution)/shard_map/ppermute | solution.py:79
  128.4 2.8 %bitcast_add_fusion.2 = f32[4,16,2304]{2,1,0:T(8,128)} fusion(f32[4,4,16,2304]{3,2,1,0:T(8,128)} %collective-permute-done.17, s32[]{:T(128)S(6)} %select_n.255, bf16[2304,512]{1,0:T(8,128)(2,1)S(1)} %copy-done.2, bf16[4,4,2,16,512]{4,3,2,1,0:T(8,128)(2,1)} %bitcast.35, s32[]{:T(128)S(6)} %select_n.256, s32[]{:T(128)S(6)} %select_n.253), kind=kOutput, calls=%fused_computation.43 | convolution fusion | flops 151142400 | bytes 3604492 | tf_op jit(solution)/shard_map/dot_general | solution.py:72
  132.7 1.9 bitcast_add_fusion.1
  136.2 2.8 %bitcast_add_fusion = f32[4,16,2304]{2,1,0:T(8,128)} fusion(f32[4,4,16,2304]{3,2,1,0:T(8,128)} %collective-permute-done.17, s32[]{:T(128)S(6)} %select_n.259, bf16[2304,512]{1,0:T(8,128)(2,1)S(1)} %copy-done.2, bf16[4,4,2,16,512]{4,3,2,1,0:T(8,128)(2,1)} %bitcast.35, s32[]{:T(128)S(6)} %select_n.260, s32[]{:T(128)S(6)} %select_n.253), kind=kOutput, calls=%fused_computation.41 | convolution fusion | flops 151142400 | bytes 3604492 | tf_op jit(solution)/shard_map/dot_general | solution.py:72
  140.9 2.2 %collective-permute-start.13 = (bf16[512,512]{1,0:T(8,128)(2,1)}, bf16[512,512]{1,0:T(8,128)(2,1)}, u32[]{:S(2)}, u32[]{:S(2)}) collective-permute-start(bf16[512,512]{1,0:T(8,128)(2,1)} %fusion.17), channel_id=1, source_target_pairs={{8,0},{16,8},{24,16},{9,1},{17,9},{25,17},{10,2},{18,10},{26,18},{... | collective-permute-start | bytes 1572872 | tf_op jit(solution)/shard_map/ppermute | solution.py:53
  144.7 19.3 %collective-permute-done.15 = bf16[512,512]{1,0:T(8,128)(2,1)} collective-permute-done((bf16[512,512]{1,0:T(8,128)(2,1)}, bf16[512,512]{1,0:T(8,128)(2,1)}, u32[]{:S(2)}, u32[]{:S(2)}) %collective-permute-start.15) | collective-permute-done | bytes 524320 | tf_op jit(solution)/shard_map/ppermute | solution.py:22
  166.6 2.6 %fusion.27 = f32[4,16,2304]{2,1,0:T(8,128)} fusion(f32[4,16,2304]{2,1,0:T(8,128)} %collective-permute-done.20, f32[4,16,2304]{2,1,0:T(8,128)} %collective-permute-done.19, f32[4,16,2304]{2,1,0:T(8,128)} %collective-permute-done.18, f32[4,16,2304]{2,1,0:T(8,128)S(1)} %fusion.8, f32[4,4,16,2304]{3,2,1,0:T(8,128)} %collective-permute-done.17, s32[]{:T(128)S(6)} %select_n.249), kind=kLoop, calls=%fused_computation.47 | loop fusion | flops 589824 | bytes 3538948 | tf_op jit(solution)/shard_map/add | solution.py:89
  169.3 8.6 %all-to-all-start.2 = ((f32[4,16,2304]{2,1,0:T(8,128)}), f32[4,16,2304]{2,1,0:T(8,128)S(1)}, u32[]{:S(2)}, u32[]{:S(2)}) async-start(f32[4,16,2304]{2,1,0:T(8,128)} %fusion.27), calls=%async_computation.2 | async-start | bytes 1179648 | tf_op jit(solution)/shard_map/all_to_all | solution.py:329
  179.5 2.8 %fusion.15 = bf16[576,2048]{1,0:T(8,128)(2,1)} fusion(bf16[576,2048]{1,0:T(8,128)(2,1)} %broadcast_in_dim.56, s32[]{:T(128)S(6)} %select_n.237, bf16[512,512]{1,0:T(8,128)(2,1)} %fusion.17, bf16[512,2304]{1,0:T(8,128)(2,1)S(1)} %bitcast.133, s32[]{:T(128)S(6)} %select_n.218), kind=kOutput, calls=%fused_computation.28 | convolution fusion | flops 302284800 | bytes 1769480 | tf_op jit(solution)/shard_map/dot_general | solution.py:335
  182.3 1.9 collective-permute-done.14
  184.2 2.8 %fusion.14 = bf16[576,2048]{1,0:T(8,128)(2,1)} fusion(bf16[576,2048]{1,0:T(8,128)(2,1)} %fusion.15, s32[]{:T(128)S(6)} %select_n.241, bf16[512,512]{1,0:T(8,128)(2,1)} %collective-permute-done.13, bf16[512,512]{1,0:T(8,128)(2,1)} %collective-permute-done.14, pred[]{:T(512)S(6)} %eq.112, bf16[512,2304]{1,0:T(8,128)(2,1)S(1)} %bitcast.134, s32[]{:T(128)S(6)} %select_n.218), kind=kOutput, calls=%fused_computation.26 | convolution fusion | flops 302546944 | bytes 2293769 | tf_op jit(solution)/shard_map/dot_general | solution.py:335
  187.0 2.8 %fusion.13 = bf16[576,2048]{1,0:T(8,128)(2,1)} fusion(bf16[576,2048]{1,0:T(8,128)(2,1)} %fusion.14, s32[]{:T(128)S(6)} %select_n.242, bf16[512,512]{1,0:T(8,128)(2,1)} %collective-permute-done.15, bf16[512,2304]{1,0:T(8,128)(2,1)S(1)} %bitcast.135, s32[]{:T(128)S(6)} %select_n.218), kind=kOutput, calls=%fused_computation.24 | convolution fusion | flops 302284800 | bytes 1769480 | tf_op jit(solution)/shard_map/dot_general | solution.py:335
  189.7 8.8 %collective-permute-done.16 = bf16[512,512]{1,0:T(8,128)(2,1)} collective-permute-done((bf16[512,512]{1,0:T(8,128)(2,1)}, bf16[512,512]{1,0:T(8,128)(2,1)}, u32[]{:S(2)}, u32[]{:S(2)}) %collective-permute-start.16) | collective-permute-done | bytes 524320 | tf_op jit(solution)/shard_map/ppermute | solution.py:54
  198.6 2.8 %fusion.12 = bf16[576,2048]{1,0:T(8,128)(2,1)} fusion(bf16[576,2048]{1,0:T(8,128)(2,1)} %fusion.13, s32[]{:T(128)S(6)} %select_n.247, bf16[512,512]{1,0:T(8,128)(2,1)} %collective-permute-done.16, bf16[512,512]{1,0:T(8,128)(2,1)} %collective-permute-done.13, pred[]{:T(512)S(6)} %or.3, bf16[512,2304]{1,0:T(8,128)(2,1)S(1)} %bitcast.136, s32[]{:T(128)S(6)} %select_n.218), kind=kOutput, calls=%fused_computation.22 | convolution fusion | flops 302546944 | bytes 2293769 | tf_op jit(solution)/shard_map/dot_general | solution.py:335
  (105 shorter events, 47.0 us)
Async XLA Ops:
  2.3 27.7 %collective-permute-start = (bf16[16,2304]{1,0:T(8,128)(2,1)}, bf16[16,2304]{1,0:T(8,128)(2,1)}, u32[]{:S(2)}, u32[]{:S(2)}) collective-permute-start(bf16[16,2304]{1,0:T(8,128)(2,1)} %constant_dynamic-slice_fusion.5), channel_id=1, source_target_pairs={{0,8},{8,16},{16,24},{24,0},{1,9},{9,17},{17,25},{25,1},{2,10},{10... | collective-permute-start | bytes 221192 | tf_op jit(solution)/shard_map/ppermute | solution.py:22
  2.3 27.7 %collective-permute-start.1 = (bf16[16,2304]{1,0:T(8,128)(2,1)}, bf16[16,2304]{1,0:T(8,128)(2,1)}, u32[]{:S(2)}, u32[]{:S(2)}) collective-permute-start(bf16[16,2304]{1,0:T(8,128)(2,1)} %constant_dynamic-slice_fusion.5), channel_id=1, source_target_pairs={{0,16},{8,24},{16,0},{24,8},{1,17},{9,25},{17,1},{25,9},{2,18},{10... | collective-permute-start | bytes 221192 | tf_op jit(solution)/shard_map/ppermute | solution.py:22
  4.3 25.8 %collective-permute-start.2 = (bf16[16,2304]{1,0:T(8,128)(2,1)}, bf16[16,2304]{1,0:T(8,128)(2,1)}, u32[]{:S(2)}, u32[]{:S(2)}) collective-permute-start(bf16[16,2304]{1,0:T(8,128)(2,1)} %constant_dynamic-slice_fusion.5), channel_id=1, source_target_pairs={{0,24},{8,0},{16,8},{24,16},{1,25},{9,1},{17,9},{25,17},{2,26},{10... | collective-permute-start | bytes 221192 | tf_op jit(solution)/shard_map/ppermute | solution.py:22
  11.0 13.4 %copy-start.7 = (bf16[576,2048]{1,0:T(8,128)(2,1)S(1)}, bf16[576,2048]{1,0:T(8,128)(2,1)}, u32[]{:S(2)}) copy-start(bf16[576,2048]{1,0:T(8,128)(2,1)} %param.8) | copy-start | bytes 7077892
  20.2 46.0 %all-to-all-start = ((bf16[8,5,128,128]{3,2,1,0:T(8,128)(2,1)}), bf16[8,5,128,128]{3,2,1,0:T(8,128)(2,1)}, u32[]{:S(2)}, u32[]{:S(2)}) async-start(bf16[8,5,128,128]{3,2,1,0:T(8,128)(2,1)} %shard_map.77), calls=%async_computation | async-start | bytes 2621440 | tf_op jit(solution)/shard_map/all_to_all | solution.py:290
  25.3 43.3 %collective-permute-start.7 = (bf16[576,512]{1,0:T(8,128)(2,1)}, bf16[576,512]{1,0:T(8,128)(2,1)}, u32[]{:S(2)}, u32[]{:S(2)}) collective-permute-start(bf16[576,512]{1,0:T(8,128)(2,1)} %constant_dynamic-slice_fusion.4), channel_id=1, source_target_pairs={{0,8},{8,16},{16,24},{24,0},{1,9},{9,17},{17,25},{25,1},{2,10},{10... | collective-permute-start | bytes 1769480 | tf_op jit(solution)/shard_map/ppermute | solution.py:22
  28.7 6.6 %copy-start.11 = (s32[128]{0:T(128)S(1)}, s32[128]{0:T(128)}, u32[]{:S(2)}) copy-start(s32[128]{0:T(128)} %param.10) | copy-start | bytes 1540
  30.0 36.2 %copy-start.6 = (bf16[576,512]{1,0:T(8,128)(2,1)}, bf16[576,512]{1,0:T(8,128)(2,1)S(1)}, u32[]{:S(2)}) copy-start(bf16[576,512]{1,0:T(8,128)(2,1)S(1)} %get-tuple-element.24.refs_0_) | copy-start | bytes 1769476
  30.0 36.8 %collective-permute-start.9 = (bf16[576,512]{1,0:T(8,128)(2,1)}, bf16[576,512]{1,0:T(8,128)(2,1)}, u32[]{:S(2)}, u32[]{:S(2)}) collective-permute-start(bf16[576,512]{1,0:T(8,128)(2,1)} %get-tuple-element.46), channel_id=1, source_target_pairs={{0,24},{8,0},{16,8},{24,16},{1,25},{9,1},{17,9},{25,17},{2,26},{10... | collective-permute-start | bytes 1769480 | tf_op jit(solution)/shard_map/ppermute | solution.py:22
  30.1 26.3 %copy-start.1 = (s32[128]{0:T(128)S(1)}, s32[128]{0:T(128)}, u32[]{:S(2)}) copy-start(s32[128]{0:T(128)} %param.11) | copy-start | bytes 1540
  31.8 16.7 %collective-permute-start.3 = (bf16[4,16,2304]{2,1,0:T(8,128)(2,1)S(1)}, bf16[4,16,2304]{2,1,0:T(8,128)(2,1)S(1)}, u32[]{:S(2)}, u32[]{:S(2)}) collective-permute-start(bf16[4,16,2304]{2,1,0:T(8,128)(2,1)S(1)} %gather_fusion.1), channel_id=1, source_target_pairs={{0,2},{1,3},{2,0},{3,1},{4,6},{5,7},{6,4},{7,5},{8,10},{9,11},{10,... | collective-permute-start | bytes 884744 | tf_op jit(solution)/shard_map/ppermute | solution.py:35
  33.7 17.4 %collective-permute-start.4 = (bf16[4,16,2304]{2,1,0:T(8,128)(2,1)S(1)}, bf16[4,16,2304]{2,1,0:T(8,128)(2,1)S(1)}, u32[]{:S(2)}, u32[]{:S(2)}) collective-permute-start(bf16[4,16,2304]{2,1,0:T(8,128)(2,1)S(1)} %gather_fusion.1), channel_id=1, source_target_pairs={{0,4},{1,5},{2,6},{3,7},{4,0},{5,1},{6,2},{7,3},{8,12},{9,13},{10,... | collective-permute-start | bytes 884744 | tf_op jit(solution)/shard_map/ppermute | solution.py:35
  35.2 20.0 %collective-permute-start.5 = (bf16[4,16,2304]{2,1,0:T(8,128)(2,1)S(1)}, bf16[4,16,2304]{2,1,0:T(8,128)(2,1)S(1)}, u32[]{:S(2)}, u32[]{:S(2)}) collective-permute-start(bf16[4,16,2304]{2,1,0:T(8,128)(2,1)S(1)} %gather_fusion.1), channel_id=1, source_target_pairs={{0,6},{1,7},{2,4},{3,5},{4,2},{5,3},{6,0},{7,1},{8,14},{9,15},{10,... | collective-permute-start | bytes 884744 | tf_op jit(solution)/shard_map/ppermute | solution.py:35
  48.5 32.6 %collective-permute-start.8 = (bf16[576,512]{1,0:T(8,128)(2,1)}, bf16[576,512]{1,0:T(8,128)(2,1)}, u32[]{:S(2)}, u32[]{:S(2)}) collective-permute-start(bf16[576,512]{1,0:T(8,128)(2,1)} %get-tuple-element.47), channel_id=1, source_target_pairs={{0,16},{8,24},{16,0},{24,8},{1,17},{9,25},{17,1},{25,9},{2,18},{10... | collective-permute-start | bytes 1769480 | tf_op jit(solution)/shard_map/ppermute | solution.py:22
  56.4 5.7 %collective-permute-start.6 = (bf16[4,4,16,2304]{3,2,1,0:T(8,128)(2,1)}, bf16[4,4,16,2304]{3,2,1,0:T(8,128)(2,1)S(1)}, u32[]{:S(2)}, u32[]{:S(2)}) collective-permute-start(bf16[4,4,16,2304]{3,2,1,0:T(8,128)(2,1)} %get-tuple-element.50), channel_id=1, source_target_pairs={{0,1},{1,0},{2,3},{3,2},{4,5},{5,4},{6,7},{7,6},{8,9},{9,8},{10,11... | collective-permute-start | bytes 3538952 | tf_op jit(solution)/shard_map/ppermute | solution.py:37
  66.2 15.0 %copy-start.3 = (bf16[32,16,2304]{2,1,0:T(8,128)(2,1)}, bf16[32,16,2304]{2,1,0:T(8,128)(2,1)S(1)}, u32[]{:S(2)}) copy-start(bf16[32,16,2304]{2,1,0:T(8,128)(2,1)S(1)} %gather_fusion.2) | copy-start | bytes 7077892
  88.5 28.8 %all-to-all-start.1 = ((f32[32,3,512]{2,1,0:T(4,128)}), f32[32,3,512]{2,1,0:T(4,128)S(1)}, u32[]{:S(2)}, u32[]{:S(2)}) async-start(f32[32,3,512]{2,1,0:T(4,128)} %broadcast_in_dim.99), calls=%async_computation.1 | async-start | bytes 524288 | tf_op jit(solution)/shard_map/all_to_all | solution.py:17
  96.3 6.8 %collective-permute-start.10 = (bf16[4,128,128]{2,1,0:T(8,128)(2,1)S(1)}, bf16[4,128,128]{2,1,0:T(8,128)(2,1)S(1)}, u32[]{:S(2)}, u32[]{:S(2)}) collective-permute-start(bf16[4,128,128]{2,1,0:T(8,128)(2,1)S(1)} %get-tuple-element.53), channel_id=1, source_target_pairs={{0,8},{8,16},{16,24},{24,0},{1,9},{9,17},{17,25},{25,1},{2,10},{10... | collective-permute-start | bytes 393224 | tf_op jit(solution)/shard_map/ppermute | solution.py:22
  96.5 16.3 %collective-permute-start.11 = (bf16[4,128,128]{2,1,0:T(8,128)(2,1)S(1)}, bf16[4,128,128]{2,1,0:T(8,128)(2,1)S(1)}, u32[]{:S(2)}, u32[]{:S(2)}) collective-permute-start(bf16[4,128,128]{2,1,0:T(8,128)(2,1)S(1)} %get-tuple-element.52), channel_id=1, source_target_pairs={{0,16},{8,24},{16,0},{24,8},{1,17},{9,25},{17,1},{25,9},{2,18},{10... | collective-permute-start | bytes 393224 | tf_op jit(solution)/shard_map/ppermute | solution.py:22
  98.3 14.5 %collective-permute-start.12 = (bf16[4,128,128]{2,1,0:T(8,128)(2,1)S(1)}, bf16[4,128,128]{2,1,0:T(8,128)(2,1)S(1)}, u32[]{:S(2)}, u32[]{:S(2)}) collective-permute-start(bf16[4,128,128]{2,1,0:T(8,128)(2,1)S(1)} %get-tuple-element.51), channel_id=1, source_target_pairs={{0,24},{8,0},{16,8},{24,16},{1,25},{9,1},{17,9},{25,17},{2,26},{10... | collective-permute-start | bytes 393224 | tf_op jit(solution)/shard_map/ppermute | solution.py:22
  103.1 9.8 %copy-start.8 = (bf16[4,128,128]{2,1,0:T(8,128)(2,1)}, bf16[4,128,128]{2,1,0:T(8,128)(2,1)S(1)}, u32[]{:S(2)}) copy-start(bf16[4,128,128]{2,1,0:T(8,128)(2,1)S(1)} %collective-permute-done.10.refs_5_) | copy-start | bytes 393220
  117.3 3.0 %copy-start.2 = (bf16[2304,512]{1,0:T(8,128)(2,1)S(1)}, bf16[2304,512]{1,0:T(8,128)(2,1)}, u32[]{:S(2)}) copy-start(bf16[2304,512]{1,0:T(8,128)(2,1)} %get-tuple-element.33) | copy-start | bytes 7077892
  123.5 4.9 %collective-permute-start.17 = (f32[4,4,16,2304]{3,2,1,0:T(8,128)}, f32[4,4,16,2304]{3,2,1,0:T(8,128)}, u32[]{:S(2)}, u32[]{:S(2)}) collective-permute-start(f32[4,4,16,2304]{3,2,1,0:T(8,128)} %fusion), channel_id=1, source_target_pairs={{0,1},{1,0},{2,3},{3,2},{4,5},{5,4},{6,7},{7,6},{8,9},{9,8},{10,11... | collective-permute-start | bytes 7077896 | tf_op jit(solution)/shard_map/ppermute | solution.py:79
  131.2 34.1 %collective-permute-start.18 = (f32[4,16,2304]{2,1,0:T(8,128)}, f32[4,16,2304]{2,1,0:T(8,128)}, u32[]{:S(2)}, u32[]{:S(2)}) collective-permute-start(f32[4,16,2304]{2,1,0:T(8,128)} %bitcast_add_fusion.2), channel_id=1, source_target_pairs={{0,2},{1,3},{2,0},{3,1},{4,6},{5,7},{6,4},{7,5},{8,10},{9,11},{10,... | collective-permute-start | bytes 1769480 | tf_op jit(solution)/shard_map/ppermute | solution.py:89
  134.7 32.0 %collective-permute-start.19 = (f32[4,16,2304]{2,1,0:T(8,128)S(1)}, f32[4,16,2304]{2,1,0:T(8,128)}, u32[]{:S(2)}, u32[]{:S(2)}) collective-permute-start(f32[4,16,2304]{2,1,0:T(8,128)S(1)} %bitcast_add_fusion.1), channel_id=1, source_target_pairs={{0,4},{1,5},{2,6},{3,7},{4,0},{5,1},{6,2},{7,3},{8,12},{9,13},{10,... | collective-permute-start | bytes 1769480 | tf_op jit(solution)/shard_map/ppermute | solution.py:89
  138.9 27.7 %collective-permute-start.20 = (f32[4,16,2304]{2,1,0:T(8,128)}, f32[4,16,2304]{2,1,0:T(8,128)}, u32[]{:S(2)}, u32[]{:S(2)}) collective-permute-start(f32[4,16,2304]{2,1,0:T(8,128)} %bitcast_add_fusion), channel_id=1, source_target_pairs={{0,6},{1,7},{2,4},{3,5},{4,2},{5,3},{6,0},{7,1},{8,14},{9,15},{10,... | collective-permute-start | bytes 1769480 | tf_op jit(solution)/shard_map/ppermute | solution.py:89
  139.4 24.6 %collective-permute-start.15 = (bf16[512,512]{1,0:T(8,128)(2,1)}, bf16[512,512]{1,0:T(8,128)(2,1)}, u32[]{:S(2)}, u32[]{:S(2)}) collective-permute-start(bf16[512,512]{1,0:T(8,128)(2,1)} %fusion.17), channel_id=1, source_target_pairs={{0,16},{8,24},{16,0},{24,8},{1,17},{9,25},{17,1},{25,9},{2,18},{10... | collective-permute-start | bytes 1572872 | tf_op jit(solution)/shard_map/ppermute | solution.py:22
  140.9 41.4 %collective-permute-start.13 = (bf16[512,512]{1,0:T(8,128)(2,1)}, bf16[512,512]{1,0:T(8,128)(2,1)}, u32[]{:S(2)}, u32[]{:S(2)}) collective-permute-start(bf16[512,512]{1,0:T(8,128)(2,1)} %fusion.17), channel_id=1, source_target_pairs={{8,0},{16,8},{24,16},{9,1},{17,9},{25,17},{10,2},{18,10},{26,18},{... | collective-permute-start | bytes 1572872 | tf_op jit(solution)/shard_map/ppermute | solution.py:53
  164.0 20.2 %collective-permute-start.14 = (bf16[512,512]{1,0:T(8,128)(2,1)}, bf16[512,512]{1,0:T(8,128)(2,1)}, u32[]{:S(2)}, u32[]{:S(2)}) collective-permute-start(bf16[512,512]{1,0:T(8,128)(2,1)} %fusion.17), channel_id=1, source_target_pairs={{0,8},{8,16},{16,24},{1,9},{9,17},{17,25},{2,10},{10,18},{18,26},{... | collective-permute-start | bytes 1572872 | tf_op jit(solution)/shard_map/ppermute | solution.py:52
  165.3 33.2 %collective-permute-start.16 = (bf16[512,512]{1,0:T(8,128)(2,1)}, bf16[512,512]{1,0:T(8,128)(2,1)}, u32[]{:S(2)}, u32[]{:S(2)}) collective-permute-start(bf16[512,512]{1,0:T(8,128)(2,1)} %collective-permute-done.15), channel_id=1, source_target_pairs={{8,0},{16,24},{9,1},{17,25},{10,2},{18,26},{11,3},{19,27},{12,4},{... | collective-permute-start | bytes 1572872 | tf_op jit(solution)/shard_map/ppermute | solution.py:54
  169.3 10.2 %copy-start.4 = (bf16[32,16,2304]{2,1,0:T(8,128)(2,1)S(1)}, bf16[32,16,2304]{2,1,0:T(8,128)(2,1)}, u32[]{:S(2)}) copy-start(bf16[32,16,2304]{2,1,0:T(8,128)(2,1)} %copy-done.3) | copy-start | bytes 7077892
  169.3 32.1 %all-to-all-start.2 = ((f32[4,16,2304]{2,1,0:T(8,128)}), f32[4,16,2304]{2,1,0:T(8,128)S(1)}, u32[]{:S(2)}, u32[]{:S(2)}) async-start(f32[4,16,2304]{2,1,0:T(8,128)} %fusion.27), calls=%async_computation.2 | async-start | bytes 1179648 | tf_op jit(solution)/shard_map/all_to_all | solution.py:329
  (4 other events, 3.4 us)
